TPU v7x, 32 devices: a whole 2x2x4 slice. The times are simulated.
32 devices in a mesh: dp: 16 (over z, x, core), tensor: 2 (over y).
Axes of the slice: x: 2, y: 2, z: 4, core: 2. Of those that a mesh axis runs over, the one named last changes fastest.
Arguments:
- tokens: bfloat16 [6144, 2048], P(('dp', 'tensor')), may hold values from -6 to 6
- routes: int32 [6144, 8], P('dp'), may hold values from 0 to 15, all different within a row; in each aligned block of 192 rows (0 to 191, 192 to 383, ...) at most 128 rows name the same one
- cotangent: bfloat16 [6144, 2048], P(('dp', 'tensor')), may hold values from -6 to 6
- attn_gain: float32 [2048], replicated, may hold values from 0.5 to 1.5
- q_gain: float32 [2048], replicated, may hold values from 0.5 to 1.5
- k_gain: float32 [2048], replicated, may hold values from 0.5 to 1.5
- w_query: bfloat16 [2048, 2048], P('dp', 'tensor'), may hold values from -0.125 to 0.125
- w_key: bfloat16 [2048, 2048], P('dp', 'tensor'), may hold values from -0.125 to 0.125
- w_value: bfloat16 [2048, 2048], P('dp', 'tensor'), may hold values from -0.125 to 0.125
- w_out: bfloat16 [2048, 2048], P('tensor', 'dp'), may hold values from -1 to 1
- mlp_gain: float32 [2048], replicated, may hold values from 0.5 to 1.5
- router: bfloat16 [2048, 16], replicated, may hold values from -0.0625 to 0.0625
- w_gate: bfloat16 [16, 2048, 1024], P('dp', None, 'tensor'), may hold values from -0.125 to 0.125
- w_up: bfloat16 [16, 2048, 1024], P('dp', None, 'tensor'), may hold values from -0.125 to 0.125
- w_down: bfloat16 [16, 1024, 2048], P('dp', 'tensor'), may hold values from -1.75 to 1.75
Outputs:
- layer_out: bfloat16 [6144, 2048], P(('dp', 'tensor'))
- tokens_grad: float32 [6144, 2048], P(('dp', 'tensor'))
- attn_gain_grad: float32 [2048], replicated
- q_gain_grad: float32 [2048], replicated
- k_gain_grad: float32 [2048], replicated
- w_query_grad: float32 [2048, 2048], P('dp', 'tensor')
- w_key_grad: float32 [2048, 2048], P('dp', 'tensor')
- w_value_grad: float32 [2048, 2048], P('dp', 'tensor')
- w_out_grad: float32 [2048, 2048], P('tensor', 'dp')
- mlp_gain_grad: float32 [2048], replicated
- router_grad: float32 [2048, 16], replicated
- w_gate_grad: float32 [16, 2048, 1024], P('dp', None, 'tensor')
- w_up_grad: float32 [16, 2048, 1024], P('dp', None, 'tensor')
- w_down_grad: float32 [16, 1024, 2048], P('dp', 'tensor')
Inputs may be any that keep to these rules, and one draw needn't show every extreme that they name: `routes`: each row names 8 different experts; in each aligned block of 192 rows no expert is named by more than 128 rows, and in some block one expert is named by exactly 128 rows.
All inputs are finite; a program needn't handle non-finite values.
Results may differ from a plain program's by a relative error of at most 0.018.
Values may be sent and summed in bfloat16 or wider, within the bound.
A program may use at most 320 MiB of HBM per device.

v0:
```python
import jax
import jax.numpy as jnp
from jax import lax
from jax.sharding import PartitionSpec as P

D = 2048
HEAD = 128
TOPK = 8
PROMPT = 256
CONT = 64
GROUP = 384


EPSILON = 1e-05
ROPE_BASE = 10000.0
HIGHEST = lax.Precision.HIGHEST


def matmul(first_op, second_op):
    return jnp.dot(first_op, second_op, preferred_element_type=jnp.float32)


def gather_rows(values):
    return lax.all_gather(values, "tensor", axis=0, tiled=True)


def sum_rows(values):
    return lax.psum_scatter(values, "tensor", scatter_dimension=0, tiled=True)


def tensor_total(values):
    return lax.psum((values[0], values[1]), "tensor")


def expert_swap(values):
    return lax.all_to_all(values, "dp", split_axis=0, concat_axis=0, tiled=True)


def sum_slots(values):
    return lax.psum_scatter(values, "tensor", scatter_dimension=1, tiled=True)


def group_positions():
    position = jnp.arange(GROUP, dtype=jnp.int32)
    return jnp.where(position < PROMPT, position, PROMPT + (position - PROMPT) % CONT)


def visible_keys():
    position = jnp.arange(GROUP, dtype=jnp.int32)
    member = jnp.where(position < PROMPT, -1, (position - PROMPT) // CONT)
    causal = position[None, :] <= position[:, None]
    return causal & ((member[None, :] == -1) | (member[None, :] == member[:, None]))


def rope_tables():
    half_head = HEAD // 2
    frequency = ROPE_BASE ** (-2.0 * jnp.arange(half_head, dtype=jnp.float32) / HEAD)
    angles = group_positions().astype(jnp.float32)[:, None] * frequency[None, :]
    angles = jnp.concatenate([angles, angles], axis=1)
    return (jnp.cos(angles), jnp.sin(angles))


def rotate(values, cosine_table, sine_table):
    half_head = HEAD // 2
    turned = jnp.concatenate([-values[..., half_head:], values[..., :half_head]], axis=-1)
    return values * cosine_table[:, None, :] + turned * sine_table[:, None, :]


def unrotate(values, cosine_table, sine_table):
    half_head = HEAD // 2
    scaled = values * sine_table[:, None, :]
    turned = jnp.concatenate([scaled[..., half_head:], -scaled[..., :half_head]], axis=-1)
    return values * cosine_table[:, None, :] + turned


def gate_split(rows_in, hot_table, router):
    gates = jax.nn.softmax(matmul(rows_in, router), axis=1)
    weights = jnp.sum(jnp.where(hot_table, gates[:, None, :], 0.0), axis=2)
    return (gates, weights)


def body(
    tokens,
    routes,
    cotangent,
    attn_gain,
    q_gain,
    k_gain,
    w_query,
    w_key,
    w_value,
    w_out,
    mlp_gain,
    router,
    w_gate,
    w_up,
    w_down,
):
    rank_index = lax.axis_index("tensor")
    tensor_count = lax.axis_size("tensor")
    own_rows = tokens.shape[0]
    head_cols = w_query.shape[1]
    local_heads = head_cols // HEAD
    col_start = rank_index * head_cols
    row_start = rank_index * own_rows
    experts = router.shape[1]
    half_cap = (own_rows * TOPK * 4 + 3 * experts - 1) // (3 * experts)
    capacity = tensor_count * half_cap
    attn_scale = HEAD ** (-0.5)
    head_shape = (GROUP, local_heads, HEAD)
    q_gain_local = lax.dynamic_slice_in_dim(q_gain, col_start, head_cols)
    k_gain_local = lax.dynamic_slice_in_dim(k_gain, col_start, head_cols)
    inputs = tokens.astype(jnp.float32)
    attn_inv = lax.rsqrt(jnp.mean(inputs * inputs, axis=1, keepdims=True) + EPSILON)
    normed = gather_rows((inputs * attn_inv * attn_gain).astype(jnp.bfloat16))
    pieces = (
        lax.all_gather(w_query, "dp", axis=0, tiled=True),
        lax.all_gather(w_key, "dp", axis=0, tiled=True),
        lax.all_gather(w_value, "dp", axis=0, tiled=True),
    )
    normed_part = normed
    queries = matmul(normed_part, pieces[0])
    keys_raw = matmul(normed_part, pieces[1])
    values_raw = matmul(normed_part, pieces[2])
    query_sq, key_sq = tensor_total(
        (jnp.sum(queries * queries, axis=1), jnp.sum(keys_raw * keys_raw, axis=1))
    )
    query_inv = lax.rsqrt(query_sq / D + EPSILON)[:, None]
    key_inv = lax.rsqrt(key_sq / D + EPSILON)[:, None]
    cosine_table, sine_table = rope_tables()
    query_rot = rotate(
        (queries * query_inv * q_gain_local).reshape(head_shape), cosine_table, sine_table
    ).astype(jnp.bfloat16)
    key_rot = rotate(
        (keys_raw * key_inv * k_gain_local).reshape(head_shape), cosine_table, sine_table
    ).astype(jnp.bfloat16)
    value_heads = values_raw.astype(jnp.bfloat16).reshape(head_shape)
    visible = visible_keys()[None]

    def masked_scores():
        raw_scores = (
            jnp.einsum("qhd,khd->hqk", query_rot, key_rot, preferred_element_type=jnp.float32)
            * attn_scale
        )
        return jnp.where(visible, raw_scores, -1e30)

    scores = masked_scores()
    row_max = jnp.max(scores, axis=2, keepdims=True)
    exponent = jnp.exp(scores - row_max)
    row_total = jnp.sum(exponent, axis=2, keepdims=True)
    log_total = row_max + jnp.log(row_total)
    mixed_heads = jnp.einsum(
        "hqk,khd->qhd",
        (exponent / row_total).astype(jnp.bfloat16),
        value_heads,
        preferred_element_type=jnp.float32,
    )
    mixed_heads = mixed_heads.reshape(GROUP, head_cols).astype(jnp.bfloat16)
    attn_part = matmul(mixed_heads, lax.all_gather(w_out, "dp", axis=1, tiled=True))
    attended = sum_rows(attn_part)
    hidden_one = inputs + attended
    mlp_inv = lax.rsqrt(jnp.mean(hidden_one * hidden_one, axis=1, keepdims=True) + EPSILON)
    normed_two = (hidden_one * mlp_inv * mlp_gain).astype(jnp.bfloat16)
    expert_ids = jnp.arange(experts, dtype=jnp.int32)
    route_hot = routes[:, :, None] == expert_ids[None, None, :]
    flat_hot = route_hot.astype(jnp.int32).reshape(tensor_count, own_rows * TOPK, experts)
    within = jnp.sum((jnp.cumsum(flat_hot, axis=1) - flat_hot) * flat_hot, axis=2).reshape(
        GROUP, TOPK
    )
    owner_of = (jnp.arange(GROUP, dtype=jnp.int32) // own_rows)[:, None]
    own_routes = lax.dynamic_slice_in_dim(routes, row_start, own_rows, 0)
    own_within = lax.dynamic_slice_in_dim(within, row_start, own_rows, 0)
    own_hot = lax.dynamic_slice_in_dim(route_hot, row_start, own_rows, 0)
    own_dest = own_routes * half_cap + own_within
    gate_weight = w_gate[0]
    up_weight = w_up[0]
    down_weight = w_down[0]
    normed_two_all = gather_rows(normed_two)
    gates_every, gate_every = gate_split(normed_two_all, route_hot, router)
    own_probs = lax.dynamic_slice_in_dim(gates_every, row_start, own_rows, 0)
    gate_weights = lax.dynamic_slice_in_dim(gate_every, row_start, own_rows, 0)
    destination = routes * capacity + owner_of * half_cap + within
    send_rows = (
        jnp.zeros((experts * capacity, D), jnp.bfloat16)
        .at[destination]
        .set(jnp.broadcast_to(normed_two_all[:, None, :], (GROUP, TOPK, D)))
        .reshape(experts, capacity, D)
    )
    received = lax.all_to_all(send_rows, "dp", split_axis=0, concat_axis=0, tiled=True)
    gate_pre = jnp.einsum("scd,df->scf", received, gate_weight, preferred_element_type=jnp.float32)
    up_pre = jnp.einsum("scd,df->scf", received, up_weight, preferred_element_type=jnp.float32)
    hidden = (jax.nn.silu(gate_pre) * up_pre).astype(jnp.bfloat16)
    expert_part = jnp.einsum("scf,fd->scd", hidden, down_weight, preferred_element_type=jnp.float32)
    expert_part, gate_pre, up_pre, hidden, received = (
        expert_part,
        gate_pre,
        up_pre,
        hidden,
        received,
    )
    back_rows = expert_swap(sum_slots(expert_part).astype(jnp.bfloat16)).reshape(
        experts * half_cap, D
    )
    picked = back_rows[own_dest].astype(jnp.float32)
    mixture = jnp.sum(gate_weights[:, :, None] * picked, axis=1)
    layer_out = (hidden_one + mixture).astype(jnp.bfloat16)
    upstream = cotangent.astype(jnp.float32)
    gate_grad = jnp.sum(upstream[:, None, :] * picked, axis=2)
    upstream_all = gather_rows(cotangent).astype(jnp.float32)
    send_grads = (
        jnp.zeros((experts * capacity, D), jnp.bfloat16)
        .at[destination]
        .set((gate_every[:, :, None] * upstream_all[:, None, :]).astype(jnp.bfloat16))
        .reshape(experts, capacity, D)
    )
    out_grads = expert_swap(send_grads)
    hidden_grad = jnp.einsum(
        "scd,fd->scf", out_grads, down_weight, preferred_element_type=jnp.float32
    )
    sigmoid = jax.nn.sigmoid(gate_pre)
    up_grad = (hidden_grad * gate_pre * sigmoid).astype(jnp.bfloat16)
    gate_pre_grad = (hidden_grad * up_pre * sigmoid * (1.0 + gate_pre * (1.0 - sigmoid))).astype(
        jnp.bfloat16
    )
    row_part = jnp.einsum(
        "scf,df->scd", gate_pre_grad, gate_weight, preferred_element_type=jnp.float32
    ) + jnp.einsum("scf,df->scd", up_grad, up_weight, preferred_element_type=jnp.float32)
    down_weight_grad = jnp.einsum(
        "scf,scd->fd", hidden, out_grads, preferred_element_type=jnp.float32
    )
    gate_weight_grad = jnp.einsum(
        "scd,scf->df", received, gate_pre_grad, preferred_element_type=jnp.float32
    )
    up_weight_grad = jnp.einsum(
        "scd,scf->df", received, up_grad, preferred_element_type=jnp.float32
    )
    returned_grads = expert_swap(sum_slots(row_part).astype(jnp.bfloat16)).reshape(
        experts * half_cap, D
    )
    normed_two_part = jnp.sum(returned_grads[own_dest].astype(jnp.float32), axis=1)
    expert_grad = jnp.sum(jnp.where(own_hot, gate_grad[:, :, None], 0.0), axis=1)
    logit_grad = own_probs * (expert_grad - jnp.sum(expert_grad * own_probs, axis=1, keepdims=True))
    router_grad = jnp.dot(normed_two.astype(jnp.float32).T, logit_grad, precision=HIGHEST)
    normed_two_grad = normed_two_part + jnp.dot(
        logit_grad, router.astype(jnp.float32).T, precision=HIGHEST
    )
    scaled_grad = normed_two_grad * mlp_gain
    hidden_one_grad = (
        upstream
        + mlp_inv * scaled_grad
        - hidden_one * mlp_inv**3 * jnp.mean(hidden_one * scaled_grad, axis=1, keepdims=True)
    )
    mlp_gain_grad = jnp.sum(normed_two_grad * hidden_one * mlp_inv, axis=0)
    attended_grad = gather_rows(hidden_one_grad.astype(jnp.bfloat16))
    mixed_grad = jnp.einsum(
        "gd,cd->gc",
        attended_grad,
        lax.all_gather(w_out, "dp", axis=1, tiled=True),
        preferred_element_type=jnp.float32,
    )
    mixed_grad = mixed_grad.astype(jnp.bfloat16).reshape(head_shape)
    attn_probs = jnp.exp(masked_scores() - log_total)
    prob_grad = jnp.einsum(
        "qhd,khd->hqk", mixed_grad, value_heads, preferred_element_type=jnp.float32
    )
    row_dot = jnp.sum(prob_grad * attn_probs, axis=2, keepdims=True)
    score_grad = (attn_probs * (prob_grad - row_dot)).astype(jnp.bfloat16)
    query_rot_grad = (
        jnp.einsum("hqk,khd->qhd", score_grad, key_rot, preferred_element_type=jnp.float32)
        * attn_scale
    )
    key_rot_grad = (
        jnp.einsum("hqk,qhd->khd", score_grad, query_rot, preferred_element_type=jnp.float32)
        * attn_scale
    )
    value_grad = (
        jnp.einsum(
            "hqk,qhd->khd",
            attn_probs.astype(jnp.bfloat16),
            mixed_grad,
            preferred_element_type=jnp.float32,
        )
        .reshape(GROUP, head_cols)
        .astype(jnp.bfloat16)
    )
    query_norm_grad = unrotate(query_rot_grad, cosine_table, sine_table).reshape(GROUP, head_cols)
    key_norm_grad = unrotate(key_rot_grad, cosine_table, sine_table).reshape(GROUP, head_cols)
    query_scaled = query_norm_grad * q_gain_local
    key_scaled = key_norm_grad * k_gain_local
    query_dot, key_dot = tensor_total(
        (jnp.sum(queries * query_scaled, axis=1), jnp.sum(keys_raw * key_scaled, axis=1))
    )
    query_grad = (
        query_inv * query_scaled - queries * query_inv**3 * (query_dot / D)[:, None]
    ).astype(jnp.bfloat16)
    key_grad = (key_inv * key_scaled - keys_raw * key_inv**3 * (key_dot / D)[:, None]).astype(
        jnp.bfloat16
    )
    q_gain_part = jnp.sum(query_norm_grad * queries * query_inv, axis=0)
    k_gain_part = jnp.sum(key_norm_grad * keys_raw * key_inv, axis=0)
    pieces = lax.all_gather((w_query, w_key, w_value), "dp", axis=0, tiled=True)
    normed_part = (
        jnp.einsum("gc,rc->gr", query_grad, pieces[0], preferred_element_type=jnp.float32)
        + jnp.einsum("gc,rc->gr", key_grad, pieces[1], preferred_element_type=jnp.float32)
        + jnp.einsum("gc,rc->gr", value_grad, pieces[2], preferred_element_type=jnp.float32)
    )
    weight_sums = lax.psum_scatter(
        jnp.concatenate(
            [
                jnp.einsum("gr,gc->rc", normed, query_grad, preferred_element_type=jnp.float32),
                jnp.einsum("gr,gc->rc", normed, key_grad, preferred_element_type=jnp.float32),
                jnp.einsum("gr,gc->rc", normed, value_grad, preferred_element_type=jnp.float32),
                jnp.einsum(
                    "gr,gc->rc", attended_grad, mixed_heads, preferred_element_type=jnp.float32
                ),
            ],
            axis=1,
        ),
        "dp",
        scatter_dimension=0,
        tiled=True,
    )
    normed_grad = sum_rows(normed_part)
    scaled_input = normed_grad * attn_gain
    tokens_grad = (
        hidden_one_grad
        + attn_inv * scaled_input
        - inputs * attn_inv**3 * jnp.mean(inputs * scaled_input, axis=1, keepdims=True)
    )
    attn_gain_grad = jnp.sum(normed_grad * inputs * attn_inv, axis=0)
    zero_width = jnp.zeros((D,), jnp.float32)
    q_gain_full = lax.dynamic_update_slice_in_dim(zero_width, q_gain_part, col_start, 0)
    k_gain_full = lax.dynamic_update_slice_in_dim(zero_width, k_gain_part, col_start, 0)
    attn_gain_grad, q_gain_grad, k_gain_grad, mlp_gain_grad, router_grad = lax.psum(
        (attn_gain_grad, q_gain_full, k_gain_full, mlp_gain_grad, router_grad), ("dp", "tensor")
    )
    return (
        layer_out,
        tokens_grad,
        attn_gain_grad,
        q_gain_grad,
        k_gain_grad,
        weight_sums[:, :head_cols],
        weight_sums[:, head_cols : 2 * head_cols],
        weight_sums[:, 2 * head_cols : 3 * head_cols],
        jnp.transpose(weight_sums[:, 3 * head_cols :]),
        mlp_gain_grad,
        router_grad,
        gate_weight_grad[None],
        up_weight_grad[None],
        down_weight_grad[None],
    )


def solution(mesh):
    in_specs = (
        P(("dp", "tensor"), None),
        P("dp", None),
        P(("dp", "tensor"), None),
        P(),
        P(),
        P(),
        P("dp", "tensor"),
        P("dp", "tensor"),
        P("dp", "tensor"),
        P("tensor", "dp"),
        P(),
        P(),
        P("dp", None, "tensor"),
        P("dp", None, "tensor"),
        P("dp", "tensor", None),
    )
    out_specs = (
        P(("dp", "tensor"), None),
        P(("dp", "tensor"), None),
        P(),
        P(),
        P(),
        P("dp", "tensor"),
        P("dp", "tensor"),
        P("dp", "tensor"),
        P("tensor", "dp"),
        P(),
        P(),
        P("dp", None, "tensor"),
        P("dp", None, "tensor"),
        P("dp", "tensor", None),
    )
    return jax.shard_map(body, mesh=mesh, in_specs=in_specs, out_specs=out_specs, check_vma=False)
```

profile of v0, /device:TPU:0, one launch (start us, length us, event | category | flops | bytes accessed | tf_op | source)
XLA Modules:
  0.0 2718.6 jit_solution(3922574708786858665)
XLA Ops:
  16.7 25.5 all-gather.9.cloned.1.call-done
  42.2 52.9 %all-gather.15.cloned.1.call-done = bf16[2048,1024]{1,0:T(8,128)(2,1)} async-done(((bf16[128,1024]{1,0:T(8,128)(2,1)}), bf16[2048,1024]{1,0:T(8,128)(2,1)}) %all-gather.15.cloned.1.call-update) | async-done | bytes 4194320 | tf_op jit(solution)/shard_map/all_gather | solution.py:118
  100.7 45.7 %all-gather.13.cloned.1.call-done = bf16[2048,1024]{1,0:T(8,128)(2,1)} async-done(((bf16[128,1024]{1,0:T(8,128)(2,1)}), bf16[2048,1024]{1,0:T(8,128)(2,1)}) %all-gather.13.cloned.1.call-update) | async-done | bytes 4194320 | tf_op jit(solution)/shard_map/all_gather | solution.py:117
  177.6 20.0 all-gather.11.cloned.1.call-done
  204.2 47.0 %all-gather.17.cloned.1.call-done = bf16[1024,2048]{1,0:T(8,128)(2,1)} async-done(((bf16[1024,128]{1,0:T(8,128)(2,1)}), bf16[1024,2048]{1,0:T(8,128)(2,1)}) %all-gather.17.cloned.1.call-update) | async-done | bytes 4194320 | tf_op jit(solution)/shard_map/all_gather | solution.py:159
  257.2 41.4 %reduce-scatter.6.cloned.1.call-done = f32[192,2048]{1,0:T(8,128)} async-done(((f32[384,2048]{1,0:T(8,128)}), f32[192,2048]{1,0:T(8,128)}) %reduce-scatter.6.cloned.1.call-update) | async-done | bytes 1572880 | tf_op jit(solution)/shard_map/reduce_scatter | solution.py:28
  313.4 16.6 all-gather.19.cloned.1.call-done
  330.0 27.6 %scatter_custom_fusion = bf16[4096,2048]{1,0:T(8,128)(2,1)} fusion(s32[3072]{0:T(1024)S(1)} %reshape.372, bf16[]{:T(256)} %constant.98.clone.1, bf16[384,2048]{1,0:T(8,128)(2,1)} %all-gather.19.cloned.1.call-done), kind=kCustom, calls=%fused_computation.14 | custom fusion | bytes 18350082 | tf_op jit(solution)/shard_map/scatter | solution.py:186
  364.1 29.3 %all-gather.21.cloned.1.call-done = bf16[384,2048]{1,0:T(8,128)(2,1)} async-done(((bf16[192,2048]{1,0:T(8,128)(2,1)}), bf16[384,2048]{1,0:T(8,128)(2,1)}) %all-gather.21.cloned.1.call-update) | async-done | bytes 1572880 | tf_op jit(solution)/shard_map/all_gather | solution.py:24
  398.4 28.4 %scatter_custom_fusion.1 = bf16[4096,2048]{1,0:T(8,128)(2,1)} fusion(s32[3072]{0:T(1024)S(1)} %reshape.372, f32[384,2048]{1,0:T(8,128)} %convert_element_type.127, f32[384,8]{1,0:T(8,128)S(1)} %copy.176, bf16[]{:T(256)} %constant.98.clone.1), kind=kCustom, calls=%fused_computation.12 | custom fusion | flops 12582912 | bytes 20119554 | tf_op jit(solution)/shard_map/scatter | solution.py:213
  426.8 233.3 %all-to-all-done = bf16[16,256,2048]{2,1,0:T(8,128)(2,1)} async-done(((bf16[16,256,2048]{2,1,0:T(8,128)(2,1)}), bf16[16,256,2048]{2,1,0:T(8,128)(2,1)}, u32[]{:S(2)}, u32[]{:S(2)}) %all-to-all-start) | async-done | bytes 16777248 | tf_op jit(solution)/shard_map/all_to_all | solution.py:189
  660.1 70.3 %all-to-all-start.2 = ((bf16[16,256,2048]{2,1,0:T(8,128)(2,1)}), bf16[16,256,2048]{2,1,0:T(8,128)(2,1)}, u32[]{:S(2)}, u32[]{:S(2)}) async-start(bf16[16,256,2048]{2,1,0:T(8,128)(2,1)} %bitcast.140), calls=%async_computation.4 | async-start | bytes 33554432 | tf_op jit(solution)/shard_map/all_to_all | solution.py:36
  730.6 15.2 fusion.23
  745.8 14.5 fusion.27
  760.3 266.8 %all-to-all-done.2 = bf16[16,256,2048]{2,1,0:T(8,128)(2,1)} async-done(((bf16[16,256,2048]{2,1,0:T(8,128)(2,1)}), bf16[16,256,2048]{2,1,0:T(8,128)(2,1)}, u32[]{:S(2)}, u32[]{:S(2)}) %all-to-all-start.2) | async-done | bytes 16777248 | tf_op jit(solution)/shard_map/all_to_all | solution.py:36
  1027.2 24.2 multiply_convert_fusion.1
  1051.4 17.9 fusion.25
  1069.3 28.5 %convolution_add_fusion = f32[16,256,2048]{2,1,0:T(8,128)} fusion(f32[16,256,2048]{2,1,0:T(8,128)} %fusion.25, bf16[16,256,512]{2,1,0:T(8,128)(2,1)} %get-tuple-element.106, bf16[1,2048,512]{2,1,0:T(8,128)(2,1)} %param.28), kind=kOutput, calls=%fused_computation.6 | convolution fusion | flops 8598323200 | bytes 73400320 | tf_op jit(solution)/shard_map/scf,df->scd/dot_general | solution.py:227
  1097.8 17.6 fusion.20
  1115.4 416.0 %reduce-scatter.10.cloned.1.call-done = f32[16,128,2048]{2,1,0:T(8,128)} async-done(((f32[16,256,2048]{2,1,0:T(8,128)}), f32[16,128,2048]{2,1,0:T(8,128)}) %reduce-scatter.10.cloned.1.call-update) | async-done | bytes 16777232 | tf_op jit(solution)/shard_map/reduce_scatter | solution.py:40
  1546.2 356.4 %reduce-scatter.8.cloned.1.call-done = f32[16,128,2048]{2,1,0:T(8,128)} async-done(((f32[16,256,2048]{2,1,0:T(8,128)}), f32[16,128,2048]{2,1,0:T(8,128)}) %reduce-scatter.8.cloned.1.call-update) | async-done | bytes 16777232 | tf_op jit(solution)/shard_map/reduce_scatter | solution.py:40
  1919.4 17.3 gather_fusion.1
  1945.6 122.6 %all-to-all-done.1 = bf16[16,128,2048]{2,1,0:T(8,128)(2,1)} async-done(((bf16[16,128,2048]{2,1,0:T(8,128)(2,1)}), bf16[16,128,2048]{2,1,0:T(8,128)(2,1)}, u32[]{:S(2)}, u32[]{:S(2)}) %all-to-all-start.1) | async-done | bytes 8388640 | tf_op jit(solution)/shard_map/all_to_all | solution.py:36
  2068.2 17.1 gather_fusion
  2099.2 58.2 %all-gather.23.cloned.1.call-done = bf16[384,2048]{1,0:T(8,128)(2,1)} async-done(((bf16[192,2048]{1,0:T(8,128)(2,1)}), bf16[384,2048]{1,0:T(8,128)(2,1)}) %all-gather.23.cloned.1.call-update) | async-done | bytes 1572880 | tf_op jit(solution)/shard_map/all_gather | solution.py:24
  2216.1 25.2 pad_maximum_fusion
  2241.6 15.2 convolution_bitcast_fusion
  2256.8 15.6 convolution_bitcast_fusion.1
  2272.4 15.5 convolution_bitcast_fusion.2
  2291.9 42.9 %all-reduce = (f32[2048]{0:T(1024)}, f32[2048]{0:T(1024)}, f32[2048]{0:T(1024)}, f32[2048]{0:T(1024)}) all-reduce(f32[2048]{0:T(1024)S(1)} %get-tuple-element.92, f32[2048]{0:T(1024)S(1)} %dynamic_update_slice.6, f32[2048]{0:T(1024)S(1)} %dynamic_update_slice.7, ...), channel_id=1, replica_groups=mesh['dp'=16,'tensor'=2] {'dp','tensor'}, use_global_device_ids=true, to_apply=%region_33.34 | all-reduce | flops 8192 | bytes 65536 | tf_op jit(solution)/shard_map/psum | solution.py:334
  2338.3 244.4 %reduce-scatter.14.cloned.1.call-done = f32[128,4096]{0,1:T(8,128)} async-done(((f32[2048,4096]{0,1:T(8,128)}), f32[128,4096]{0,1:T(8,128)}) %reduce-scatter.14.cloned.1.call-update) | async-done | bytes 2097168 | tf_op jit(solution)/shard_map/reduce_scatter | solution.py:307
  2589.5 120.7 %all-reduce.5.cloned.1.call-done = f32[2048,16]{0,1:T(8,128)} async-done(((f32[2048,16]{0,1:T(8,128)}), f32[2048,16]{0,1:T(8,128)}) %all-reduce.5.cloned.1.call-update) | async-done | bytes 131088 | tf_op jit(solution)/shard_map/psum | solution.py:334
  (298 shorter events, 213.4 us)
Async XLA Ops:
  7.2 1020.0 %copy-start = (bf16[1,512,2048]{2,1,0:T(8,128)(2,1)S(1)}, bf16[1,512,2048]{2,1,0:T(8,128)(2,1)}, u32[]{:S(2)}) copy-start(bf16[1,512,2048]{2,1,0:T(8,128)(2,1)} %param.29) | copy-start | bytes 6291460
  7.2 35.0 %all-gather.9.cloned.1.call-start = ((), (), s32[]{:S(2)}) async-start(), calls=%async_computation.9 | async-start | bytes 2359296 | tf_op jit(solution)/shard_map/all_gather | solution.py:24
  12.2 83.0 %all-gather.15.cloned.1.call-start = ((), (), s32[]{:S(2)}) async-start(), calls=%async_computation.12 | async-start | bytes 4456448 | tf_op jit(solution)/shard_map/all_gather | solution.py:118
  12.9 133.5 %all-gather.13.cloned.1.call-start = ((), (), s32[]{:S(2)}) async-start(), calls=%async_computation.11 | async-start | bytes 4456448 | tf_op jit(solution)/shard_map/all_gather | solution.py:117
  13.7 183.9 %all-gather.11.cloned.1.call-start = ((), (), s32[]{:S(2)}) async-start(), calls=%async_computation.10 | async-start | bytes 4456448 | tf_op jit(solution)/shard_map/all_gather | solution.py:119
  14.2 237.0 %all-gather.17.cloned.1.call-start = ((), (), s32[]{:S(2)}) async-start(), calls=%async_computation.13 | async-start | bytes 4456448 | tf_op jit(solution)/shard_map/all_gather | solution.py:159
  14.8 283.8 %reduce-scatter.6.cloned.1.call-start = ((), (), s32[]{:S(2)}) async-start(), calls=%async_computation.14 | async-start | bytes 4718592 | tf_op jit(solution)/shard_map/reduce_scatter | solution.py:28
  14.9 149.2 %copy-start.51 = (f32[1024]{0:T(1024)}, f32[1024]{0:T(1024)S(1)}, u32[]{:S(2)}) copy-start(f32[1024]{0:T(1024)S(1)} %dynamic_slice.21) | copy-start | bytes 12292
  14.9 142.8 %copy-start.49 = (f32[1024]{0:T(1024)}, f32[1024]{0:T(1024)S(1)}, u32[]{:S(2)}) copy-start(f32[1024]{0:T(1024)S(1)} %dynamic_slice.22) | copy-start | bytes 12292
  174.8 27.4 %copy-start.42 = (f32[8,384]{1,0:T(8,128)}, f32[8,384]{1,0:T(8,128)S(1)}, u32[]{:S(2)}) copy-start(f32[8,384]{1,0:T(8,128)S(1)} %get-tuple-element.144) | copy-start | bytes 36868
  204.2 47.0 %copy-start.21 = (bf16[8,128,384]{2,1,0:T(8,128)(2,1)}, bf16[8,128,384]{2,1,0:T(8,128)(2,1)S(1)}, u32[]{:S(2)}) copy-start(bf16[8,128,384]{2,1,0:T(8,128)(2,1)S(1)} %fusion.41) | copy-start | bytes 2359300
  256.9 41.7 %copy-start.6 = (bf16[192,2048]{1,0:T(8,128)(2,1)S(1)}, bf16[192,2048]{1,0:T(8,128)(2,1)}, u32[]{:S(2)}) copy-start(bf16[192,2048]{1,0:T(8,128)(2,1)} %param.15) | copy-start | bytes 2359300
  257.0 44.6 %copy-start.47 = (f32[2048]{0:T(1024)S(1)}, f32[2048]{0:T(1024)}, u32[]{:S(2)}) copy-start(f32[2048]{0:T(1024)} %param.25) | copy-start | bytes 24580
  257.0 73.1 %all-gather.19.cloned.1.call-start = ((), (), s32[]{:S(2)}) async-start(), calls=%async_computation.15 | async-start | bytes 2359296 | tf_op jit(solution)/shard_map/all_gather | solution.py:24
  302.8 54.9 %copy-start.28 = (s32[384,8]{1,0:T(8,128)}, s32[384,8]{1,0:T(8,128)S(1)}, u32[]{:S(2)}) copy-start(s32[384,8]{1,0:T(8,128)S(1)} %copy.169) | copy-start | bytes 36868
  313.1 44.6 %copy-start.30 = (s32[384,8]{1,0:T(8,128)}, s32[384,8]{1,0:T(8,128)S(1)}, u32[]{:S(2)}) copy-start(s32[384,8]{1,0:T(8,128)S(1)} %reshape.346) | copy-start | bytes 36868
  357.7 302.4 %all-to-all-start = ((bf16[16,256,2048]{2,1,0:T(8,128)(2,1)}), bf16[16,256,2048]{2,1,0:T(8,128)(2,1)}, u32[]{:S(2)}, u32[]{:S(2)}) async-start(bf16[16,256,2048]{2,1,0:T(8,128)(2,1)} %bitcast.139), calls=%async_computation.1 | async-start | bytes 33554432 | tf_op jit(solution)/shard_map/all_to_all | solution.py:189
  363.4 30.1 %all-gather.21.cloned.1.call-start = ((), (), s32[]{:S(2)}) async-start(), calls=%async_computation.17 | async-start | bytes 2359296 | tf_op jit(solution)/shard_map/all_gather | solution.py:24
  364.1 32.9 %copy-start.38 = (bf16[2048,16]{0,1:T(8,128)(2,1)S(1)}, bf16[2048,16]{0,1:T(8,128)(2,1)}, u32[]{:S(2)}) copy-start(bf16[2048,16]{0,1:T(8,128)(2,1)} %param.26) | copy-start | bytes 196612
  398.3 28.5 %copy-start.44 = (f32[384,8]{0,1:T(8,128)}, f32[384,8]{0,1:T(8,128)S(1)}, u32[]{:S(2)}) copy-start(f32[384,8]{0,1:T(8,128)S(1)} %select_reduce_fusion) | copy-start | bytes 36868
  660.1 367.0 %all-to-all-start.2 = ((bf16[16,256,2048]{2,1,0:T(8,128)(2,1)}), bf16[16,256,2048]{2,1,0:T(8,128)(2,1)}, u32[]{:S(2)}, u32[]{:S(2)}) async-start(bf16[16,256,2048]{2,1,0:T(8,128)(2,1)} %bitcast.140), calls=%async_computation.4 | async-start | bytes 33554432 | tf_op jit(solution)/shard_map/all_to_all | solution.py:36
  730.4 801.0 %reduce-scatter.10.cloned.1.call-start = ((), (), s32[]{:S(2)}) async-start(), calls=%async_computation.18 | async-start | bytes 50331648 | tf_op jit(solution)/shard_map/reduce_scatter | solution.py:40
  1097.8 804.9 %reduce-scatter.8.cloned.1.call-start = ((), (), s32[]{:S(2)}) async-start(), calls=%async_computation.16 | async-start | bytes 50331648 | tf_op jit(solution)/shard_map/reduce_scatter | solution.py:40
  1540.6 371.2 %all-to-all-start.3 = ((bf16[16,128,2048]{2,1,0:T(8,128)(2,1)}), bf16[16,128,2048]{2,1,0:T(8,128)(2,1)}, u32[]{:S(2)}, u32[]{:S(2)}) async-start(bf16[16,128,2048]{2,1,0:T(8,128)(2,1)} %convert_element_type.131), calls=%async_computation.6 | async-start | bytes 16777216 | tf_op jit(solution)/shard_map/all_to_all | solution.py:36
  1911.7 156.5 %all-to-all-start.1 = ((bf16[16,128,2048]{2,1,0:T(8,128)(2,1)}), bf16[16,128,2048]{2,1,0:T(8,128)(2,1)}, u32[]{:S(2)}, u32[]{:S(2)}) async-start(bf16[16,128,2048]{2,1,0:T(8,128)(2,1)} %convert_element_type.123), calls=%async_computation.3 | async-start | bytes 16777216 | tf_op jit(solution)/shard_map/all_to_all | solution.py:36
  1917.6 239.8 %all-gather.23.cloned.1.call-start = ((), (), s32[]{:S(2)}) async-start(), calls=%async_computation.19 | async-start | bytes 2359296 | tf_op jit(solution)/shard_map/all_gather | solution.py:24
  2099.1 190.5 %reduce-scatter.12.cloned.1.call-start = ((), (), s32[]{:S(2)}) async-start(), calls=%async_computation.20 | async-start | bytes 4718592 | tf_op jit(solution)/shard_map/reduce_scatter | solution.py:28
  2165.6 31.9 %copy-start.26 = (bf16[8,128,384]{2,1,0:T(8,128)(2,1)}, bf16[8,128,384]{2,1,0:T(8,128)(2,1)S(1)}, u32[]{:S(2)}) copy-start(bf16[8,128,384]{2,1,0:T(8,128)(2,1)S(1)} %fusion.42) | copy-start | bytes 2359300
  2201.5 381.2 %reduce-scatter.14.cloned.1.call-start = ((), (), s32[]{:S(2)}) async-start(), calls=%async_computation.21 | async-start | bytes 35651584 | tf_op jit(solution)/shard_map/reduce_scatter | solution.py:307
  2241.3 468.9 %all-reduce.5.cloned.1.call-start = ((), (), s32[]{:S(2)}) async-start(), calls=%async_computation.22 | async-start | bytes 262144 | tf_op jit(solution)/shard_map/psum | solution.py:334
  2287.9 46.8 %copy-start.66 = (f32[192]{0:T(256)S(1)}, f32[192]{0:T(256)}, u32[]{:S(2)}) copy-start(f32[192]{0:T(256)} %get-tuple-element.136) | copy-start | bytes 2308
  2582.7 129.1 %copy-start.1 = (bf16[1,512,2048]{2,1,0:T(8,128)(2,1)S(1)}, bf16[1,512,2048]{2,1,0:T(8,128)(2,1)}, u32[]{:S(2)}) copy-start(bf16[1,512,2048]{2,1,0:T(8,128)(2,1)} %param.29) | copy-start | bytes 6291460
  (62 other events, 335.2 us)
Sparse Core Ops, SparseCore 0:
  12.3 29.8 all-gather.8
  44.4 50.7 all-gather.14
  97.3 49.0 all-gather.12
  148.4 49.0 all-gather.10
  199.5 51.7 all-gather.16
  257.1 41.5 reduce-scatter.5
  302.8 27.2 all-gather.18
  365.8 27.5 all-gather.20
  1097.9 433.5 reduce-scatter.9
  1533.7 368.9 reduce-scatter.7
  2099.3 58.0 all-gather.22
  2201.6 43.3 reduce-scatter.11
  2249.2 333.4 reduce-scatter.13
  2588.7 121.4 all-reduce.4
where the time goes:
time: 2720 us
  waiting for transfers between devices  2100 us (77%)
  matrix products  227 us (8%)
  other arithmetic  141 us (5%)
  local copies, waits for them, and re-layouts  93.5 us (3%)
  starting transfers between devices  88.8 us (3%)
  blocking collectives  53.1 us (2%)
    reduce_scatter x2, waiting for transfers between devices, sum_slots(): return lax.psum_scatter(values, 'tensor', scatter_dimension=1, tiled=True)  772 us
    all_to_all x3, waiting for transfers between devices, expert_swap(): return lax.all_to_all(values, 'dp', split_axis=0, concat_axis=0, tiled=True)  389 us
    reduce_scatter x1, waiting for transfers between devices, body(): lax.psum_scatter(jnp.concatenate([jnp.einsum('gr,gc->rc', normed, query_g...  244 us
    all_to_all x1, waiting for transfers between devices, body(): lax.all_to_all(send_rows, 'dp', split_axis=0, concat_axis=0, tiled=True)  233 us
    all_gather x4, waiting for transfers between devices, gather_rows(): return lax.all_gather(values, 'tensor', axis=0, tiled=True)  130 us
    psum x1, waiting for transfers between devices, body(): lax.psum((attn_gain_grad, q_gain_full, k_gain_full, mlp_gain_grad, router...  121 us
    all_to_all x3, starting transfers between devices, expert_swap(): return lax.all_to_all(values, 'dp', split_axis=0, concat_axis=0, tiled=True)  81.7 us
  transfers between devices with their start and end apart: 18, of which 16 were waited for; matrix products, arithmetic and copies ran while one was open for 10% of the time, Pallas kernels for 0%

commit v1 on v0

--- a/solution.py
+++ b/solution.py
@@ -1,6 +1,8 @@
 import jax
 import jax.numpy as jnp
 from jax import lax
+from jax.experimental import pallas as pl
+from jax.experimental.pallas import tpu as pltpu
 from jax.sharding import PartitionSpec as P
 
 D = 2048
@@ -79,7 +81,7 @@
     return (gates, weights)
 
 
-def body(
+def routed_body(
     tokens,
     routes,
     cotangent,
@@ -352,6 +354,297 @@
     )
 
 
+def dot_nn(a, b):
+    return lax.dot_general(a, b, (((1,), (0,)), ((), ())), preferred_element_type=jnp.float32)
+
+
+def dot_nt(a, b):
+    return lax.dot_general(a, b, (((1,), (1,)), ((), ())), preferred_element_type=jnp.float32)
+
+
+def dot_tn(a, b):
+    return lax.dot_general(a, b, (((0,), (0,)), ((), ())), preferred_element_type=jnp.float32)
+
+
+def expert_kernel(
+    x_ref,
+    g_ref,
+    gate_ref,
+    wg_ref,
+    wu_ref,
+    wd_ref,
+    y_ref,
+    r_ref,
+    gate_grad_ref,
+    wg_grad_ref,
+    wu_grad_ref,
+    wd_grad_ref,
+):
+    @pl.when(pl.program_id(0) == 0)
+    def _():
+        wg_grad_ref[...] = jnp.zeros_like(wg_grad_ref)
+        wu_grad_ref[...] = jnp.zeros_like(wu_grad_ref)
+        wd_grad_ref[...] = jnp.zeros_like(wd_grad_ref)
+
+    rows = x_ref[...]
+    upstream = g_ref[...]
+    gate = gate_ref[...]
+    gate_pre = dot_nn(rows, wg_ref[...])
+    up_pre = dot_nn(rows, wu_ref[...])
+    raw_grad = dot_nt(upstream, wd_ref[...])
+    sigmoid = jax.nn.sigmoid(gate_pre)
+    silu = gate_pre * sigmoid
+    hidden = silu * up_pre
+    gate_grad_ref[...] = jnp.sum(hidden * raw_grad, axis=1, keepdims=True)
+    hidden_gated = (gate * hidden).astype(jnp.bfloat16)
+    y_ref[...] = dot_nn(hidden_gated, wd_ref[...]).astype(jnp.bfloat16)
+    hidden_grad = gate * raw_grad
+    up_grad = (hidden_grad * silu).astype(jnp.bfloat16)
+    gate_pre_grad = (
+        hidden_grad * up_pre * sigmoid * (1.0 + gate_pre * (1.0 - sigmoid))
+    ).astype(jnp.bfloat16)
+    r_ref[...] = (dot_nt(gate_pre_grad, wg_ref[...]) + dot_nt(up_grad, wu_ref[...])).astype(
+        jnp.bfloat16
+    )
+    wg_grad_ref[...] += dot_tn(rows, gate_pre_grad)
+    wu_grad_ref[...] += dot_tn(rows, up_grad)
+    wd_grad_ref[...] += dot_tn(hidden_gated, upstream)
+
+
+def expert_pass(rows, upstream, gate, w_gate, w_up, w_down):
+    count, width = rows.shape
+    units = w_gate.shape[1]
+    tile = 512 if count % 512 == 0 else GROUP // 2
+
+    def by_row(cols):
+        return pl.BlockSpec((tile, cols), lambda i: (i, 0))
+
+    def whole(first, second):
+        return pl.BlockSpec((first, second), lambda i: (0, 0), pipeline_mode=pl.Buffered(1))
+
+    weights = [whole(width, units), whole(width, units), whole(units, width)]
+    return pl.pallas_call(
+        expert_kernel,
+        grid=(count // tile,),
+        in_specs=[by_row(width), by_row(width), by_row(1)] + weights,
+        out_specs=[by_row(width), by_row(width), by_row(1)] + weights,
+        out_shape=[
+            jax.ShapeDtypeStruct((count, width), jnp.bfloat16),
+            jax.ShapeDtypeStruct((count, width), jnp.bfloat16),
+            jax.ShapeDtypeStruct((count, 1), jnp.float32),
+            jax.ShapeDtypeStruct((width, units), jnp.float32),
+            jax.ShapeDtypeStruct((width, units), jnp.float32),
+            jax.ShapeDtypeStruct((units, width), jnp.float32),
+        ],
+        cost_estimate=pl.CostEstimate(
+            flops=18 * count * width * units,
+            bytes_accessed=8 * count * width + 18 * width * units,
+            transcendentals=count * units,
+        ),
+        compiler_params=pltpu.CompilerParams(vmem_limit_bytes=60 << 20),
+    )(rows, upstream, gate, w_gate, w_up, w_down)
+
+
+EVERY = ("dp", "tensor")
+
+
+def dense_body(
+    tokens,
+    routes,
+    cotangent,
+    attn_gain,
+    q_gain,
+    k_gain,
+    w_query,
+    w_key,
+    w_value,
+    w_out,
+    mlp_gain,
+    router,
+    w_gate,
+    w_up,
+    w_down,
+):
+    rank_index = lax.axis_index("tensor")
+    own_rows = tokens.shape[0]
+    head_cols = w_query.shape[1]
+    local_heads = head_cols // HEAD
+    col_start = rank_index * head_cols
+    row_start = rank_index * own_rows
+    experts = router.shape[1]
+    attn_scale = HEAD ** (-0.5)
+    head_shape = (GROUP, local_heads, HEAD)
+    q_gain_local = lax.dynamic_slice_in_dim(q_gain, col_start, head_cols)
+    k_gain_local = lax.dynamic_slice_in_dim(k_gain, col_start, head_cols)
+    inputs = tokens.astype(jnp.float32)
+    attn_inv = lax.rsqrt(jnp.mean(inputs * inputs, axis=1, keepdims=True) + EPSILON)
+    normed = gather_rows((inputs * attn_inv * attn_gain).astype(jnp.bfloat16))
+    q_all = lax.all_gather(w_query, "dp", axis=0, tiled=True)
+    k_all = lax.all_gather(w_key, "dp", axis=0, tiled=True)
+    v_all = lax.all_gather(w_value, "dp", axis=0, tiled=True)
+    o_all = lax.all_gather(w_out, "dp", axis=1, tiled=True)
+    upstream_all = lax.all_gather(cotangent, EVERY, axis=0, tiled=True)
+    queries = matmul(normed, q_all)
+    keys_raw = matmul(normed, k_all)
+    values_raw = matmul(normed, v_all)
+    query_sq, key_sq = tensor_total(
+        (jnp.sum(queries * queries, axis=1), jnp.sum(keys_raw * keys_raw, axis=1))
+    )
+    query_inv = lax.rsqrt(query_sq / D + EPSILON)[:, None]
+    key_inv = lax.rsqrt(key_sq / D + EPSILON)[:, None]
+    cosine_table, sine_table = rope_tables()
+    query_rot = rotate(
+        (queries * query_inv * q_gain_local).reshape(head_shape), cosine_table, sine_table
+    ).astype(jnp.bfloat16)
+    key_rot = rotate(
+        (keys_raw * key_inv * k_gain_local).reshape(head_shape), cosine_table, sine_table
+    ).astype(jnp.bfloat16)
+    value_heads = values_raw.astype(jnp.bfloat16).reshape(head_shape)
+    visible = visible_keys()[None]
+
+    def masked_scores():
+        raw_scores = (
+            jnp.einsum("qhd,khd->hqk", query_rot, key_rot, preferred_element_type=jnp.float32)
+            * attn_scale
+        )
+        return jnp.where(visible, raw_scores, -1e30)
+
+    scores = masked_scores()
+    row_max = jnp.max(scores, axis=2, keepdims=True)
+    exponent = jnp.exp(scores - row_max)
+    row_total = jnp.sum(exponent, axis=2, keepdims=True)
+    log_total = row_max + jnp.log(row_total)
+    mixed_heads = jnp.einsum(
+        "hqk,khd->qhd",
+        (exponent / row_total).astype(jnp.bfloat16),
+        value_heads,
+        preferred_element_type=jnp.float32,
+    )
+    mixed_heads = mixed_heads.reshape(GROUP, head_cols).astype(jnp.bfloat16)
+    attended = sum_rows(matmul(mixed_heads, o_all))
+    hidden_one = inputs + attended
+    mlp_inv = lax.rsqrt(jnp.mean(hidden_one * hidden_one, axis=1, keepdims=True) + EPSILON)
+    normed_two = (hidden_one * mlp_inv * mlp_gain).astype(jnp.bfloat16)
+    own_routes = lax.dynamic_slice_in_dim(routes, row_start, own_rows, 0)
+    expert_ids = jnp.arange(experts, dtype=jnp.int32)
+    own_hot = jnp.any(own_routes[:, :, None] == expert_ids[None, None, :], axis=1)
+    own_probs = jax.nn.softmax(matmul(normed_two, router), axis=1)
+    rows_all = lax.all_gather(normed_two, EVERY, axis=0, tiled=True)
+    gates_all = lax.all_gather(jnp.where(own_hot, own_probs, 0.0), EVERY, axis=0, tiled=True)
+    own_expert = lax.axis_index("dp")
+    own_gate = lax.dynamic_slice_in_dim(gates_all, own_expert, 1, 1)
+    y_part, r_part, gate_grad, gate_weight_grad, up_weight_grad, down_weight_grad = expert_pass(
+        rows_all, upstream_all, own_gate, w_gate[0], w_up[0], w_down[0]
+    )
+    returned = lax.psum_scatter(r_part, EVERY, scatter_dimension=0, tiled=True)
+    grad_table = jnp.where(expert_ids[None, :] == own_expert, gate_grad, 0.0)
+    expert_grad = lax.psum_scatter(grad_table, EVERY, scatter_dimension=0, tiled=True)
+    expert_grad = jnp.where(own_hot, expert_grad, 0.0)
+    mixture = lax.psum_scatter(y_part, EVERY, scatter_dimension=0, tiled=True)
+    layer_out = (hidden_one + mixture.astype(jnp.float32)).astype(jnp.bfloat16)
+    upstream = cotangent.astype(jnp.float32)
+    logit_grad = own_probs * (expert_grad - jnp.sum(expert_grad * own_probs, axis=1, keepdims=True))
+    router_grad = jnp.dot(normed_two.astype(jnp.float32).T, logit_grad, precision=HIGHEST)
+    normed_two_grad = returned.astype(jnp.float32) + jnp.dot(
+        logit_grad, router.astype(jnp.float32).T, precision=HIGHEST
+    )
+    scaled_grad = normed_two_grad * mlp_gain
+    hidden_one_grad = (
+        upstream
+        + mlp_inv * scaled_grad
+        - hidden_one * mlp_inv**3 * jnp.mean(hidden_one * scaled_grad, axis=1, keepdims=True)
+    )
+    mlp_gain_grad = jnp.sum(normed_two_grad * hidden_one * mlp_inv, axis=0)
+    attended_grad = gather_rows(hidden_one_grad.astype(jnp.bfloat16))
+    mixed_grad = jnp.einsum("gd,cd->gc", attended_grad, o_all, preferred_element_type=jnp.float32)
+    mixed_grad = mixed_grad.astype(jnp.bfloat16).reshape(head_shape)
+    attn_probs = jnp.exp(masked_scores() - log_total)
+    prob_grad = jnp.einsum(
+        "qhd,khd->hqk", mixed_grad, value_heads, preferred_element_type=jnp.float32
+    )
+    row_dot = jnp.sum(prob_grad * attn_probs, axis=2, keepdims=True)
+    score_grad = (attn_probs * (prob_grad - row_dot)).astype(jnp.bfloat16)
+    query_rot_grad = (
+        jnp.einsum("hqk,khd->qhd", score_grad, key_rot, preferred_element_type=jnp.float32)
+        * attn_scale
+    )
+    key_rot_grad = (
+        jnp.einsum("hqk,qhd->khd", score_grad, query_rot, preferred_element_type=jnp.float32)
+        * attn_scale
+    )
+    value_grad = (
+        jnp.einsum(
+            "hqk,qhd->khd",
+            attn_probs.astype(jnp.bfloat16),
+            mixed_grad,
+            preferred_element_type=jnp.float32,
+        )
+        .reshape(GROUP, head_cols)
+        .astype(jnp.bfloat16)
+    )
+    query_norm_grad = unrotate(query_rot_grad, cosine_table, sine_table).reshape(GROUP, head_cols)
+    key_norm_grad = unrotate(key_rot_grad, cosine_table, sine_table).reshape(GROUP, head_cols)
+    query_scaled = query_norm_grad * q_gain_local
+    key_scaled = key_norm_grad * k_gain_local
+    query_dot, key_dot = tensor_total(
+        (jnp.sum(queries * query_scaled, axis=1), jnp.sum(keys_raw * key_scaled, axis=1))
+    )
+    query_grad = (
+        query_inv * query_scaled - queries * query_inv**3 * (query_dot / D)[:, None]
+    ).astype(jnp.bfloat16)
+    key_grad = (key_inv * key_scaled - keys_raw * key_inv**3 * (key_dot / D)[:, None]).astype(
+        jnp.bfloat16
+    )
+    q_gain_part = jnp.sum(query_norm_grad * queries * query_inv, axis=0)
+    k_gain_part = jnp.sum(key_norm_grad * keys_raw * key_inv, axis=0)
+    normed_part = (
+        jnp.einsum("gc,rc->gr", query_grad, q_all, preferred_element_type=jnp.float32)
+        + jnp.einsum("gc,rc->gr", key_grad, k_all, preferred_element_type=jnp.float32)
+        + jnp.einsum("gc,rc->gr", value_grad, v_all, preferred_element_type=jnp.float32)
+    )
+    weight_sums = [
+        lax.psum_scatter(
+            dot_tn(first, second).astype(jnp.bfloat16), "dp", scatter_dimension=0, tiled=True
+        ).astype(jnp.float32)
+        for first, second in (
+            (normed, query_grad),
+            (normed, key_grad),
+            (normed, value_grad),
+            (attended_grad, mixed_heads),
+        )
+    ]
+    normed_grad = sum_rows(normed_part)
+    scaled_input = normed_grad * attn_gain
+    tokens_grad = (
+        hidden_one_grad
+        + attn_inv * scaled_input
+        - inputs * attn_inv**3 * jnp.mean(inputs * scaled_input, axis=1, keepdims=True)
+    )
+    attn_gain_grad = jnp.sum(normed_grad * inputs * attn_inv, axis=0)
+    zero_width = jnp.zeros((D,), jnp.float32)
+    q_gain_full = lax.dynamic_update_slice_in_dim(zero_width, q_gain_part, col_start, 0)
+    k_gain_full = lax.dynamic_update_slice_in_dim(zero_width, k_gain_part, col_start, 0)
+    attn_gain_grad, q_gain_grad, k_gain_grad, mlp_gain_grad, router_grad = lax.psum(
+        (attn_gain_grad, q_gain_full, k_gain_full, mlp_gain_grad, router_grad), EVERY
+    )
+    return (
+        layer_out,
+        tokens_grad,
+        attn_gain_grad,
+        q_gain_grad,
+        k_gain_grad,
+        weight_sums[0],
+        weight_sums[1],
+        weight_sums[2],
+        jnp.transpose(weight_sums[3]),
+        mlp_gain_grad,
+        router_grad,
+        gate_weight_grad[None],
+        up_weight_grad[None],
+        down_weight_grad[None],
+    )
+
+
 def solution(mesh):
     in_specs = (
         P(("dp", "tensor"), None),
@@ -386,4 +679,6 @@
         P("dp", None, "tensor"),
         P("dp", "tensor", None),
     )
+    experts = mesh.shape["dp"]
+    body = dense_body if experts <= 2 * TOPK else routed_body
     return jax.shard_map(body, mesh=mesh, in_specs=in_specs, out_specs=out_specs, check_vma=False)

time: 2720 us -> 1810 us (0.67)
  waiting for transfers between devices: 2100 us -> 1380 us
  matrix products: 227 us -> 69 us
  Pallas kernels: 0 us -> 134 us
  other arithmetic: 141 us -> 40.1 us
  starting transfers between devices: 88.8 us -> 1.16 us
  blocking collectives: 53.1 us -> 126 us
  local copies, waits for them, and re-layouts: 93.5 us -> 34.5 us
    all_to_all x4 -> x0, waiting for transfers between devices: 623 us -> none  [the longest x3 389 us: expert_swap(): return lax.all_to_all(values, 'dp', split_axis=0, concat_axis=0, tiled=True)]
    reduce_scatter x3 -> x6, waiting for transfers between devices: 1020 us -> 788 us  [the longest x4 295 us: dense_body(): lax.psum_scatter(dot_tn(first, second).astype(jnp.bfloat16), 'dp', scatte...]
    all_gather x4 -> x6, waiting for transfers between devices: 166 us -> 383 us  [the longest x1 157 us: dense_body(): rows_all = lax.all_gather(normed_two, EVERY, axis=0, tiled=True)]
    dot_general x24 -> x15, matrix products: 204 us -> 46.4 us  [the longest x4 20.8 us: dot_tn(): lax.dot_general(a, b, (((0,), (0,)), ((), ())), preferred_element_type=jn...]
    pallas_call x0 -> x1, Pallas kernels: none -> 134 us  [expert_pass(): pl.pallas_call(expert_kernel, grid=(count // tile,), in_specs=[by_row(wid...]
    psum x1, waiting for transfers between devices: 121 us -> 0.01 us  [dense_body(): lax.psum((attn_gain_grad, q_gain_full, k_gain_full, mlp_gain_grad, router...]
    unnamed x14 -> x19, waiting for transfers between devices: 2.98 us -> 103 us
    all_to_all x4 -> x0, starting transfers between devices: 87.4 us -> none  [the longest x3 81.7 us: expert_swap(): return lax.all_to_all(values, 'dp', split_axis=0, concat_axis=0, tiled=True)]
  transfers between devices with their start and end apart: 18 -> 18, of which waited for: 16 -> 17; matrix products, arithmetic and copies ran while one was open for 10% -> 4% of each run, Pallas kernels for 0% -> 0%
where the time goes in v1:
time: 1810 us; the launch traced here: 1800 us
  waiting for transfers between devices  1380 us (76%)
  Pallas kernels  134 us (7%)
  blocking collectives  126 us (7%)
  matrix products  69 us (4%)
  other arithmetic  40.1 us (2%)
  local copies, waits for them, and re-layouts  34.5 us (2%)
    reduce_scatter x4, waiting for transfers between devices, dense_body(): lax.psum_scatter(dot_tn(first, second).astype(jnp.bfloat16), 'dp', scatte...  295 us
    reduce_scatter x1, waiting for transfers between devices, dense_body(): returned = lax.psum_scatter(r_part, EVERY, scatter_dimension=0, tiled=True)  248 us
    reduce_scatter x1, waiting for transfers between devices, dense_body(): mixture = lax.psum_scatter(y_part, EVERY, scatter_dimension=0, tiled=True)  246 us
    all_gather x1, waiting for transfers between devices, dense_body(): rows_all = lax.all_gather(normed_two, EVERY, axis=0, tiled=True)  157 us
    pallas_call x1, Pallas kernels, expert_pass(): pl.pallas_call(expert_kernel, grid=(count // tile,), in_specs=[by_row(wid...  134 us
    unnamed x19, waiting for transfers between devices  103 us
    all_gather x1, blocking collectives, dense_body(): lax.all_gather(jnp.where(own_hot, own_probs, 0.0), EVERY, axis=0, tiled=T...  73.9 us
    reduce_scatter x2, waiting for transfers between devices, sum_rows(): return lax.psum_scatter(values, 'tensor', scatter_dimension=0, tiled=True)  58.1 us
  transfers between devices with their start and end apart: 18, of which 17 were waited for; matrix products, arithmetic and copies ran while one was open for 4% of the time, Pallas kernels for 0%

profile of v1, /device:TPU:0, one launch (start us, length us, event | category | flops | bytes accessed | tf_op | source)
XLA Modules:
  0.0 1804.5 jit_solution(17038261050487517374)
XLA Ops:
  18.6 24.4 %all-gather.10.cloned.1.call-done = bf16[384,2048]{1,0:T(8,128)(2,1)} async-done(((bf16[192,2048]{1,0:T(8,128)(2,1)}), bf16[384,2048]{1,0:T(8,128)(2,1)}) %all-gather.10.cloned.1.call-update) | async-done | bytes 1572880 | tf_op jit(solution)/shard_map/all_gather | solution.py:26
  43.0 52.9 %all-gather.14.cloned.1.call-done = bf16[2048,1024]{1,0:T(8,128)(2,1)} async-done(((bf16[128,1024]{1,0:T(8,128)(2,1)}), bf16[2048,1024]{1,0:T(8,128)(2,1)}) %all-gather.14.cloned.1.call-update) | async-done | bytes 4194320 | tf_op jit(solution)/shard_map/all_gather | solution.py:482
  95.9 5.1 multiply_reduce_fusion.9
  101.0 46.1 %all-gather.16.cloned.1.call-done = bf16[2048,1024]{1,0:T(8,128)(2,1)} async-done(((bf16[128,1024]{1,0:T(8,128)(2,1)}), bf16[2048,1024]{1,0:T(8,128)(2,1)}) %all-gather.16.cloned.1.call-update) | async-done | bytes 4194320 | tf_op jit(solution)/shard_map/all_gather | solution.py:483
  147.2 5.1 multiply_reduce_fusion.8
  152.3 5.9 all-reduce.2
  173.6 24.7 %all-gather.12.cloned.1.call-done = bf16[2048,1024]{1,0:T(8,128)(2,1)} async-done(((bf16[128,1024]{1,0:T(8,128)(2,1)}), bf16[2048,1024]{1,0:T(8,128)(2,1)}) %all-gather.12.cloned.1.call-update) | async-done | bytes 4194320 | tf_op jit(solution)/shard_map/all_gather | solution.py:484
  204.5 47.6 %all-gather.18.cloned.1.call-done = bf16[1024,2048]{1,0:T(8,128)(2,1)} async-done(((bf16[1024,128]{1,0:T(8,128)(2,1)}), bf16[1024,2048]{1,0:T(8,128)(2,1)}) %all-gather.18.cloned.1.call-update) | async-done | bytes 4194320 | tf_op jit(solution)/shard_map/all_gather | solution.py:485
  252.0 5.7 fusion.55
  258.4 41.3 %reduce-scatter.12.cloned.1.call-done = f32[192,2048]{1,0:T(8,128)} async-done(((f32[384,2048]{1,0:T(8,128)}), f32[192,2048]{1,0:T(8,128)}) %reduce-scatter.12.cloned.1.call-update) | async-done | bytes 1572880 | tf_op jit(solution)/shard_map/reduce_scatter | solution.py:30
  304.2 73.9 %all-gather = f32[32,192,16]{1,2,0:T(8,128)S(1)} all-gather(f32[1,192,16]{1,2,0:T(8,128)S(1)} %select_bitcast_fusion), channel_id=1, replica_groups=mesh['dp'=16,'tensor'=2] {'dp','tensor'}, dimensions={0}, use_global_device_ids=true | all-gather | bytes 405504 | tf_op jit(solution)/shard_map/all_gather | solution.py:533
  380.4 4.5 constant_dynamic-slice_fusion.gate_ref
  384.9 55.3 %all-gather.22.cloned.1.call-done.g_ref = bf16[6144,2048]{1,0:T(8,128)(2,1)} async-done(((bf16[192,2048]{1,0:T(8,128)(2,1)}), bf16[6144,2048]{1,0:T(8,128)(2,1)}) %all-gather.22.cloned.1.call-update) | async-done | bytes 25165840 | tf_op jit(solution)/shard_map/all_gather | solution.py:486
  440.2 156.6 %all-gather.20.cloned.1.call-done.x_ref = bf16[6144,2048]{1,0:T(8,128)(2,1)} async-done(((bf16[192,2048]{1,0:T(8,128)(2,1)}), bf16[6144,2048]{1,0:T(8,128)(2,1)}) %all-gather.20.cloned.1.call-update) | async-done | bytes 25165840 | tf_op jit(solution)/shard_map/all_gather | solution.py:532
  596.8 134.2 %shard_map.254 = (bf16[6144,2048]{1,0:T(8,128)(2,1)}, bf16[6144,2048]{1,0:T(8,128)(2,1)}, f32[6144,1]{1,0:T(8,128)}, f32[2048,512]{1,0:T(8,128)}, f32[2048,512]{1,0:T(8,128)}, /*index=5*/f32[512,2048]{1,0:T(8,128)}) custom-call(bf16[6144,2048]{1,0:T(8,128)(2,1)} %all-gather.20.cloned.1.call-done.x_ref, ...), custom_call_target="tpu_custom_call" | custom-call | flops 115964116992 | bytes 119537664 | tf_op jit(solution)/shard_map/pallas_call | solution.py:426
  737.7 98.1 %reduce-scatter.28.cloned.1.call-done = f32[192,16]{1,0:T(8,128)} async-done(((f32[6144,16]{1,0:T(8,128)}), f32[192,16]{1,0:T(8,128)}) %reduce-scatter.28.cloned.1.call-update) | async-done | bytes 12304
  836.8 247.9 %reduce-scatter.16.cloned.1.call-done = bf16[192,2048]{1,0:T(8,128)(2,1)} async-done(((bf16[6144,2048]{1,0:T(8,128)(2,1)}), bf16[192,2048]{1,0:T(8,128)(2,1)}) %reduce-scatter.16.cloned.1.call-update) | async-done | bytes 786448 | tf_op jit(solution)/shard_map/reduce_scatter | solution.py:539
  1087.1 245.9 %reduce-scatter.14.cloned.1.call-done = bf16[192,2048]{1,0:T(8,128)(2,1)} async-done(((bf16[6144,2048]{1,0:T(8,128)(2,1)}), bf16[192,2048]{1,0:T(8,128)(2,1)}) %reduce-scatter.14.cloned.1.call-update) | async-done | bytes 786448 | tf_op jit(solution)/shard_map/reduce_scatter | solution.py:543
  1336.7 26.8 %all-gather.24.cloned.1.call-done = bf16[384,2048]{1,0:T(8,128)(2,1)} async-done(((bf16[192,2048]{1,0:T(8,128)(2,1)}), bf16[384,2048]{1,0:T(8,128)(2,1)}) %all-gather.24.cloned.1.call-update) | async-done | bytes 1572880 | tf_op jit(solution)/shard_map/all_gather | solution.py:26
  1363.5 4.5 convolution_convert_fusion.4
  1368.4 4.3 fusion.19
  1388.7 5.1 all-reduce.1
  1406.7 6.2 convolution_convert_fusion
  1413.0 5.8 convolution_convert_fusion.1
  1420.4 4.3 convolution_convert_fusion.2
  1424.8 4.4 convolution_convert_fusion.3
  1432.3 16.8 reduce-scatter.18.cloned.1.call-done
  1452.7 73.1 %reduce-scatter.26.cloned.1.call-done = bf16[128,1024]{1,0:T(8,128)(2,1)} async-done(((bf16[2048,1024]{1,0:T(8,128)(2,1)}), bf16[128,1024]{1,0:T(8,128)(2,1)}) %reduce-scatter.26.cloned.1.call-update) | async-done | bytes 262160 | tf_op jit(solution)/shard_map/reduce_scatter | solution.py:606
  1527.9 73.5 %reduce-scatter.24.cloned.1.call-done = bf16[128,1024]{1,0:T(8,128)(2,1)} async-done(((bf16[2048,1024]{1,0:T(8,128)(2,1)}), bf16[128,1024]{1,0:T(8,128)(2,1)}) %reduce-scatter.24.cloned.1.call-update) | async-done | bytes 262160 | tf_op jit(solution)/shard_map/reduce_scatter | solution.py:606
  1603.2 73.8 %reduce-scatter.22.cloned.1.call-done = bf16[128,1024]{1,0:T(8,128)(2,1)} async-done(((bf16[2048,1024]{1,0:T(8,128)(2,1)}), bf16[128,1024]{1,0:T(8,128)(2,1)}) %reduce-scatter.22.cloned.1.call-update) | async-done | bytes 262160 | tf_op jit(solution)/shard_map/reduce_scatter | solution.py:606
  1678.8 74.1 %reduce-scatter.20.cloned.1.call-done = bf16[128,1024]{1,0:T(8,128)(2,1)} async-done(((bf16[2048,1024]{1,0:T(8,128)(2,1)}), bf16[128,1024]{1,0:T(8,128)(2,1)}) %reduce-scatter.20.cloned.1.call-update) | async-done | bytes 262160 | tf_op jit(solution)/shard_map/reduce_scatter | solution.py:606
  1754.7 40.6 %all-reduce = (f32[2048]{0:T(1024)}, f32[2048]{0:T(1024)}, f32[2048]{0:T(1024)}, f32[2048]{0:T(1024)}) all-reduce(f32[2048]{0:T(1024)S(1)} %get-tuple-element.88, f32[2048]{0:T(1024)S(1)} %dynamic_update_slice.6, f32[2048]{0:T(1024)S(1)} %dynamic_update_slice.7, ...), channel_id=1, replica_groups=mesh['dp'=16,'tensor'=2] {'dp','tensor'}, use_global_device_ids=true, to_apply=%region_25.26 | all-reduce | flops 8192 | bytes 65536 | tf_op jit(solution)/shard_map/psum | solution.py:627
  (210 shorter events, 99.4 us)
Async XLA Ops:
  8.0 294.7 %copy-start = (bf16[2048,16]{0,1:T(8,128)(2,1)S(1)}, bf16[2048,16]{0,1:T(8,128)(2,1)}, u32[]{:S(2)}) copy-start(bf16[2048,16]{0,1:T(8,128)(2,1)} %param.26) | copy-start | bytes 196612
  8.0 35.0 %all-gather.10.cloned.1.call-start = ((), (), s32[]{:S(2)}) async-start(), calls=%async_computation.9 | async-start | bytes 2359296 | tf_op jit(solution)/shard_map/all_gather | solution.py:26
  12.9 83.0 %all-gather.14.cloned.1.call-start = ((), (), s32[]{:S(2)}) async-start(), calls=%async_computation.11 | async-start | bytes 4456448 | tf_op jit(solution)/shard_map/all_gather | solution.py:482
  13.7 133.5 %all-gather.16.cloned.1.call-start = ((), (), s32[]{:S(2)}) async-start(), calls=%async_computation.12 | async-start | bytes 4456448 | tf_op jit(solution)/shard_map/all_gather | solution.py:483
  14.4 183.9 %all-gather.12.cloned.1.call-start = ((), (), s32[]{:S(2)}) async-start(), calls=%async_computation.10 | async-start | bytes 4456448 | tf_op jit(solution)/shard_map/all_gather | solution.py:484
  15.0 237.0 %all-gather.18.cloned.1.call-start = ((), (), s32[]{:S(2)}) async-start(), calls=%async_computation.13 | async-start | bytes 4456448 | tf_op jit(solution)/shard_map/all_gather | solution.py:485
  15.6 284.1 %reduce-scatter.12.cloned.1.call-start = ((), (), s32[]{:S(2)}) async-start(), calls=%async_computation.14 | async-start | bytes 4718592 | tf_op jit(solution)/shard_map/reduce_scatter | solution.py:30
  101.0 58.5 %copy-start.5 = (f32[384,1024]{1,0:T(8,128)}, f32[384,1024]{1,0:T(8,128)S(1)}, u32[]{:S(2)}) copy-start(f32[384,1024]{1,0:T(8,128)S(1)} %get-tuple-element.130) | copy-start | bytes 4718596
  152.3 11.7 copy-start.7
  173.0 25.3 %copy-start.44 = (bf16[384,2048]{1,0:T(8,128)(2,1)S(1)}, bf16[384,2048]{1,0:T(8,128)(2,1)}, u32[]{:S(2)}) copy-start(bf16[384,2048]{1,0:T(8,128)(2,1)} %all-gather.10.cloned.1.call-done) | copy-start | bytes 4718596
  204.5 53.2 %copy-start.16 = (bf16[8,128,384]{2,1,0:T(8,128)(2,1)}, bf16[8,128,384]{2,1,0:T(8,128)(2,1)S(1)}, u32[]{:S(2)}) copy-start(bf16[8,128,384]{2,1,0:T(8,128)(2,1)S(1)} %fusion.18) | copy-start | bytes 2359300
  257.7 41.9 %copy-start.3 = (bf16[192,2048]{1,0:T(8,128)(2,1)S(1)}, bf16[192,2048]{1,0:T(8,128)(2,1)}, u32[]{:S(2)}) copy-start(bf16[192,2048]{1,0:T(8,128)(2,1)} %param.15) | copy-start | bytes 2359300
  257.8 182.4 %all-gather.22.cloned.1.call-start = ((), (), s32[]{:S(2)}) async-start(), calls=%async_computation.16 | async-start | bytes 25952256 | tf_op jit(solution)/shard_map/all_gather | solution.py:486
  258.3 43.1 %copy-start.27 = (f32[2048]{0:T(1024)S(1)}, f32[2048]{0:T(1024)}, u32[]{:S(2)}) copy-start(f32[2048]{0:T(1024)} %param.25) | copy-start | bytes 24580
  258.3 338.4 %all-gather.20.cloned.1.call-start = ((), (), s32[]{:S(2)}) async-start(), calls=%async_computation.15 | async-start | bytes 25952256 | tf_op jit(solution)/shard_map/all_gather | solution.py:532
  302.5 533.3 %reduce-scatter.28.cloned.1.call-start = ((), (), s32[]{:S(2)}) async-start(), calls=%async_computation.26 | async-start | bytes 3244032
  736.0 348.7 %reduce-scatter.16.cloned.1.call-start = ((), (), s32[]{:S(2)}) async-start(), calls=%async_computation.18 | async-start | bytes 25952256 | tf_op jit(solution)/shard_map/reduce_scatter | solution.py:539
  736.8 596.2 %reduce-scatter.14.cloned.1.call-start = ((), (), s32[]{:S(2)}) async-start(), calls=%async_computation.17 | async-start | bytes 25952256 | tf_op jit(solution)/shard_map/reduce_scatter | solution.py:543
  737.5 626.0 %all-gather.24.cloned.1.call-start = ((), (), s32[]{:S(2)}) async-start(), calls=%async_computation.19 | async-start | bytes 2359296 | tf_op jit(solution)/shard_map/all_gather | solution.py:26
  1336.6 112.5 %reduce-scatter.18.cloned.1.call-start = ((), (), s32[]{:S(2)}) async-start(), calls=%async_computation.20 | async-start | bytes 4718592 | tf_op jit(solution)/shard_map/reduce_scatter | solution.py:30
  1368.4 7.7 slice-start
  1386.9 7.0 copy-start.36
  1405.5 120.3 %reduce-scatter.26.cloned.1.call-start = ((), (), s32[]{:S(2)}) async-start(), calls=%async_computation.24 | async-start | bytes 4456448 | tf_op jit(solution)/shard_map/reduce_scatter | solution.py:606
  1412.9 188.5 %reduce-scatter.24.cloned.1.call-start = ((), (), s32[]{:S(2)}) async-start(), calls=%async_computation.23 | async-start | bytes 4456448 | tf_op jit(solution)/shard_map/reduce_scatter | solution.py:606
  1418.8 258.2 %reduce-scatter.22.cloned.1.call-start = ((), (), s32[]{:S(2)}) async-start(), calls=%async_computation.22 | async-start | bytes 4456448 | tf_op jit(solution)/shard_map/reduce_scatter | solution.py:606
  1424.8 328.1 %reduce-scatter.20.cloned.1.call-start = ((), (), s32[]{:S(2)}) async-start(), calls=%async_computation.21 | async-start | bytes 4456448 | tf_op jit(solution)/shard_map/reduce_scatter | solution.py:606
  1429.2 19.9 %copy-start.26 = (f32[2048]{0:T(1024)S(1)}, f32[2048]{0:T(1024)}, u32[]{:S(2)}) copy-start(f32[2048]{0:T(1024)} %param.18) | copy-start | bytes 24580
  1429.2 19.9 %copy-start.34 = (f32[192]{0:T(256)S(1)}, f32[192]{0:T(256)}, u32[]{:S(2)}) copy-start(f32[192]{0:T(256)} %copy-done.33) | copy-start | bytes 2308
  1429.2 21.9 %copy-start.15 = (f32[192,2048]{1,0:T(8,128)S(1)}, f32[192,2048]{1,0:T(8,128)}, u32[]{:S(2)}) copy-start(f32[192,2048]{1,0:T(8,128)} %get-tuple-element.99) | copy-start | bytes 4718596
  1429.3 19.8 %copy-start.4 = (bf16[192,2048]{1,0:T(8,128)(2,1)S(1)}, bf16[192,2048]{1,0:T(8,128)(2,1)}, u32[]{:S(2)}) copy-start(bf16[192,2048]{1,0:T(8,128)(2,1)} %param.15) | copy-start | bytes 2359300
  1429.3 21.8 %copy-start.38 = (f32[192]{0:T(256)S(1)}, f32[192]{0:T(256)}, u32[]{:S(2)}) copy-start(f32[192]{0:T(256)} %get-tuple-element.125) | copy-start | bytes 2308
  1429.3 366.0 %all-reduce.5.cloned.1.call-start = ((), (), s32[]{:S(2)}) async-start(), calls=%async_computation.25 | async-start | bytes 262144 | tf_op jit(solution)/shard_map/psum | solution.py:627
  (34 other events, 68.2 us)
Sparse Core Ops, SparseCore 0:
  13.1 29.8 all-gather.9
  45.2 50.7 all-gather.13
  98.1 49.0 all-gather.15
  149.2 49.0 all-gather.11
  200.3 51.7 all-gather.17
  257.9 41.7 reduce-scatter.11
  1336.7 26.7 all-gather.23
  1405.7 43.3 reduce-scatter.17
  1453.0 72.8 reduce-scatter.25
  1530.1 71.2 reduce-scatter.23
  1605.3 71.6 reduce-scatter.21
  1681.2 71.6 reduce-scatter.19
Sparse Core Ops, SparseCore 1:
  261.5 178.6 all-gather.21
  443.4 153.3 all-gather.19
  736.1 99.6 reduce-scatter.27
  843.4 241.2 reduce-scatter.15
  1091.1 241.8 reduce-scatter.13
  1436.2 138.8 all-reduce.4

commit v2 on v1

--- a/solution.py
+++ b/solution.py
@@ -1,3 +1,5 @@
+import functools
+
 import jax
 import jax.numpy as jnp
 from jax import lax
@@ -354,6 +356,572 @@
     )
 
 
+MESH_ID = pl.DeviceIdType.MESH
+EVERY = ("dp", "tensor")
+LANES = 128
+ANYWHERE = pl.BlockSpec(memory_space=pl.ANY)
+IN_VMEM = pl.BlockSpec(memory_space=pltpu.VMEM)
+
+
+class Place:
+    def __init__(self):
+        dp = lax.axis_index("dp")
+        self.y = lax.axis_index("tensor")
+        self.z, self.x, self.c = dp // 4, (dp // 2) % 2, dp % 2
+        self.z_count = lax.axis_size("dp") // 4
+
+    def device(self, z=None, x=None, c=None, y=None):
+        z = self.z if z is None else z
+        x = self.x if x is None else x
+        c = self.c if c is None else c
+        y = self.y if y is None else y
+        return (z * 4 + x * 2 + c, y)
+
+    def meet(self, use_y=True):
+        barrier = pltpu.get_barrier_semaphore()
+        partners = [self.device(x=1 - self.x), self.device(c=1 - self.c)]
+        if use_y:
+            partners.append(self.device(y=1 - self.y))
+        for partner in partners:
+            pl.semaphore_signal(barrier, inc=1, device_id=partner, device_id_type=MESH_ID)
+
+        @pl.when(self.z > 0)
+        def _():
+            pl.semaphore_signal(
+                barrier, inc=1, device_id=self.device(z=self.z - 1), device_id_type=MESH_ID
+            )
+
+        @pl.when(self.z < self.z_count - 1)
+        def _():
+            pl.semaphore_signal(
+                barrier, inc=1, device_id=self.device(z=self.z + 1), device_id_type=MESH_ID
+            )
+
+        ends = jnp.where(self.z > 0, 1, 0) + jnp.where(self.z < self.z_count - 1, 1, 0)
+        pl.semaphore_wait(barrier, len(partners) + ends)
+
+    def far_first(self, step):
+        last = self.z_count - 1
+        low = jnp.where(step < last - self.z, last - step, step - (last - self.z))
+        high = jnp.where(step < self.z, step, last - (step - self.z))
+        return jnp.where(self.z * 2 < self.z_count, low, high)
+
+
+def send(src, dst, send_sem, recv_sem, device):
+    copy = pltpu.make_async_remote_copy(
+        src_ref=src, dst_ref=dst, send_sem=send_sem, recv_sem=recv_sem, device_id=device, device_id_type=MESH_ID
+    )
+    copy.start()
+    return copy
+
+
+def add_rows(total, part, rows, step=16):
+    def chunk(i, carry):
+        here = pl.ds(pl.multiple_of(i * step, step), step)
+        total[here] = total[here] + part[here]
+        return carry
+
+    lax.fori_loop(0, rows // step, chunk, 0)
+
+
+def spread_rows(place, src, whole, half, sems):
+    z, x, c, y, nz = place.z, place.x, place.c, place.y, place.z_count
+    sent, got, kept = sems
+    ZU, ZD, XF, YF, XH, YH, CO, CX, CY, CA, CB = range(11)
+    up, down = place.device(z=z + 1), place.device(z=z - 1)
+    over_x, over_y, over_c = place.device(x=1 - x), place.device(y=1 - y), place.device(c=1 - c)
+    full = slice(None)
+    low, high = pl.ds(0, half), pl.ds(half, half)
+
+    def at(zz, xx, yy, rows=full):
+        return whole.at[zz, xx, c, yy, rows]
+
+    def push(kind, zz, xx, yy, rows, device, origin=None):
+        ref = at(zz, xx, yy, rows)
+        send(ref if origin is None else origin, ref, sent.at[kind, zz], got.at[kind, zz], device)
+
+    def arrival(kind, zz, xx, yy, rows=full, cc=None):
+        ref = whole.at[zz, xx, c if cc is None else cc, yy, rows]
+        pltpu.make_async_copy(ref, ref, got.at[kind, zz]).wait()
+
+    def departure(kind, zz, xx, yy, rows=full):
+        ref = at(zz, xx, yy, rows)
+        pltpu.make_async_copy(ref, ref, sent.at[kind, zz]).wait()
+
+    def spread_own(zz, origin=None):
+        push(XF, zz, x, y, full, over_x, origin)
+        push(YF, zz, x, y, full, over_y, origin)
+        push(CO, zz, x, y, full, over_c, origin)
+
+    @pl.when(z < nz - 1)
+    def _():
+        push(ZU, z, x, y, full, up, src)
+
+    @pl.when(z > 0)
+    def _():
+        push(ZD, z, x, y, full, down, src)
+
+    spread_own(z, src)
+    keep = pltpu.make_async_copy(src, at(z, x, y), kept)
+    keep.start()
+
+    def relay(zz):
+        arrival(XF, zz, 1 - x, y)
+        push(YH, zz, 1 - x, y, low, over_y)
+        push(CX, zz, 1 - x, y, full, over_c)
+        arrival(YF, zz, x, 1 - y)
+        push(XH, zz, x, 1 - y, high, over_x)
+        push(CY, zz, x, 1 - y, full, over_c)
+
+    for d in range(nz):
+        below, above = z - d - 1, z + d + 1
+        if d < nz - 1:
+            @pl.when(below >= 0)
+            def _():
+                arrival(ZU, below, x, y)
+
+                @pl.when(z < nz - 1)
+                def _():
+                    push(ZU, below, x, y, full, up)
+
+                spread_own(below)
+
+            @pl.when(above < nz)
+            def _():
+                arrival(ZD, above, x, y)
+
+                @pl.when(z > 0)
+                def _():
+                    push(ZD, above, x, y, full, down)
+
+                spread_own(above)
+
+        if d == 0:
+            relay(z)
+        else:
+            @pl.when(z - d >= 0)
+            def _():
+                relay(z - d)
+
+            @pl.when(z + d < nz)
+            def _():
+                relay(z + d)
+
+    def diagonal(zz):
+        arrival(XH, zz, 1 - x, 1 - y, high)
+        push(CB, zz, 1 - x, 1 - y, high, over_c)
+        arrival(YH, zz, 1 - x, 1 - y, low)
+        push(CA, zz, 1 - x, 1 - y, low, over_c)
+
+    diagonal(z)
+    for d in range(1, nz):
+        @pl.when(z - d >= 0)
+        def _():
+            diagonal(z - d)
+
+        @pl.when(z + d < nz)
+        def _():
+            diagonal(z + d)
+
+    keep.wait()
+    for zz in range(nz):
+        arrival(CO, zz, x, y, cc=1 - c)
+        arrival(CX, zz, 1 - x, y, cc=1 - c)
+        arrival(CY, zz, x, 1 - y, cc=1 - c)
+        arrival(CA, zz, 1 - x, 1 - y, low, cc=1 - c)
+        arrival(CB, zz, 1 - x, 1 - y, high, cc=1 - c)
+        departure(XF, zz, x, y)
+        departure(YF, zz, x, y)
+        departure(CO, zz, x, y)
+        departure(CX, zz, 1 - x, y)
+        departure(CY, zz, x, 1 - y)
+        departure(YH, zz, 1 - x, y, low)
+        departure(XH, zz, x, 1 - y, high)
+        departure(CA, zz, 1 - x, 1 - y, low)
+        departure(CB, zz, 1 - x, 1 - y, high)
+
+        @pl.when((zz <= z) & (z < nz - 1))
+        def _():
+            departure(ZU, zz, x, y)
+
+        @pl.when((zz >= z) & (z > 0))
+        def _():
+            departure(ZD, zz, x, y)
+
+
+def gather_kernel(src, whole, sent, got, kept):
+    place = Place()
+    place.meet()
+    spread_rows(place, src, whole, src.shape[0] // 2, (sent, got, kept))
+
+
+def gather_everywhere(block, collective):
+    rows, cols = block.shape
+    nz = lax.axis_size("dp") // 4
+    return pl.pallas_call(
+        gather_kernel,
+        out_shape=jax.ShapeDtypeStruct((nz, 2, 2, 2, rows, cols), block.dtype),
+        in_specs=[ANYWHERE],
+        out_specs=ANYWHERE,
+        scratch_shapes=[
+            pltpu.SemaphoreType.DMA((11, nz)),
+            pltpu.SemaphoreType.DMA((11, nz)),
+            pltpu.SemaphoreType.DMA,
+        ],
+        compiler_params=pltpu.CompilerParams(collective_id=collective, has_side_effects=True),
+    )(block)
+
+
+def scatter_kernel(parts, out, total, from_c, half_x, half_y, full_x, full_y, up_buf, down_buf, sent, got, loaded):
+    place = Place()
+    z, x, c, y, nz = place.z, place.x, place.c, place.y, place.z_count
+    rows = total.shape[3]
+    half = rows // 2
+    CD, CX, CY, CO, XH, YH, XF, YF, ZU, ZD = range(10)
+    over_x, over_y, over_c = place.device(x=1 - x), place.device(y=1 - y), place.device(c=1 - c)
+    place.meet()
+
+    def spot(kind):
+        return {CD: (1, 1), CX: (1, 0), CY: (0, 1), CO: (0, 0)}[kind]
+
+    for kind in (CD, CX, CY, CO):
+        dx, dy = spot(kind)
+        for i in range(nz):
+            zz = place.far_first(i)
+            xx, yy = (1 - x if dx else x), (1 - y if dy else y)
+            send(parts.at[zz, xx, 1 - c, yy], from_c.at[dx, dy, zz], sent.at[kind, zz], got.at[kind, zz], over_c)
+            pltpu.make_async_copy(parts.at[zz, xx, c, yy], total.at[dx, dy, zz], loaded.at[kind, zz]).start()
+
+    def arrival(kind, zz, ref):
+        pltpu.make_async_copy(ref, ref, got.at[kind, zz]).wait()
+
+    def join_cores(kind, zz):
+        dx, dy = spot(kind)
+        here, there = total.at[dx, dy, zz], from_c.at[dx, dy, zz]
+        pltpu.make_async_copy(here, here, loaded.at[kind, zz]).wait()
+        arrival(kind, zz, there)
+        add_rows(here, there, rows)
+
+    low, high = pl.ds(0, half), pl.ds(half, half)
+    for i in range(nz):
+        zz = place.far_first(i)
+        join_cores(CD, zz)
+        send(total.at[1, 1, zz, low], half_x.at[zz], sent.at[XH, zz], got.at[XH, zz], over_x)
+        send(total.at[1, 1, zz, high], half_y.at[zz], sent.at[YH, zz], got.at[YH, zz], over_y)
+    for i in range(nz):
+        zz = place.far_first(i)
+        join_cores(CX, zz)
+        join_cores(CY, zz)
+        arrival(XH, zz, half_x.at[zz])
+        add_rows(total.at[0, 1, zz, low], half_x.at[zz], half)
+        send(total.at[0, 1, zz], full_y.at[zz], sent.at[YF, zz], got.at[YF, zz], over_y)
+        arrival(YH, zz, half_y.at[zz])
+        add_rows(total.at[1, 0, zz, high], half_y.at[zz], half)
+        send(total.at[1, 0, zz], full_x.at[zz], sent.at[XF, zz], got.at[XF, zz], over_x)
+    for i in range(nz):
+        zz = place.far_first(i)
+        mine = total.at[0, 0, zz]
+        join_cores(CO, zz)
+        arrival(XF, zz, full_x.at[zz])
+        add_rows(mine, full_x.at[zz], rows)
+        arrival(YF, zz, full_y.at[zz])
+        add_rows(mine, full_y.at[zz], rows)
+
+        @pl.when((z > 0) & (zz >= z))
+        def _():
+            arrival(ZU, zz, up_buf.at[zz])
+            add_rows(mine, up_buf.at[zz], rows)
+
+        @pl.when((z < nz - 1) & (zz <= z))
+        def _():
+            arrival(ZD, zz, down_buf.at[zz])
+            add_rows(mine, down_buf.at[zz], rows)
+
+        @pl.when(zz > z)
+        def _():
+            send(mine, up_buf.at[zz], sent.at[ZU, zz], got.at[ZU, zz], place.device(z=z + 1))
+
+        @pl.when(zz < z)
+        def _():
+            send(mine, down_buf.at[zz], sent.at[ZD, zz], got.at[ZD, zz], place.device(z=z - 1))
+
+    out[...] = total[0, 0, z]
+
+    def departure(kind, zz, ref):
+        pltpu.make_async_copy(ref, ref, sent.at[kind, zz]).wait()
+
+    for zz in range(nz):
+        for kind in (CD, CX, CY, CO):
+            departure(kind, zz, total.at[0, 0, zz])
+        departure(XH, zz, half_x.at[zz])
+        departure(YH, zz, half_y.at[zz])
+        departure(XF, zz, full_x.at[zz])
+        departure(YF, zz, full_y.at[zz])
+
+        @pl.when(zz > z)
+        def _():
+            departure(ZU, zz, up_buf.at[zz])
+
+        @pl.when(zz < z)
+        def _():
+            departure(ZD, zz, down_buf.at[zz])
+
+
+def scatter_sum(parts, collective):
+    nz, _, _, _, rows, cols = parts.shape
+    dt = parts.dtype
+    return pl.pallas_call(
+        scatter_kernel,
+        out_shape=jax.ShapeDtypeStruct((rows, cols), dt),
+        in_specs=[ANYWHERE],
+        out_specs=IN_VMEM,
+        scratch_shapes=[
+            pltpu.VMEM((2, 2, nz, rows, cols), dt),
+            pltpu.VMEM((2, 2, nz, rows, cols), dt),
+            pltpu.VMEM((nz, rows // 2, cols), dt),
+            pltpu.VMEM((nz, rows // 2, cols), dt),
+            pltpu.VMEM((nz, rows, cols), dt),
+            pltpu.VMEM((nz, rows, cols), dt),
+            pltpu.VMEM((nz, rows, cols), dt),
+            pltpu.VMEM((nz, rows, cols), dt),
+            pltpu.SemaphoreType.DMA((10, nz)),
+            pltpu.SemaphoreType.DMA((10, nz)),
+            pltpu.SemaphoreType.DMA((4, nz)),
+        ],
+        compiler_params=pltpu.CompilerParams(
+            collective_id=collective, has_side_effects=True, vmem_limit_bytes=58 << 20
+        ),
+    )(parts)
+
+
+def plane_gather_kernel(count, *refs):
+    srcs, outs = refs[:count], refs[count : 2 * count]
+    sent, got, kept = refs[2 * count :]
+    place = Place()
+    z, x, c, nz = place.z, place.x, place.c, place.z_count
+    ZU, ZD, XF, CO, CX = range(5)
+    up, down = place.device(z=z + 1), place.device(z=z - 1)
+    over_x, over_c = place.device(x=1 - x), place.device(c=1 - c)
+    place.meet(use_y=False)
+    every = range(count)
+
+    def push(a, kind, zz, xx, device, own=False):
+        ref = outs[a].at[zz, xx, c]
+        send(srcs[a] if own else ref, ref, sent.at[kind, a, zz], got.at[kind, a, zz], device)
+
+    def arrival(a, kind, zz, xx, cc):
+        ref = outs[a].at[zz, xx, cc]
+        pltpu.make_async_copy(ref, ref, got.at[kind, a, zz]).wait()
+
+    def departure(a, kind, zz, xx):
+        ref = outs[a].at[zz, xx, c]
+        pltpu.make_async_copy(ref, ref, sent.at[kind, a, zz]).wait()
+
+    keeps = []
+    for a in every:
+        push(a, XF, z, x, over_x, own=True)
+
+        @pl.when(z < nz - 1)
+        def _():
+            push(a, ZU, z, x, up, own=True)
+
+        @pl.when(z > 0)
+        def _():
+            push(a, ZD, z, x, down, own=True)
+
+        push(a, CO, z, x, over_c, own=True)
+        keep = pltpu.make_async_copy(srcs[a], outs[a].at[z, x, c], kept.at[a])
+        keep.start()
+        keeps.append(keep)
+
+    def relay(a, zz):
+        arrival(a, XF, zz, 1 - x, c)
+        push(a, CX, zz, 1 - x, over_c)
+
+    for d in range(nz):
+        below, above = z - d - 1, z + d + 1
+        for a in every:
+            if d < nz - 1:
+                @pl.when(below >= 0)
+                def _():
+                    arrival(a, ZU, below, x, c)
+
+                    @pl.when(z < nz - 1)
+                    def _():
+                        push(a, ZU, below, x, up)
+
+                    push(a, XF, below, x, over_x)
+                    push(a, CO, below, x, over_c)
+
+                @pl.when(above < nz)
+                def _():
+                    arrival(a, ZD, above, x, c)
+
+                    @pl.when(z > 0)
+                    def _():
+                        push(a, ZD, above, x, down)
+
+                    push(a, XF, above, x, over_x)
+                    push(a, CO, above, x, over_c)
+
+    for d in range(nz):
+        for a in every:
+            if d == 0:
+                relay(a, z)
+            else:
+                @pl.when(z - d >= 0)
+                def _():
+                    relay(a, z - d)
+
+                @pl.when(z + d < nz)
+                def _():
+                    relay(a, z + d)
+
+    for a in every:
+        keeps[a].wait()
+        for zz in range(nz):
+            arrival(a, CO, zz, x, 1 - c)
+            arrival(a, CX, zz, 1 - x, 1 - c)
+            departure(a, XF, zz, x)
+            departure(a, CO, zz, x)
+            departure(a, CX, zz, 1 - x)
+
+            @pl.when((zz <= z) & (z < nz - 1))
+            def _():
+                departure(a, ZU, zz, x)
+
+            @pl.when((zz >= z) & (z > 0))
+            def _():
+                departure(a, ZD, zz, x)
+
+
+def gather_in_plane(shards, collective):
+    nz = lax.axis_size("dp") // 4
+    count = len(shards)
+    return pl.pallas_call(
+        functools.partial(plane_gather_kernel, count),
+        out_shape=[jax.ShapeDtypeStruct((nz, 2, 2) + s.shape, s.dtype) for s in shards],
+        in_specs=[ANYWHERE] * count,
+        out_specs=[ANYWHERE] * count,
+        scratch_shapes=[
+            pltpu.SemaphoreType.DMA((5, count, nz)),
+            pltpu.SemaphoreType.DMA((5, count, nz)),
+            pltpu.SemaphoreType.DMA((count,)),
+        ],
+        compiler_params=pltpu.CompilerParams(collective_id=collective, has_side_effects=True),
+    )(*shards)
+
+
+def plane_scatter_kernel(count, *refs):
+    parts, outs = refs[:count], refs[count : 2 * count]
+    total, from_c, full_x, up_buf, down_buf, sent, got, loaded = refs[2 * count :]
+    place = Place()
+    z, x, c, nz = place.z, place.x, place.c, place.z_count
+    rows = total.shape[3]
+    C0, C1, XF, ZU, ZD = range(5)
+    over_x, over_c = place.device(x=1 - x), place.device(c=1 - c)
+    place.meet(use_y=False)
+
+    def arrival(a, kind, zz, ref):
+        pltpu.make_async_copy(ref, ref, got.at[kind, a, zz]).wait()
+
+    for dx, kind in ((1, C1), (0, C0)):
+        for i in range(nz):
+            zz = place.far_first(i)
+            xx = 1 - x if dx else x
+            for a in range(count):
+                send(parts[a].at[zz, xx, 1 - c], from_c.at[dx, zz, a], sent.at[kind, a, zz], got.at[kind, a, zz], over_c)
+                pltpu.make_async_copy(parts[a].at[zz, xx, c], total.at[dx, zz, a], loaded.at[dx, a, zz]).start()
+
+    def join_cores(a, dx, zz):
+        here, there = total.at[dx, zz, a], from_c.at[dx, zz, a]
+        pltpu.make_async_copy(here, here, loaded.at[dx, a, zz]).wait()
+        arrival(a, C1 if dx else C0, zz, there)
+        add_rows(here, there, rows)
+
+    for i in range(nz):
+        zz = place.far_first(i)
+        for a in range(count):
+            join_cores(a, 1, zz)
+            send(total.at[1, zz, a], full_x.at[zz, a], sent.at[XF, a, zz], got.at[XF, a, zz], over_x)
+    for i in range(nz):
+        zz = place.far_first(i)
+        for a in range(count):
+            mine = total.at[0, zz, a]
+            join_cores(a, 0, zz)
+            arrival(a, XF, zz, full_x.at[zz, a])
+            add_rows(mine, full_x.at[zz, a], rows)
+
+            @pl.when((z > 0) & (zz >= z))
+            def _():
+                arrival(a, ZU, zz, up_buf.at[zz, a])
+                add_rows(mine, up_buf.at[zz, a], rows)
+
+            @pl.when((z < nz - 1) & (zz <= z))
+            def _():
+                arrival(a, ZD, zz, down_buf.at[zz, a])
+                add_rows(mine, down_buf.at[zz, a], rows)
+
+            @pl.when(zz > z)
+            def _():
+                send(mine, up_buf.at[zz, a], sent.at[ZU, a, zz], got.at[ZU, a, zz], place.device(z=z + 1))
+
+            @pl.when(zz < z)
+            def _():
+                send(mine, down_buf.at[zz, a], sent.at[ZD, a, zz], got.at[ZD, a, zz], place.device(z=z - 1))
+
+    for a in range(count):
+
+        def widen(i, carry):
+            here = pl.ds(pl.multiple_of(i * 16, 16), 16)
+            outs[a][here] = total[0, z, a, here].astype(jnp.float32)
+            return carry
+
+        lax.fori_loop(0, rows // 16, widen, 0)
+
+    def departure(a, kind, zz, ref):
+        pltpu.make_async_copy(ref, ref, sent.at[kind, a, zz]).wait()
+
+    for a in range(count):
+        for zz in range(nz):
+            departure(a, C0, zz, total.at[0, 0, a])
+            departure(a, C1, zz, total.at[0, 0, a])
+            departure(a, XF, zz, total.at[0, 0, a])
+
+            @pl.when(zz > z)
+            def _():
+                departure(a, ZU, zz, total.at[0, 0, a])
+
+            @pl.when(zz < z)
+            def _():
+                departure(a, ZD, zz, total.at[0, 0, a])
+
+
+def scatter_in_plane(parts, collective):
+    nz, _, _, rows, cols = parts[0].shape
+    count = len(parts)
+    dt = parts[0].dtype
+    return pl.pallas_call(
+        functools.partial(plane_scatter_kernel, count),
+        out_shape=[jax.ShapeDtypeStruct((rows, cols), jnp.float32)] * count,
+        in_specs=[ANYWHERE] * count,
+        out_specs=[IN_VMEM] * count,
+        scratch_shapes=[
+            pltpu.VMEM((2, nz, count, rows, cols), dt),
+            pltpu.VMEM((2, nz, count, rows, cols), dt),
+            pltpu.VMEM((nz, count, rows, cols), dt),
+            pltpu.VMEM((nz, count, rows, cols), dt),
+            pltpu.VMEM((nz, count, rows, cols), dt),
+            pltpu.SemaphoreType.DMA((5, count, nz)),
+            pltpu.SemaphoreType.DMA((5, count, nz)),
+            pltpu.SemaphoreType.DMA((2, count, nz)),
+        ],
+        compiler_params=pltpu.CompilerParams(
+            collective_id=collective, has_side_effects=True, vmem_limit_bytes=58 << 20
+        ),
+    )(*parts)
+
+
 def dot_nn(a, b):
     return lax.dot_general(a, b, (((1,), (0,)), ((), ())), preferred_element_type=jnp.float32)
 
@@ -369,13 +937,14 @@
 def expert_kernel(
     x_ref,
     g_ref,
-    gate_ref,
+    hot_ref,
+    router_ref,
+    lanes_ref,
     wg_ref,
     wu_ref,
     wd_ref,
     y_ref,
     r_ref,
-    gate_grad_ref,
     wg_grad_ref,
     wu_grad_ref,
     wd_grad_ref,
@@ -388,14 +957,22 @@
 
     rows = x_ref[...]
     upstream = g_ref[...]
-    gate = gate_ref[...]
+    logits = jnp.where(lanes_ref[1:2] > 0.0, dot_nn(rows, router_ref[...]), -1e30)
+    weights = jnp.exp(logits - jnp.max(logits, axis=1, keepdims=True))
+    own_weight = jnp.sum(weights * lanes_ref[0:1], axis=1, keepdims=True)
+    gate = hot_ref[...] * own_weight / jnp.sum(weights, axis=1, keepdims=True)
     gate_pre = dot_nn(rows, wg_ref[...])
     up_pre = dot_nn(rows, wu_ref[...])
     raw_grad = dot_nt(upstream, wd_ref[...])
     sigmoid = jax.nn.sigmoid(gate_pre)
     silu = gate_pre * sigmoid
     hidden = silu * up_pre
-    gate_grad_ref[...] = jnp.sum(hidden * raw_grad, axis=1, keepdims=True)
+    width = x_ref.shape[1]
+    gate_grad = jnp.sum(hidden * raw_grad, axis=1, keepdims=True)
+    coarse = gate_grad.astype(jnp.bfloat16).astype(jnp.float32)
+    r_ref[:, width:] = (coarse * lanes_ref[2:3] + (gate_grad - coarse) * lanes_ref[3:4]).astype(
+        jnp.bfloat16
+    )
     hidden_gated = (gate * hidden).astype(jnp.bfloat16)
     y_ref[...] = dot_nn(hidden_gated, wd_ref[...]).astype(jnp.bfloat16)
     hidden_grad = gate * raw_grad
@@ -403,15 +980,15 @@
     gate_pre_grad = (
         hidden_grad * up_pre * sigmoid * (1.0 + gate_pre * (1.0 - sigmoid))
     ).astype(jnp.bfloat16)
-    r_ref[...] = (dot_nt(gate_pre_grad, wg_ref[...]) + dot_nt(up_grad, wu_ref[...])).astype(
-        jnp.bfloat16
-    )
+    r_ref[:, :width] = (
+        dot_nt(gate_pre_grad, wg_ref[...]) + dot_nt(up_grad, wu_ref[...])
+    ).astype(jnp.bfloat16)
     wg_grad_ref[...] += dot_tn(rows, gate_pre_grad)
     wu_grad_ref[...] += dot_tn(rows, up_grad)
     wd_grad_ref[...] += dot_tn(hidden_gated, upstream)
 
 
-def expert_pass(rows, upstream, gate, w_gate, w_up, w_down):
+def expert_pass(rows, upstream, hot, router, lanes, w_gate, w_up, w_down):
     count, width = rows.shape
     units = w_gate.shape[1]
     tile = 512 if count % 512 == 0 else GROUP // 2
@@ -426,12 +1003,12 @@
     return pl.pallas_call(
         expert_kernel,
         grid=(count // tile,),
-        in_specs=[by_row(width), by_row(width), by_row(1)] + weights,
-        out_specs=[by_row(width), by_row(width), by_row(1)] + weights,
+        in_specs=[by_row(width), by_row(width), by_row(1), whole(width, LANES), whole(8, LANES)]
+        + weights,
+        out_specs=[by_row(width), by_row(width + LANES)] + weights,
         out_shape=[
             jax.ShapeDtypeStruct((count, width), jnp.bfloat16),
-            jax.ShapeDtypeStruct((count, width), jnp.bfloat16),
-            jax.ShapeDtypeStruct((count, 1), jnp.float32),
+            jax.ShapeDtypeStruct((count, width + LANES), jnp.bfloat16),
             jax.ShapeDtypeStruct((width, units), jnp.float32),
             jax.ShapeDtypeStruct((width, units), jnp.float32),
             jax.ShapeDtypeStruct((units, width), jnp.float32),
@@ -442,10 +1019,7 @@
             transcendentals=count * units,
         ),
         compiler_params=pltpu.CompilerParams(vmem_limit_bytes=60 << 20),
-    )(rows, upstream, gate, w_gate, w_up, w_down)
-
-
-EVERY = ("dp", "tensor")
+    )(rows, upstream, hot, router, lanes, w_gate, w_up, w_down)
 
 
 def dense_body(
@@ -479,10 +1053,19 @@
     inputs = tokens.astype(jnp.float32)
     attn_inv = lax.rsqrt(jnp.mean(inputs * inputs, axis=1, keepdims=True) + EPSILON)
     normed = gather_rows((inputs * attn_inv * attn_gain).astype(jnp.bfloat16))
-    q_all = lax.all_gather(w_query, "dp", axis=0, tiled=True)
-    k_all = lax.all_gather(w_key, "dp", axis=0, tiled=True)
-    v_all = lax.all_gather(w_value, "dp", axis=0, tiled=True)
-    o_all = lax.all_gather(w_out, "dp", axis=1, tiled=True)
+    q_all, k_all, v_all, o_all = gather_in_plane((w_query, w_key, w_value, w_out), 1)
+    q_all, k_all, v_all = (w.reshape(D, head_cols) for w in (q_all, k_all, v_all))
+    o_all = jnp.transpose(o_all.reshape(-1, *w_out.shape), (1, 0, 2)).reshape(head_cols, D)
+    routes_all = lax.all_gather(routes, "dp", axis=0, tiled=True)
+    own_expert = lax.axis_index("dp")
+    hot = jnp.any(routes_all == own_expert, axis=1, keepdims=True).astype(jnp.float32)
+    lane = jnp.arange(LANES)
+    marked = own_expert + experts * rank_index
+    lanes = jnp.stack(
+        [lane == own_expert, lane < experts, lane == marked, lane == marked + 2 * experts]
+        + [lane < 0] * 4
+    ).astype(jnp.float32)
+    router_wide = jnp.pad(router, ((0, 0), (0, LANES - experts)))
     upstream_all = lax.all_gather(cotangent, EVERY, axis=0, tiled=True)
     queries = matmul(normed, q_all)
     keys_raw = matmul(normed, k_all)
@@ -529,19 +1112,20 @@
     expert_ids = jnp.arange(experts, dtype=jnp.int32)
     own_hot = jnp.any(own_routes[:, :, None] == expert_ids[None, None, :], axis=1)
     own_probs = jax.nn.softmax(matmul(normed_two, router), axis=1)
-    rows_all = lax.all_gather(normed_two, EVERY, axis=0, tiled=True)
-    gates_all = lax.all_gather(jnp.where(own_hot, own_probs, 0.0), EVERY, axis=0, tiled=True)
-    own_expert = lax.axis_index("dp")
-    own_gate = lax.dynamic_slice_in_dim(gates_all, own_expert, 1, 1)
-    y_part, r_part, gate_grad, gate_weight_grad, up_weight_grad, down_weight_grad = expert_pass(
-        rows_all, upstream_all, own_gate, w_gate[0], w_up[0], w_down[0]
-    )
-    returned = lax.psum_scatter(r_part, EVERY, scatter_dimension=0, tiled=True)
-    grad_table = jnp.where(expert_ids[None, :] == own_expert, gate_grad, 0.0)
-    expert_grad = lax.psum_scatter(grad_table, EVERY, scatter_dimension=0, tiled=True)
-    expert_grad = jnp.where(own_hot, expert_grad, 0.0)
+    rows_all = gather_everywhere(normed_two, 2).reshape(-1, D)
+    y_part, r_part, gate_weight_grad, up_weight_grad, down_weight_grad = expert_pass(
+        rows_all, upstream_all, hot, router_wide, lanes, w_gate[0], w_up[0], w_down[0]
+    )
+    blocks = (lax.axis_size("dp") // 4, 2, 2, 2, own_rows)
+    returned = scatter_sum(r_part.reshape(*blocks, D + LANES), 3)
+    y_part, returned = lax.optimization_barrier((y_part, returned))
     mixture = lax.psum_scatter(y_part, EVERY, scatter_dimension=0, tiled=True)
     layer_out = (hidden_one + mixture.astype(jnp.float32)).astype(jnp.bfloat16)
+    expert_grad = jnp.sum(
+        returned[:, D : D + 4 * experts].astype(jnp.float32).reshape(own_rows, 4, experts), axis=1
+    )
+    expert_grad = jnp.where(own_hot, expert_grad, 0.0)
+    returned = returned[:, :D]
     upstream = cotangent.astype(jnp.float32)
     logit_grad = own_probs * (expert_grad - jnp.sum(expert_grad * own_probs, axis=1, keepdims=True))
     router_grad = jnp.dot(normed_two.astype(jnp.float32).T, logit_grad, precision=HIGHEST)
@@ -602,17 +1186,19 @@
         + jnp.einsum("gc,rc->gr", key_grad, k_all, preferred_element_type=jnp.float32)
         + jnp.einsum("gc,rc->gr", value_grad, v_all, preferred_element_type=jnp.float32)
     )
-    weight_sums = [
-        lax.psum_scatter(
-            dot_tn(first, second).astype(jnp.bfloat16), "dp", scatter_dimension=0, tiled=True
-        ).astype(jnp.float32)
-        for first, second in (
-            (normed, query_grad),
-            (normed, key_grad),
-            (normed, value_grad),
-            (attended_grad, mixed_heads),
-        )
-    ]
+    shard = (lax.axis_size("dp") // 4, 2, 2, w_query.shape[0], head_cols)
+    weight_sums = scatter_in_plane(
+        [
+            dot_tn(first, second).astype(jnp.bfloat16).reshape(shard)
+            for first, second in (
+                (normed, query_grad),
+                (normed, key_grad),
+                (normed, value_grad),
+                (attended_grad, mixed_heads),
+            )
+        ],
+        4,
+    )
     normed_grad = sum_rows(normed_part)
     scaled_input = normed_grad * attn_gain
     tokens_grad = (

time: 1810 us -> 1170 us (0.65)
  waiting for transfers between devices: 1380 us -> 315 us
  Pallas kernels: 134 us -> 631 us
  blocking collectives: 126 us -> 72.6 us
    reduce_scatter x5 -> x0, waiting for transfers between devices: 542 us -> none  [the longest x4 295 us: dense_body(): lax.psum_scatter(dot_tn(first, second).astype(jnp.bfloat16), 'dp', scatte...]
    pallas_call x0 -> x4, Pallas kernels: none -> 492 us  [the longest x1 174 us: gather_everywhere(): pl.pallas_call(gather_kernel, out_shape=jax.ShapeDtypeStruct((nz, 2, 2, 2...]
    all_gather x5 -> x0, waiting for transfers between devices: 328 us -> none  [the longest x1 157 us: dense_body(): rows_all = lax.all_gather(normed_two, EVERY, axis=0, tiled=True)]
    unnamed x19 -> x7, waiting for transfers between devices: 103 us -> 0.62 us
    all_gather x1, blocking collectives: 73.9 us -> 21.5 us  [dense_body(): routes_all = lax.all_gather(routes, 'dp', axis=0, tiled=True)]
    reduce_scatter x2, waiting for transfers between devices: 58.1 us -> 17.6 us  [sum_rows(): return lax.psum_scatter(values, 'tensor', scatter_dimension=0, tiled=True)]
    all_gather x2, waiting for transfers between devices: 51.2 us -> 26.8 us  [gather_rows(): return lax.all_gather(values, 'tensor', axis=0, tiled=True)]
    all_gather x1, waiting for transfers between devices: 55.3 us -> 33.4 us  [dense_body(): upstream_all = lax.all_gather(cotangent, EVERY, axis=0, tiled=True)]
  transfers between devices with their start and end apart: 18 -> 7, of which waited for: 17 -> 4; matrix products, arithmetic and copies ran while one was open for 4% -> 4% of each run, Pallas kernels for 0% -> 32%
where the time goes in v2:
time: 1170 us; the launch traced here: 1160 us
  Pallas kernels  631 us (54%)
  waiting for transfers between devices  315 us (27%)
  blocking collectives  72.6 us (6%)
  matrix products  60.5 us (5%)
  local copies, waits for them, and re-layouts  35 us (3%)
  other arithmetic  32.7 us (3%)
  between operations  16.8 us (1%)
    reduce_scatter x1, waiting for transfers between devices, dense_body(): mixture = lax.psum_scatter(y_part, EVERY, scatter_dimension=0, tiled=True)  237 us
    pallas_call x1, Pallas kernels, gather_everywhere(): pl.pallas_call(gather_kernel, out_shape=jax.ShapeDtypeStruct((nz, 2, 2, 2...  174 us
    pallas_call x1, Pallas kernels, expert_pass(): pl.pallas_call(expert_kernel, grid=(count // tile,), in_specs=[by_row(wid...  139 us
    pallas_call x1, Pallas kernels, scatter_sum(): pl.pallas_call(scatter_kernel, out_shape=jax.ShapeDtypeStruct((rows, cols...  119 us
    pallas_call x1, Pallas kernels, scatter_in_plane(): pl.pallas_call(functools.partial(plane_scatter_kernel, count), out_shape=...  99.9 us
    pallas_call x1, Pallas kernels, gather_in_plane(): pl.pallas_call(functools.partial(plane_gather_kernel, count), out_shape=[...  98.2 us
    psum x1, blocking collectives, dense_body(): lax.psum((attn_gain_grad, q_gain_full, k_gain_full, mlp_gain_grad, router...  40.3 us
    all_gather x1, waiting for transfers between devices, dense_body(): upstream_all = lax.all_gather(cotangent, EVERY, axis=0, tiled=True)  33.4 us
  transfers between devices with their start and end apart: 7, of which 4 were waited for; matrix products, arithmetic and copies ran while one was open for 4% of the time, Pallas kernels for 32%

profile of v2, /device:TPU:0, one launch (start us, length us, event | category | flops | bytes accessed | tf_op | source)
XLA Modules:
  0.0 1163.7 jit_solution(682505579326958415)
XLA Ops:
  10.6 2.3 fusion.8
  13.0 98.2 %shard_map.254 = (bf16[4,2,2,128,1024]{4,3,2,1,0:T(8,128)(2,1)}, bf16[4,2,2,128,1024]{4,3,2,1,0:T(8,128)(2,1)}, bf16[4,2,2,128,1024]{4,3,2,1,0:T(8,128)(2,1)}, bf16[4,2,2,1024,128]{4,3,2,1,0:T(8,128)(2,1)}) custom-call(bf16[128,1024]{1,0:T(8,128)(2,1)} %refs_0_.1, bf16[128,1024]{1,0:T(8,128)(2,1)} %refs_1_.1, bf16[128,1024]{1,0:T(8,128)(2,1)} %refs_2_.1, ...), custom_call_target="tpu_custom_call" | custom-call | tf_op jit(solution)/shard_map/pallas_call | solution.py:801
  111.2 6.4 copy.107
  120.0 4.7 multiply_reduce_fusion.9
  126.6 5.8 all-reduce.3
  146.1 3.3 copy-done.53
  154.0 3.6 fusion.51
  158.9 21.5 %all_gather.14 = s32[6144,8]{0,1:T(8,128)S(1)} all-gather(s32[384,8]{0,1:T(8,128)S(1)} %copy-done.41), channel_id=1, replica_groups=mesh['dp'=16,'tensor'=2] {'dp'}, dimensions={0}, use_global_device_ids=true | all-gather | bytes 208896 | tf_op jit(solution)/shard_map/all_gather | solution.py:1059
  180.6 2.2 copy.109.hot_ref
  184.0 17.6 %reduce-scatter.4.cloned.1.call-done = f32[192,2048]{1,0:T(8,128)} async-done(((f32[384,2048]{1,0:T(8,128)}), f32[192,2048]{1,0:T(8,128)}) %reduce-scatter.4.cloned.1.call-update) | async-done | bytes 1572880 | tf_op jit(solution)/shard_map/reduce_scatter | solution.py:32
  204.4 174.2 %shard_map.255 = bf16[4,2,2,2,192,2048]{5,4,3,2,1,0:T(8,128)(2,1)} custom-call(bf16[192,2048]{1,0:T(8,128)(2,1)} %multiply_convert_fusion.1.src), custom_call_target="tpu_custom_call" | custom-call | tf_op jit(solution)/shard_map/pallas_call | solution.py:561
  378.6 33.4 %all-gather.6.cloned.1.call-done.g_ref = bf16[6144,2048]{1,0:T(8,128)(2,1)} async-done(((bf16[192,2048]{1,0:T(8,128)(2,1)}), bf16[6144,2048]{1,0:T(8,128)(2,1)}) %all-gather.6.cloned.1.call-update) | async-done | bytes 25165840 | tf_op jit(solution)/shard_map/all_gather | solution.py:1069
  412.0 139.0 %shard_map.256 = (bf16[6144,2048]{1,0:T(8,128)(2,1)}, bf16[6144,2176]{1,0:T(8,128)(2,1)}, f32[2048,512]{1,0:T(8,128)}, f32[2048,512]{1,0:T(8,128)}, f32[512,2048]{1,0:T(8,128)}) custom-call(bf16[6144,2048]{1,0:T(8,128)(2,1)} %bitcast.91, bf16[6144,2048]{1,0:T(8,128)(2,1)} %all-gather.6.cloned.1.call-done.g_ref, f32[6144,1]{1,0:T(8,128)} %copy.109.hot_ref, ...), custom_call_target="tpu_custom_call" | custom-call | flops 115964116992 | bytes 119537664 | tf_op jit(solution)/shard_map/pallas_call | solution.py:1003
  551.0 119.5 %shard_map.257 = bf16[192,2176]{1,0:T(8,128)(2,1)} custom-call(bf16[4,2,2,2,192,2176]{5,4,3,2,1,0:T(8,128)(2,1)} %bitcast.90), custom_call_target="tpu_custom_call" | custom-call | tf_op jit(solution)/shard_map/pallas_call | solution.py:673
  672.9 2.4 multiply_reduce_fusion.1
  675.4 236.5 %reduce-scatter.6.cloned.1.call-done = bf16[192,2048]{1,0:T(8,128)(2,1)} async-done(((bf16[6144,2048]{1,0:T(8,128)(2,1)}), bf16[192,2048]{1,0:T(8,128)(2,1)}) %reduce-scatter.6.cloned.1.call-update) | async-done | bytes 786448 | tf_op jit(solution)/shard_map/reduce_scatter | solution.py:1122
  911.9 3.6 fusion.46
  915.6 26.8 %all-gather.8.cloned.1.call-done = bf16[384,2048]{1,0:T(8,128)(2,1)} async-done(((bf16[192,2048]{1,0:T(8,128)(2,1)}), bf16[384,2048]{1,0:T(8,128)(2,1)}) %all-gather.8.cloned.1.call-update) | async-done | bytes 1572880 | tf_op jit(solution)/shard_map/all_gather | solution.py:28
  942.4 4.5 convolution_convert_fusion.4
  947.3 4.3 fusion.19
  951.5 3.4 multiply_reduce_fusion
  959.3 2.2 maximum_add_fusion.1
  967.6 4.9 all-reduce.2
  974.4 4.3 fusion.54
  981.6 3.6 add_add_fusion
  987.4 5.9 convolution_convert_fusion
  993.3 4.4 convolution_convert_fusion.1
  997.7 4.3 convolution_convert_fusion.2
  1002.0 4.4 convolution_convert_fusion.3
  1006.4 99.9 %shard_map.258 = (f32[128,1024]{1,0:T(8,128)}, f32[128,1024]{1,0:T(8,128)}, f32[128,1024]{1,0:T(8,128)}, f32[128,1024]{1,0:T(8,128)}) custom-call(bf16[4,2,2,128,1024]{4,3,2,1,0:T(8,128)(2,1)} %bitcast.106, bf16[4,2,2,128,1024]{4,3,2,1,0:T(8,128)(2,1)} %bitcast.105, bf16[4,2,2,128,1024]{4,3,2,1,0:T(8,128)(2,1)} %bitcast.104, ...), custom_call_target="tpu_custom_call" | custom-call | tf_op jit(solution)/shard_map/pallas_call | solution.py:904
  1106.3 2.1 copy.119
  1112.6 40.3 %all-reduce.1 = (f32[2048]{0:T(1024)}, f32[2048]{0:T(1024)}, f32[2048]{0:T(1024)}, f32[2048]{0:T(1024)}) all-reduce(f32[2048]{0:T(1024)S(1)} %get-tuple-element.106, f32[2048]{0:T(1024)S(1)} %dynamic_update_slice.6, f32[2048]{0:T(1024)S(1)} %dynamic_update_slice.7, ...), channel_id=1, replica_groups=mesh['dp'=16,'tensor'=2] {'dp','tensor'}, use_global_device_ids=true, to_apply=%region_25.26 | all-reduce | flops 8192 | bytes 65536 | tf_op jit(solution)/shard_map/psum | solution.py:1213
  (218 shorter events, 57.4 us)
Async XLA Ops:
  8.0 4.9 copy-start.51
  8.0 4.9 copy-start.52
  8.0 112.0 %all-gather.4.cloned.1.call-start = ((), (), s32[]{:S(2)}) async-start(), calls=%async_computation.3 | async-start | bytes 2359296 | tf_op jit(solution)/shard_map/all_gather | solution.py:28
  12.9 188.7 %reduce-scatter.4.cloned.1.call-start = ((), (), s32[]{:S(2)}) async-start(), calls=%async_computation.4 | async-start | bytes 4718592 | tf_op jit(solution)/shard_map/reduce_scatter | solution.py:32
  13.0 120.7 %copy-start.35 = (f32[1024]{0:T(1024)}, f32[1024]{0:T(1024)S(1)}, u32[]{:S(2)}) copy-start(f32[1024]{0:T(1024)S(1)} %dynamic_slice.9) | copy-start | bytes 12292
  13.0 125.7 %copy-start.37 = (f32[1024]{0:T(1024)}, f32[1024]{0:T(1024)S(1)}, u32[]{:S(2)}) copy-start(f32[1024]{0:T(1024)S(1)} %dynamic_slice.10) | copy-start | bytes 12292
  120.0 4.7 copy-start.56
  120.0 4.7 copy-start.57
  124.7 9.0 copy-start.3
  126.6 12.1 %copy-start.5 = (f32[384,1024]{1,0:T(8,128)}, f32[384,1024]{1,0:T(8,128)S(1)}, u32[]{:S(2)}) copy-start(f32[384,1024]{1,0:T(8,128)S(1)} %get-tuple-element.150) | copy-start | bytes 4718596
  133.7 5.1 copy-start.44
  145.4 5.9 copy-start
  145.4 5.9 copy-start.31
  146.0 5.2 copy-start.39
  157.6 254.4 %all-gather.6.cloned.1.call-start = ((), (), s32[]{:S(2)}) async-start(), calls=%async_computation.5 | async-start | bytes 25952256 | tf_op jit(solution)/shard_map/all_gather | solution.py:1069
  158.2 753.7 %reduce-scatter.6.cloned.1.call-start = ((), (), s32[]{:S(2)}) async-start(), calls=%async_computation.6 | async-start | bytes 25952256 | tf_op jit(solution)/shard_map/reduce_scatter | solution.py:1122
  182.8 18.8 %copy-start.1 = (bf16[192,2048]{1,0:T(8,128)(2,1)S(1)}, bf16[192,2048]{1,0:T(8,128)(2,1)}, u32[]{:S(2)}) copy-start(bf16[192,2048]{1,0:T(8,128)(2,1)} %param.15) | copy-start | bytes 2359300
  184.0 19.3 %copy-start.34 = (f32[2048]{0:T(1024)S(1)}, f32[2048]{0:T(1024)}, u32[]{:S(2)}) copy-start(f32[2048]{0:T(1024)} %param.25) | copy-start | bytes 24580
  670.5 271.9 %all-gather.8.cloned.1.call-start = ((), (), s32[]{:S(2)}) async-start(), calls=%async_computation.7 | async-start | bytes 2359296 | tf_op jit(solution)/shard_map/all_gather | solution.py:28
  915.6 193.3 %reduce-scatter.8.cloned.1.call-start = ((), (), s32[]{:S(2)}) async-start(), calls=%async_computation.8 | async-start | bytes 4718592 | tf_op jit(solution)/shard_map/reduce_scatter | solution.py:32
  947.3 7.7 slice-start
  965.8 6.8 copy-start.49
  974.4 4.7 copy-start.55
  985.2 167.7 %all-reduce.6.cloned.1.call-start = ((), (), s32[]{:S(2)}) async-start(), calls=%async_computation.9 | async-start | bytes 262144 | tf_op jit(solution)/shard_map/psum | solution.py:1213
  987.4 5.9 copy-start.59
  1006.4 102.5 %copy-start.33 = (f32[2048]{0:T(1024)S(1)}, f32[2048]{0:T(1024)}, u32[]{:S(2)}) copy-start(f32[2048]{0:T(1024)} %param.18) | copy-start | bytes 24580
  1006.4 102.5 %copy-start.47 = (f32[192]{0:T(256)S(1)}, f32[192]{0:T(256)}, u32[]{:S(2)}) copy-start(f32[192]{0:T(256)} %copy-done.46) | copy-start | bytes 2308
  1006.4 104.5 %copy-start.14 = (f32[192,2048]{1,0:T(8,128)S(1)}, f32[192,2048]{1,0:T(8,128)}, u32[]{:S(2)}) copy-start(f32[192,2048]{1,0:T(8,128)} %get-tuple-element.117) | copy-start | bytes 4718596
  1106.3 4.6 copy-start.50
  1110.9 42.0 %copy-start.29 = (f32[128,1024]{1,0:T(8,128)S(1)}, f32[128,1024]{1,0:T(8,128)}, u32[]{:S(2)}) copy-start(f32[128,1024]{1,0:T(8,128)} %get-tuple-element.184) | copy-start | bytes 1572868
  1110.9 42.8 %copy-start.28 = (f32[128,1024]{1,0:T(8,128)S(1)}, f32[128,1024]{1,0:T(8,128)}, u32[]{:S(2)}) copy-start(f32[128,1024]{1,0:T(8,128)} %get-tuple-element.185) | copy-start | bytes 1572868
  1112.6 41.9 %copy-start.27 = (f32[128,1024]{1,0:T(8,128)S(1)}, f32[128,1024]{1,0:T(8,128)}, u32[]{:S(2)}) copy-start(f32[128,1024]{1,0:T(8,128)} %get-tuple-element.186) | copy-start | bytes 1572868
  (39 other events, 84.1 us)
Sparse Core Ops, SparseCore 0:
  13.0 29.8 all-gather.3
  157.7 43.7 reduce-scatter.3
  915.7 26.6 all-gather.7
  985.3 43.3 reduce-scatter.7
Sparse Core Ops, SparseCore 1:
  161.4 250.5 all-gather.5
  670.6 241.2 reduce-scatter.5
  992.7 149.8 all-reduce.5

commit v3 on v2

--- a/solution.py
+++ b/solution.py
@@ -357,6 +357,7 @@
 
 
 MESH_ID = pl.DeviceIdType.MESH
+LINK_TIME = pl.CostEstimate(flops=10**11, bytes_accessed=10**8, transcendentals=0)
 EVERY = ("dp", "tensor")
 LANES = 128
 ANYWHERE = pl.BlockSpec(memory_space=pl.ANY)
@@ -377,13 +378,18 @@
         y = self.y if y is None else y
         return (z * 4 + x * 2 + c, y)
 
-    def meet(self, use_y=True):
+    def meet(self, use_y=True, all_z=False):
         barrier = pltpu.get_barrier_semaphore()
         partners = [self.device(x=1 - self.x), self.device(c=1 - self.c)]
         if use_y:
             partners.append(self.device(y=1 - self.y))
+        if all_z:
+            partners += [self.device(z=(self.z + d) % self.z_count) for d in range(1, self.z_count)]
         for partner in partners:
             pl.semaphore_signal(barrier, inc=1, device_id=partner, device_id_type=MESH_ID)
+        if all_z:
+            pl.semaphore_wait(barrier, len(partners))
+            return
 
         @pl.when(self.z > 0)
         def _():
@@ -424,152 +430,134 @@
     lax.fori_loop(0, rows // step, chunk, 0)
 
 
-def spread_rows(place, src, whole, half, sems):
-    z, x, c, y, nz = place.z, place.x, place.c, place.y, place.z_count
-    sent, got, kept = sems
+class Spread:
     ZU, ZD, XF, YF, XH, YH, CO, CX, CY, CA, CB = range(11)
-    up, down = place.device(z=z + 1), place.device(z=z - 1)
-    over_x, over_y, over_c = place.device(x=1 - x), place.device(y=1 - y), place.device(c=1 - c)
-    full = slice(None)
-    low, high = pl.ds(0, half), pl.ds(half, half)
-
-    def at(zz, xx, yy, rows=full):
-        return whole.at[zz, xx, c, yy, rows]
-
-    def push(kind, zz, xx, yy, rows, device, origin=None):
-        ref = at(zz, xx, yy, rows)
-        send(ref if origin is None else origin, ref, sent.at[kind, zz], got.at[kind, zz], device)
-
-    def arrival(kind, zz, xx, yy, rows=full, cc=None):
-        ref = whole.at[zz, xx, c if cc is None else cc, yy, rows]
-        pltpu.make_async_copy(ref, ref, got.at[kind, zz]).wait()
-
-    def departure(kind, zz, xx, yy, rows=full):
-        ref = at(zz, xx, yy, rows)
-        pltpu.make_async_copy(ref, ref, sent.at[kind, zz]).wait()
-
-    def spread_own(zz, origin=None):
-        push(XF, zz, x, y, full, over_x, origin)
-        push(YF, zz, x, y, full, over_y, origin)
-        push(CO, zz, x, y, full, over_c, origin)
-
-    @pl.when(z < nz - 1)
-    def _():
-        push(ZU, z, x, y, full, up, src)
-
-    @pl.when(z > 0)
-    def _():
-        push(ZD, z, x, y, full, down, src)
-
-    spread_own(z, src)
-    keep = pltpu.make_async_copy(src, at(z, x, y), kept)
-    keep.start()
-
-    def relay(zz):
-        arrival(XF, zz, 1 - x, y)
-        push(YH, zz, 1 - x, y, low, over_y)
-        push(CX, zz, 1 - x, y, full, over_c)
-        arrival(YF, zz, x, 1 - y)
-        push(XH, zz, x, 1 - y, high, over_x)
-        push(CY, zz, x, 1 - y, full, over_c)
-
-    for d in range(nz):
-        below, above = z - d - 1, z + d + 1
-        if d < nz - 1:
-            @pl.when(below >= 0)
+
+    def __init__(self, place, src, whole, sent, got, kept):
+        self.place, self.src, self.whole, self.sent, self.got = place, src, whole, sent, got
+        half = src.shape[0] // 2
+        self.low, self.high = pl.ds(0, half), pl.ds(half, half)
+        z, x, c, y = place.z, place.x, place.c, place.y
+        self.up, self.down = place.device(z=z + 1), place.device(z=z - 1)
+        self.over_x, self.over_y = place.device(x=1 - x), place.device(y=1 - y)
+        self.over_c = place.device(c=1 - c)
+        self.keep = pltpu.make_async_copy(src, whole.at[z, x, c, y], kept)
+
+    def push(self, kind, zz, xx, yy, rows, device, origin=None):
+        ref = self.whole.at[zz, xx, self.place.c, yy, rows]
+        send(
+            ref if origin is None else origin,
+            ref,
+            self.sent.at[kind, zz],
+            self.got.at[kind, zz],
+            device,
+        )
+
+    def arrival(self, kind, zz, xx, yy, rows=slice(None), sibling=False):
+        cc = 1 - self.place.c if sibling else self.place.c
+        ref = self.whole.at[zz, xx, cc, yy, rows]
+        pltpu.make_async_copy(ref, ref, self.got.at[kind, zz]).wait()
+
+    def departure(self, kind, zz, xx, yy, rows=slice(None)):
+        ref = self.whole.at[zz, xx, self.place.c, yy, rows]
+        pltpu.make_async_copy(ref, ref, self.sent.at[kind, zz]).wait()
+
+    def spread_own(self, zz, origin=None):
+        x, y, every = self.place.x, self.place.y, slice(None)
+        self.push(self.XF, zz, x, y, every, self.over_x, origin)
+        self.push(self.YF, zz, x, y, every, self.over_y, origin)
+        self.push(self.CO, zz, x, y, every, self.over_c, origin)
+
+    def begin(self):
+        z, x, y, nz = self.place.z, self.place.x, self.place.y, self.place.z_count
+
+        @pl.when(z < nz - 1)
+        def _():
+            self.push(self.ZU, z, x, y, slice(None), self.up, self.src)
+
+        @pl.when(z > 0)
+        def _():
+            self.push(self.ZD, z, x, y, slice(None), self.down, self.src)
+
+        self.spread_own(z, self.src)
+        self.keep.start()
+
+    def along_z(self, d):
+        z, x, y, nz = self.place.z, self.place.x, self.place.y, self.place.z_count
+        below, above = z - d, z + d
+
+        @pl.when(below >= 0)
+        def _():
+            self.arrival(self.ZU, below, x, y)
+
+            @pl.when(z < nz - 1)
             def _():
-                arrival(ZU, below, x, y)
-
-                @pl.when(z < nz - 1)
-                def _():
-                    push(ZU, below, x, y, full, up)
-
-                spread_own(below)
-
-            @pl.when(above < nz)
+                self.push(self.ZU, below, x, y, slice(None), self.up)
+
+            self.spread_own(below)
+
+        @pl.when(above < nz)
+        def _():
+            self.arrival(self.ZD, above, x, y)
+
+            @pl.when(z > 0)
             def _():
-                arrival(ZD, above, x, y)
-
-                @pl.when(z > 0)
-                def _():
-                    push(ZD, above, x, y, full, down)
-
-                spread_own(above)
-
-        if d == 0:
-            relay(z)
-        else:
-            @pl.when(z - d >= 0)
+                self.push(self.ZD, above, x, y, slice(None), self.down)
+
+            self.spread_own(above)
+
+    def relay(self, zz):
+        x, y, every = self.place.x, self.place.y, slice(None)
+        self.arrival(self.XF, zz, 1 - x, y)
+        self.push(self.YH, zz, 1 - x, y, self.low, self.over_y)
+        self.push(self.CX, zz, 1 - x, y, every, self.over_c)
+        self.arrival(self.YF, zz, x, 1 - y)
+        self.push(self.XH, zz, x, 1 - y, self.high, self.over_x)
+        self.push(self.CY, zz, x, 1 - y, every, self.over_c)
+
+    def diagonal(self, zz):
+        x, y = self.place.x, self.place.y
+        self.arrival(self.XH, zz, 1 - x, 1 - y, self.high)
+        self.push(self.CB, zz, 1 - x, 1 - y, self.high, self.over_c)
+        self.arrival(self.YH, zz, 1 - x, 1 - y, self.low)
+        self.push(self.CA, zz, 1 - x, 1 - y, self.low, self.over_c)
+
+    def sibling_near(self, zz):
+        x, y = self.place.x, self.place.y
+        self.arrival(self.CO, zz, x, y, sibling=True)
+        self.arrival(self.CY, zz, x, 1 - y, sibling=True)
+
+    def sibling_far(self, zz):
+        x, y = self.place.x, self.place.y
+        self.arrival(self.CX, zz, 1 - x, y, sibling=True)
+        self.arrival(self.CA, zz, 1 - x, 1 - y, self.low, sibling=True)
+        self.arrival(self.CB, zz, 1 - x, 1 - y, self.high, sibling=True)
+
+    def finish(self):
+        z, x, y, nz = self.place.z, self.place.x, self.place.y, self.place.z_count
+
+        def one(zz, carry):
+            self.departure(self.XF, zz, x, y)
+            self.departure(self.YF, zz, x, y)
+            self.departure(self.CO, zz, x, y)
+            self.departure(self.CX, zz, 1 - x, y)
+            self.departure(self.CY, zz, x, 1 - y)
+            self.departure(self.YH, zz, 1 - x, y, self.low)
+            self.departure(self.XH, zz, x, 1 - y, self.high)
+            self.departure(self.CA, zz, 1 - x, 1 - y, self.low)
+            self.departure(self.CB, zz, 1 - x, 1 - y, self.high)
+
+            @pl.when((zz <= z) & (z < nz - 1))
             def _():
-                relay(z - d)
-
-            @pl.when(z + d < nz)
+                self.departure(self.ZU, zz, x, y)
+
+            @pl.when((zz >= z) & (z > 0))
             def _():
-                relay(z + d)
-
-    def diagonal(zz):
-        arrival(XH, zz, 1 - x, 1 - y, high)
-        push(CB, zz, 1 - x, 1 - y, high, over_c)
-        arrival(YH, zz, 1 - x, 1 - y, low)
-        push(CA, zz, 1 - x, 1 - y, low, over_c)
-
-    diagonal(z)
-    for d in range(1, nz):
-        @pl.when(z - d >= 0)
-        def _():
-            diagonal(z - d)
-
-        @pl.when(z + d < nz)
-        def _():
-            diagonal(z + d)
-
-    keep.wait()
-    for zz in range(nz):
-        arrival(CO, zz, x, y, cc=1 - c)
-        arrival(CX, zz, 1 - x, y, cc=1 - c)
-        arrival(CY, zz, x, 1 - y, cc=1 - c)
-        arrival(CA, zz, 1 - x, 1 - y, low, cc=1 - c)
-        arrival(CB, zz, 1 - x, 1 - y, high, cc=1 - c)
-        departure(XF, zz, x, y)
-        departure(YF, zz, x, y)
-        departure(CO, zz, x, y)
-        departure(CX, zz, 1 - x, y)
-        departure(CY, zz, x, 1 - y)
-        departure(YH, zz, 1 - x, y, low)
-        departure(XH, zz, x, 1 - y, high)
-        departure(CA, zz, 1 - x, 1 - y, low)
-        departure(CB, zz, 1 - x, 1 - y, high)
-
-        @pl.when((zz <= z) & (z < nz - 1))
-        def _():
-            departure(ZU, zz, x, y)
-
-        @pl.when((zz >= z) & (z > 0))
-        def _():
-            departure(ZD, zz, x, y)
-
-
-def gather_kernel(src, whole, sent, got, kept):
-    place = Place()
-    place.meet()
-    spread_rows(place, src, whole, src.shape[0] // 2, (sent, got, kept))
-
-
-def gather_everywhere(block, collective):
-    rows, cols = block.shape
-    nz = lax.axis_size("dp") // 4
-    return pl.pallas_call(
-        gather_kernel,
-        out_shape=jax.ShapeDtypeStruct((nz, 2, 2, 2, rows, cols), block.dtype),
-        in_specs=[ANYWHERE],
-        out_specs=ANYWHERE,
-        scratch_shapes=[
-            pltpu.SemaphoreType.DMA((11, nz)),
-            pltpu.SemaphoreType.DMA((11, nz)),
-            pltpu.SemaphoreType.DMA,
-        ],
-        compiler_params=pltpu.CompilerParams(collective_id=collective, has_side_effects=True),
-    )(block)
+                self.departure(self.ZD, zz, x, y)
+
+            return carry
+
+        lax.fori_loop(0, nz, one, 0)
 
 
 def scatter_kernel(parts, out, total, from_c, half_x, half_y, full_x, full_y, up_buf, down_buf, sent, got, loaded):
@@ -688,10 +676,45 @@
             pltpu.SemaphoreType.DMA((10, nz)),
             pltpu.SemaphoreType.DMA((4, nz)),
         ],
+        cost_estimate=LINK_TIME,
         compiler_params=pltpu.CompilerParams(
             collective_id=collective, has_side_effects=True, vmem_limit_bytes=58 << 20
         ),
     )(parts)
+
+
+def swap_kernel(src, out, sent, got):
+    dp, y = lax.axis_index("dp"), lax.axis_index("tensor")
+    other = (dp, 1 - y)
+    barrier = pltpu.get_barrier_semaphore()
+    pl.semaphore_signal(barrier, inc=1, device_id=other, device_id_type=MESH_ID)
+    pl.semaphore_wait(barrier, 1)
+    send(src, out, sent, got, other).wait()
+
+
+def swap_tensor(block, collective):
+    return pl.pallas_call(
+        swap_kernel,
+        out_shape=jax.ShapeDtypeStruct(block.shape, block.dtype),
+        in_specs=[ANYWHERE],
+        out_specs=ANYWHERE,
+        scratch_shapes=[pltpu.SemaphoreType.DMA, pltpu.SemaphoreType.DMA],
+        compiler_params=pltpu.CompilerParams(collective_id=collective, has_side_effects=True),
+    )(block)
+
+
+def both_rows(block, collective):
+    other = swap_tensor(block, collective)
+    first = lax.axis_index("tensor") == 0
+    return jnp.concatenate([jnp.where(first, block, other), jnp.where(first, other, block)], axis=0)
+
+
+def own_rows_sum(part, collective):
+    rows = part.shape[0] // 2
+    index = lax.axis_index("tensor")
+    other = lax.dynamic_slice_in_dim(part, (1 - index) * rows, rows, 0).astype(jnp.bfloat16)
+    mine = lax.dynamic_slice_in_dim(part, index * rows, rows, 0)
+    return mine + swap_tensor(other, collective).astype(jnp.float32)
 
 
 def plane_gather_kernel(count, *refs):
@@ -808,19 +831,33 @@
             pltpu.SemaphoreType.DMA((5, count, nz)),
             pltpu.SemaphoreType.DMA((count,)),
         ],
+        cost_estimate=LINK_TIME,
         compiler_params=pltpu.CompilerParams(collective_id=collective, has_side_effects=True),
     )(*shards)
 
 
 def plane_scatter_kernel(count, *refs):
-    parts, outs = refs[:count], refs[count : 2 * count]
-    total, from_c, full_x, up_buf, down_buf, sent, got, loaded = refs[2 * count :]
+    parts, small = refs[:count], refs[count]
+    outs, small_out = refs[count + 1 : 2 * count + 1], refs[2 * count + 1]
+    (
+        total,
+        from_c,
+        full_x,
+        up_buf,
+        down_buf,
+        small_sum,
+        small_got,
+        sent,
+        got,
+        loaded,
+        small_sems,
+    ) = refs[2 * count + 2 :]
     place = Place()
     z, x, c, nz = place.z, place.x, place.c, place.z_count
     rows = total.shape[3]
     C0, C1, XF, ZU, ZD = range(5)
     over_x, over_c = place.device(x=1 - x), place.device(c=1 - c)
-    place.meet(use_y=False)
+    place.meet(all_z=True)
 
     def arrival(a, kind, zz, ref):
         pltpu.make_async_copy(ref, ref, got.at[kind, a, zz]).wait()
@@ -839,8 +876,36 @@
         arrival(a, C1 if dx else C0, zz, there)
         add_rows(here, there, rows)
 
+    small_sum[0] = small[...]
+
+    def small_step(i):
+        if i < 3:
+            partner = (over_c, place.device(y=1 - place.y), over_x)[i]
+            copy = send(small_sum.at[i], small_got.at[i], small_sems.at[0, i], small_sems.at[1, i], partner)
+            copy.wait()
+            small_sum[i + 1] = small_sum[i] + small_got[i]
+            return
+        copies = [
+            send(
+                small_sum.at[3],
+                small_got.at[2 + d],
+                small_sems.at[0, 2 + d],
+                small_sems.at[1, 2 + d],
+                place.device(z=(z + d) % nz),
+            )
+            for d in range(1, nz)
+        ]
+        for copy in copies:
+            copy.wait()
+        result = jnp.zeros_like(small_out)
+        for zz in range(nz):
+            away = (z - zz) % nz
+            result = result + jnp.where(away == 0, small_sum[3], small_got[jnp.maximum(2 + away, 3)])
+        small_out[...] = result
+
     for i in range(nz):
         zz = place.far_first(i)
+        small_step(min(i, 3))
         for a in range(count):
             join_cores(a, 1, zz)
             send(total.at[1, zz, a], full_x.at[zz, a], sent.at[XF, a, zz], got.at[XF, a, zz], over_x)
@@ -897,29 +962,34 @@
                 departure(a, ZD, zz, total.at[0, 0, a])
 
 
-def scatter_in_plane(parts, collective):
+def scatter_in_plane(parts, small, collective):
     nz, _, _, rows, cols = parts[0].shape
     count = len(parts)
     dt = parts[0].dtype
     return pl.pallas_call(
         functools.partial(plane_scatter_kernel, count),
-        out_shape=[jax.ShapeDtypeStruct((rows, cols), jnp.float32)] * count,
-        in_specs=[ANYWHERE] * count,
-        out_specs=[IN_VMEM] * count,
+        out_shape=[jax.ShapeDtypeStruct((rows, cols), jnp.float32)] * count
+        + [jax.ShapeDtypeStruct(small.shape, small.dtype)],
+        in_specs=[ANYWHERE] * count + [IN_VMEM],
+        out_specs=[IN_VMEM] * (count + 1),
         scratch_shapes=[
             pltpu.VMEM((2, nz, count, rows, cols), dt),
             pltpu.VMEM((2, nz, count, rows, cols), dt),
             pltpu.VMEM((nz, count, rows, cols), dt),
             pltpu.VMEM((nz, count, rows, cols), dt),
             pltpu.VMEM((nz, count, rows, cols), dt),
+            pltpu.VMEM((4,) + small.shape, small.dtype),
+            pltpu.VMEM((2 + nz,) + small.shape, small.dtype),
             pltpu.SemaphoreType.DMA((5, count, nz)),
             pltpu.SemaphoreType.DMA((5, count, nz)),
             pltpu.SemaphoreType.DMA((2, count, nz)),
+            pltpu.SemaphoreType.DMA((2, 2 + nz)),
         ],
+        cost_estimate=LINK_TIME,
         compiler_params=pltpu.CompilerParams(
             collective_id=collective, has_side_effects=True, vmem_limit_bytes=58 << 20
         ),
-    )(*parts)
+    )(*parts, small)
 
 
 def dot_nn(a, b):
@@ -934,20 +1004,225 @@
     return lax.dot_general(a, b, (((0,), (0,)), ((), ())), preferred_element_type=jnp.float32)
 
 
+def pick(table, index):
+    return sum(jnp.where(index == i, value, 0) for i, value in enumerate(table))
+
+
 def expert_kernel(
-    x_ref,
-    g_ref,
+    z_count,
+    src,
+    g_all,
     hot_ref,
     router_ref,
     lanes_ref,
     wg_ref,
     wu_ref,
     wd_ref,
-    y_ref,
-    r_ref,
-    wg_grad_ref,
-    wu_grad_ref,
-    wd_grad_ref,
+    x_all,
+    y_all,
+    r_all,
+    hidden_all,
+    gate_pre_grad_all,
+    up_grad_all,
+    x_tile,
+    g_tile,
+    y_tile,
+    r_tile,
+    hidden_tile,
+    gate_pre_grad_tile,
+    up_grad_tile,
+    load_sems,
+    store_sems,
+    sent,
+    got,
+    kept,
+):
+    place = Place()
+    place.meet()
+    spread = Spread(place, src, x_all, sent, got, kept)
+    spread.begin()
+    width = src.shape[1]
+    tile = x_tile.shape[1]
+    pairs = sorted(
+        ((k, dx) for k in range(z_count) for dx in (0, 1)), key=lambda p: p[0] + 1.3 * p[1]
+    )
+    tiles = 2 * len(pairs)
+    near_table, across_table = [p[0] for p in pairs], [p[1] for p in pairs]
+
+    def near(k):
+        return place.far_first(z_count - 1 - k)
+
+    def tile_at(i):
+        pair, second = i // 2, i % 2
+        zz = near(pick(near_table, pair))
+        xx = jnp.where(pick(across_table, pair) == 1, 1 - place.x, place.x)
+        cc = jnp.where(second == 1, 1 - place.c, place.c)
+        return zz, xx, cc
+
+    stores = (
+        (y_tile, y_all),
+        (r_tile, r_all),
+        (hidden_tile, hidden_all),
+        (gate_pre_grad_tile, gate_pre_grad_all),
+        (up_grad_tile, up_grad_all),
+    )
+
+    def loads(i, slot):
+        zz, xx, cc = tile_at(i)
+        copies = []
+        for yy in range(2):
+            rows = pl.ds(yy * (tile // 2), tile // 2)
+            copies.append(
+                pltpu.make_async_copy(
+                    x_all.at[zz, xx, cc, yy], x_tile.at[slot, rows], load_sems.at[slot, yy]
+                )
+            )
+        copies.append(
+            pltpu.make_async_copy(g_all.at[zz, xx, cc], g_tile.at[slot], load_sems.at[slot, 2])
+        )
+        return copies
+
+    def store(i, slot):
+        zz, xx, cc = tile_at(i)
+        return [
+            pltpu.make_async_copy(here.at[slot], there.at[zz, xx, cc], store_sems.at[slot, n])
+            for n, (here, there) in enumerate(stores)
+        ]
+
+    z_done, steps = 0, {}
+    for position, (k, dx) in enumerate(pairs):
+        todo = []
+        if dx == 0:
+            todo.append(("relay", k))
+            while z_done < min(k + 1, z_count - 1):
+                z_done += 1
+                todo.insert(0, ("z", z_done))
+        else:
+            todo.append(("diagonal", k))
+        steps[2 * position] = todo
+
+    def prepare(i):
+        for position in range(tiles):
+            pair = position // 2
+            k, dx = pairs[pair]
+
+            @pl.when(i == position)
+            def _():
+                if position % 2 == 0:
+                    for kind, number in steps[position]:
+                        if kind == "z":
+                            spread.along_z(number)
+                        elif kind == "relay":
+                            spread.relay(near(number))
+                        else:
+                            spread.diagonal(near(number))
+                    if position == 0:
+                        spread.keep.wait()
+                elif dx == 0:
+                    spread.sibling_near(near(k))
+                else:
+                    spread.sibling_far(near(k))
+
+        for copy in loads(i, i % 2):
+            copy.start()
+
+    def compute(i, carry):
+        slot = i % 2
+        for copy in loads(i, slot):
+            copy.wait()
+
+        @pl.when(i >= 2)
+        def _():
+            for copy in store(i - 2, slot):
+                copy.wait()
+
+        zz, xx, cc = tile_at(i)
+        first_row = pl.multiple_of(((zz * 2 + xx) * 2 + cc) * tile, tile)
+        rows = x_tile[slot]
+        logits = jnp.where(lanes_ref[1:2] > 0.0, dot_nn(rows, router_ref[...]), -1e30)
+        weights = jnp.exp(logits - jnp.max(logits, axis=1, keepdims=True))
+        own_weight = jnp.sum(weights * lanes_ref[0:1], axis=1, keepdims=True)
+        gate = hot_ref[pl.ds(first_row, tile)] * own_weight / jnp.sum(weights, axis=1, keepdims=True)
+        gate_pre = dot_nn(rows, wg_ref[...])
+        up_pre = dot_nn(rows, wu_ref[...])
+        raw_grad = dot_nt(g_tile[slot], wd_ref[...])
+
+        @pl.when(i < tiles - 1)
+        def _():
+            prepare(i + 1)
+
+        sigmoid = jax.nn.sigmoid(gate_pre)
+        silu = gate_pre * sigmoid
+        hidden = silu * up_pre
+        gate_grad = jnp.sum(hidden * raw_grad, axis=1, keepdims=True)
+        coarse = gate_grad.astype(jnp.bfloat16).astype(jnp.float32)
+        r_tile[slot, :, width:] = (
+            coarse * lanes_ref[2:3] + (gate_grad - coarse) * lanes_ref[3:4]
+        ).astype(jnp.bfloat16)
+        hidden_gated = (gate * hidden).astype(jnp.bfloat16)
+        hidden_tile[slot] = hidden_gated
+        hidden_grad = gate * raw_grad
+        up_grad = (hidden_grad * silu).astype(jnp.bfloat16)
+        up_grad_tile[slot] = up_grad
+        gate_pre_grad = (
+            hidden_grad * up_pre * sigmoid * (1.0 + gate_pre * (1.0 - sigmoid))
+        ).astype(jnp.bfloat16)
+        gate_pre_grad_tile[slot] = gate_pre_grad
+        y_tile[slot] = dot_nn(hidden_gated, wd_ref[...]).astype(jnp.bfloat16)
+        r_tile[slot, :, :width] = (
+            dot_nt(gate_pre_grad, wg_ref[...]) + dot_nt(up_grad, wu_ref[...])
+        ).astype(jnp.bfloat16)
+        for copy in store(i, slot):
+            copy.start()
+        return carry
+
+    prepare(0)
+    lax.fori_loop(0, tiles, compute, 0)
+    for i in (tiles - 2, tiles - 1):
+        for copy in store(i, i % 2):
+            copy.wait()
+    spread.finish()
+
+
+def expert_pass(block, upstream, hot, router, lanes, w_gate, w_up, w_down, collective):
+    rows, width = block.shape
+    units = w_gate.shape[1]
+    nz = lax.axis_size("dp") // 4
+    tile = 2 * rows
+    out = (nz, 2, 2, tile)
+    return pl.pallas_call(
+        functools.partial(expert_kernel, nz),
+        in_specs=[ANYWHERE] * 2 + [IN_VMEM] * 6,
+        out_specs=[ANYWHERE] * 6,
+        out_shape=[
+            jax.ShapeDtypeStruct((nz, 2, 2, 2, rows, width), jnp.bfloat16),
+            jax.ShapeDtypeStruct(out + (width,), jnp.bfloat16),
+            jax.ShapeDtypeStruct(out + (width + LANES,), jnp.bfloat16),
+        ]
+        + [jax.ShapeDtypeStruct(out + (units,), jnp.bfloat16)] * 3,
+        scratch_shapes=[
+            pltpu.VMEM((2, tile, width), jnp.bfloat16),
+            pltpu.VMEM((2, tile, width), jnp.bfloat16),
+            pltpu.VMEM((2, tile, width), jnp.bfloat16),
+            pltpu.VMEM((2, tile, width + LANES), jnp.bfloat16),
+            pltpu.VMEM((2, tile, units), jnp.bfloat16),
+            pltpu.VMEM((2, tile, units), jnp.bfloat16),
+            pltpu.VMEM((2, tile, units), jnp.bfloat16),
+            pltpu.SemaphoreType.DMA((2, 3)),
+            pltpu.SemaphoreType.DMA((2, 5)),
+            pltpu.SemaphoreType.DMA((11, nz)),
+            pltpu.SemaphoreType.DMA((11, nz)),
+            pltpu.SemaphoreType.DMA,
+        ],
+        cost_estimate=LINK_TIME,
+        compiler_params=pltpu.CompilerParams(
+            collective_id=collective, has_side_effects=True, vmem_limit_bytes=60 << 20
+        ),
+    )(block, upstream.reshape(out + (width,)), hot, router, lanes, w_gate, w_up, w_down)
+
+
+def expert_weights_kernel(
+    x_ref, g_ref, hidden_ref, gate_pre_grad_ref, up_grad_ref, wg_grad_ref, wu_grad_ref, wd_grad_ref
 ):
     @pl.when(pl.program_id(0) == 0)
     def _():
@@ -956,41 +1231,14 @@
         wd_grad_ref[...] = jnp.zeros_like(wd_grad_ref)
 
     rows = x_ref[...]
-    upstream = g_ref[...]
-    logits = jnp.where(lanes_ref[1:2] > 0.0, dot_nn(rows, router_ref[...]), -1e30)
-    weights = jnp.exp(logits - jnp.max(logits, axis=1, keepdims=True))
-    own_weight = jnp.sum(weights * lanes_ref[0:1], axis=1, keepdims=True)
-    gate = hot_ref[...] * own_weight / jnp.sum(weights, axis=1, keepdims=True)
-    gate_pre = dot_nn(rows, wg_ref[...])
-    up_pre = dot_nn(rows, wu_ref[...])
-    raw_grad = dot_nt(upstream, wd_ref[...])
-    sigmoid = jax.nn.sigmoid(gate_pre)
-    silu = gate_pre * sigmoid
-    hidden = silu * up_pre
-    width = x_ref.shape[1]
-    gate_grad = jnp.sum(hidden * raw_grad, axis=1, keepdims=True)
-    coarse = gate_grad.astype(jnp.bfloat16).astype(jnp.float32)
-    r_ref[:, width:] = (coarse * lanes_ref[2:3] + (gate_grad - coarse) * lanes_ref[3:4]).astype(
-        jnp.bfloat16
-    )
-    hidden_gated = (gate * hidden).astype(jnp.bfloat16)
-    y_ref[...] = dot_nn(hidden_gated, wd_ref[...]).astype(jnp.bfloat16)
-    hidden_grad = gate * raw_grad
-    up_grad = (hidden_grad * silu).astype(jnp.bfloat16)
-    gate_pre_grad = (
-        hidden_grad * up_pre * sigmoid * (1.0 + gate_pre * (1.0 - sigmoid))
-    ).astype(jnp.bfloat16)
-    r_ref[:, :width] = (
-        dot_nt(gate_pre_grad, wg_ref[...]) + dot_nt(up_grad, wu_ref[...])
-    ).astype(jnp.bfloat16)
-    wg_grad_ref[...] += dot_tn(rows, gate_pre_grad)
-    wu_grad_ref[...] += dot_tn(rows, up_grad)
-    wd_grad_ref[...] += dot_tn(hidden_gated, upstream)
-
-
-def expert_pass(rows, upstream, hot, router, lanes, w_gate, w_up, w_down):
+    wg_grad_ref[...] += dot_tn(rows, gate_pre_grad_ref[...])
+    wu_grad_ref[...] += dot_tn(rows, up_grad_ref[...])
+    wd_grad_ref[...] += dot_tn(hidden_ref[...], g_ref[...])
+
+
+def expert_weights_pass(rows, upstream, hidden, gate_pre_grad, up_grad):
     count, width = rows.shape
-    units = w_gate.shape[1]
+    units = hidden.shape[1]
     tile = 512 if count % 512 == 0 else GROUP // 2
 
     def by_row(cols):
@@ -999,27 +1247,20 @@
     def whole(first, second):
         return pl.BlockSpec((first, second), lambda i: (0, 0), pipeline_mode=pl.Buffered(1))
 
-    weights = [whole(width, units), whole(width, units), whole(units, width)]
+    shapes = [(width, units), (width, units), (units, width)]
     return pl.pallas_call(
-        expert_kernel,
+        expert_weights_kernel,
         grid=(count // tile,),
-        in_specs=[by_row(width), by_row(width), by_row(1), whole(width, LANES), whole(8, LANES)]
-        + weights,
-        out_specs=[by_row(width), by_row(width + LANES)] + weights,
-        out_shape=[
-            jax.ShapeDtypeStruct((count, width), jnp.bfloat16),
-            jax.ShapeDtypeStruct((count, width + LANES), jnp.bfloat16),
-            jax.ShapeDtypeStruct((width, units), jnp.float32),
-            jax.ShapeDtypeStruct((width, units), jnp.float32),
-            jax.ShapeDtypeStruct((units, width), jnp.float32),
-        ],
+        in_specs=[by_row(width)] * 2 + [by_row(units)] * 3,
+        out_specs=[whole(*shape) for shape in shapes],
+        out_shape=[jax.ShapeDtypeStruct(shape, jnp.float32) for shape in shapes],
         cost_estimate=pl.CostEstimate(
-            flops=18 * count * width * units,
-            bytes_accessed=8 * count * width + 18 * width * units,
-            transcendentals=count * units,
+            flops=6 * count * width * units,
+            bytes_accessed=4 * count * width + 12 * width * units,
+            transcendentals=0,
         ),
         compiler_params=pltpu.CompilerParams(vmem_limit_bytes=60 << 20),
-    )(rows, upstream, hot, router, lanes, w_gate, w_up, w_down)
+    )(rows, upstream, hidden, gate_pre_grad, up_grad)
 
 
 def dense_body(
@@ -1052,11 +1293,13 @@
     k_gain_local = lax.dynamic_slice_in_dim(k_gain, col_start, head_cols)
     inputs = tokens.astype(jnp.float32)
     attn_inv = lax.rsqrt(jnp.mean(inputs * inputs, axis=1, keepdims=True) + EPSILON)
-    normed = gather_rows((inputs * attn_inv * attn_gain).astype(jnp.bfloat16))
-    q_all, k_all, v_all, o_all = gather_in_plane((w_query, w_key, w_value, w_out), 1)
+    normed = both_rows((inputs * attn_inv * attn_gain).astype(jnp.bfloat16), 5)
+    q_all, k_all, v_all, o_all, routes_all = gather_in_plane(
+        (w_query, w_key, w_value, w_out, routes), 1
+    )
     q_all, k_all, v_all = (w.reshape(D, head_cols) for w in (q_all, k_all, v_all))
     o_all = jnp.transpose(o_all.reshape(-1, *w_out.shape), (1, 0, 2)).reshape(head_cols, D)
-    routes_all = lax.all_gather(routes, "dp", axis=0, tiled=True)
+    routes_all = routes_all.reshape(-1, TOPK)
     own_expert = lax.axis_index("dp")
     hot = jnp.any(routes_all == own_expert, axis=1, keepdims=True).astype(jnp.float32)
     lane = jnp.arange(LANES)
@@ -1104,7 +1347,7 @@
         preferred_element_type=jnp.float32,
     )
     mixed_heads = mixed_heads.reshape(GROUP, head_cols).astype(jnp.bfloat16)
-    attended = sum_rows(matmul(mixed_heads, o_all))
+    attended = own_rows_sum(matmul(mixed_heads, o_all), 6)
     hidden_one = inputs + attended
     mlp_inv = lax.rsqrt(jnp.mean(hidden_one * hidden_one, axis=1, keepdims=True) + EPSILON)
     normed_two = (hidden_one * mlp_inv * mlp_gain).astype(jnp.bfloat16)
@@ -1112,15 +1355,18 @@
     expert_ids = jnp.arange(experts, dtype=jnp.int32)
     own_hot = jnp.any(own_routes[:, :, None] == expert_ids[None, None, :], axis=1)
     own_probs = jax.nn.softmax(matmul(normed_two, router), axis=1)
-    rows_all = gather_everywhere(normed_two, 2).reshape(-1, D)
-    y_part, r_part, gate_weight_grad, up_weight_grad, down_weight_grad = expert_pass(
-        rows_all, upstream_all, hot, router_wide, lanes, w_gate[0], w_up[0], w_down[0]
-    )
+    rows_all, y_part, r_part, *for_weights = expert_pass(
+        normed_two, upstream_all, hot, router_wide, lanes, w_gate[0], w_up[0], w_down[0], 2
+    )
+    rows_all, y_part = rows_all.reshape(-1, D), y_part.reshape(-1, D)
+    for_weights = [array.reshape(rows_all.shape[0], -1) for array in for_weights]
     blocks = (lax.axis_size("dp") // 4, 2, 2, 2, own_rows)
     returned = scatter_sum(r_part.reshape(*blocks, D + LANES), 3)
-    y_part, returned = lax.optimization_barrier((y_part, returned))
+    y_part, returned, for_weights = lax.optimization_barrier((y_part, returned, for_weights))
+    gate_weight_grad, up_weight_grad, down_weight_grad = expert_weights_pass(
+        rows_all, upstream_all, *for_weights
+    )
     mixture = lax.psum_scatter(y_part, EVERY, scatter_dimension=0, tiled=True)
-    layer_out = (hidden_one + mixture.astype(jnp.float32)).astype(jnp.bfloat16)
     expert_grad = jnp.sum(
         returned[:, D : D + 4 * experts].astype(jnp.float32).reshape(own_rows, 4, experts), axis=1
     )
@@ -1139,7 +1385,7 @@
         - hidden_one * mlp_inv**3 * jnp.mean(hidden_one * scaled_grad, axis=1, keepdims=True)
     )
     mlp_gain_grad = jnp.sum(normed_two_grad * hidden_one * mlp_inv, axis=0)
-    attended_grad = gather_rows(hidden_one_grad.astype(jnp.bfloat16))
+    attended_grad = both_rows(hidden_one_grad.astype(jnp.bfloat16), 7)
     mixed_grad = jnp.einsum("gd,cd->gc", attended_grad, o_all, preferred_element_type=jnp.float32)
     mixed_grad = mixed_grad.astype(jnp.bfloat16).reshape(head_shape)
     attn_probs = jnp.exp(masked_scores() - log_total)
@@ -1186,20 +1432,7 @@
         + jnp.einsum("gc,rc->gr", key_grad, k_all, preferred_element_type=jnp.float32)
         + jnp.einsum("gc,rc->gr", value_grad, v_all, preferred_element_type=jnp.float32)
     )
-    shard = (lax.axis_size("dp") // 4, 2, 2, w_query.shape[0], head_cols)
-    weight_sums = scatter_in_plane(
-        [
-            dot_tn(first, second).astype(jnp.bfloat16).reshape(shard)
-            for first, second in (
-                (normed, query_grad),
-                (normed, key_grad),
-                (normed, value_grad),
-                (attended_grad, mixed_heads),
-            )
-        ],
-        4,
-    )
-    normed_grad = sum_rows(normed_part)
+    normed_grad = own_rows_sum(normed_part, 8)
     scaled_input = normed_grad * attn_gain
     tokens_grad = (
         hidden_one_grad
@@ -1210,9 +1443,30 @@
     zero_width = jnp.zeros((D,), jnp.float32)
     q_gain_full = lax.dynamic_update_slice_in_dim(zero_width, q_gain_part, col_start, 0)
     k_gain_full = lax.dynamic_update_slice_in_dim(zero_width, k_gain_part, col_start, 0)
-    attn_gain_grad, q_gain_grad, k_gain_grad, mlp_gain_grad, router_grad = lax.psum(
-        (attn_gain_grad, q_gain_full, k_gain_full, mlp_gain_grad, router_grad), EVERY
-    )
+    small_grads = jnp.concatenate(
+        [
+            jnp.stack([attn_gain_grad, q_gain_full, k_gain_full, mlp_gain_grad]),
+            jnp.zeros((4, D), jnp.float32),
+            jnp.transpose(router_grad),
+        ],
+        axis=0,
+    )
+    shard = (lax.axis_size("dp") // 4, 2, 2, w_query.shape[0], head_cols)
+    products = [
+        dot_tn(first, second).astype(jnp.bfloat16).reshape(shard)
+        for first, second in (
+            (normed, query_grad),
+            (normed, key_grad),
+            (normed, value_grad),
+            (attended_grad, mixed_heads),
+        )
+    ]
+    products, gate_weight_grad = lax.optimization_barrier((products, gate_weight_grad))
+    *weight_sums, small_sums = scatter_in_plane(products, small_grads, 4)
+    attn_gain_grad, q_gain_grad, k_gain_grad, mlp_gain_grad = (small_sums[i] for i in range(4))
+    router_grad = jnp.transpose(small_sums[8:])
+    mixture, weight_sums = lax.optimization_barrier((mixture, weight_sums))
+    layer_out = (hidden_one + mixture.astype(jnp.float32)).astype(jnp.bfloat16)
     return (
         layer_out,
         tokens_grad,

time: 1170 us -> 950 us (0.81)
  waiting for transfers between devices: 315 us -> 0.7 us
  Pallas kernels: 631 us -> 771 us
  blocking collectives: 72.6 us -> 10.1 us
  local copies, waits for them, and re-layouts: 35 us -> 52.4 us
    reduce_scatter x1, waiting for transfers between devices: 237 us -> 0.01 us  [dense_body(): mixture = lax.psum_scatter(y_part, EVERY, scatter_dimension=0, tiled=True)]
    pallas_call x1, Pallas kernels: 98.2 us -> 181 us  [gather_in_plane(): pl.pallas_call(functools.partial(plane_gather_kernel, count), out_shape=[...]
    pallas_call x1, Pallas kernels: 99.9 us -> 170 us  [scatter_in_plane(): pl.pallas_call(functools.partial(plane_scatter_kernel, count), out_shape=...]
    psum x1 -> x0, blocking collectives: 40.3 us -> none  [dense_body(): lax.psum((attn_gain_grad, q_gain_full, k_gain_full, mlp_gain_grad, router...]
    all_gather x1, waiting for transfers between devices: 33.4 us -> 0.01 us  [dense_body(): upstream_all = lax.all_gather(cotangent, EVERY, axis=0, tiled=True)]
    pallas_call x2 -> x6, Pallas kernels: 313 us -> 282 us  [the longest x1 150 us: expert_pass(): pl.pallas_call(functools.partial(expert_kernel, nz), in_specs=[ANYWHERE]...]
    all_gather x2 -> x0, waiting for transfers between devices: 26.8 us -> none  [gather_rows(): return lax.all_gather(values, 'tensor', axis=0, tiled=True)]
    all_gather x1 -> x0, blocking collectives: 21.5 us -> none  [dense_body(): routes_all = lax.all_gather(routes, 'dp', axis=0, tiled=True)]
  transfers between devices with their start and end apart: 7 -> 2, of which waited for: 4 -> 0; matrix products, arithmetic and copies ran while one was open for 4% -> 13% of each run, Pallas kernels for 32% -> 51%
where the time goes in v3:
time: 950 us; the launch traced here: 940 us
  Pallas kernels  771 us (81%)
  local copies, waits for them, and re-layouts  52.4 us (6%)
  matrix products  50.5 us (5%)
  other arithmetic  40.4 us (4%)
  between operations  15.6 us (2%)
  blocking collectives  10.1 us (1%)
    pallas_call x1, Pallas kernels, gather_in_plane(): pl.pallas_call(functools.partial(plane_gather_kernel, count), out_shape=[...  181 us
    pallas_call x1, Pallas kernels, scatter_in_plane(): pl.pallas_call(functools.partial(plane_scatter_kernel, count), out_shape=...  170 us
    pallas_call x1, Pallas kernels, expert_pass(): pl.pallas_call(functools.partial(expert_kernel, nz), in_specs=[ANYWHERE]...  150 us
    pallas_call x1, Pallas kernels, scatter_sum(): pl.pallas_call(scatter_kernel, out_shape=jax.ShapeDtypeStruct((rows, cols...  138 us
    pallas_call x4, Pallas kernels, swap_tensor(): pl.pallas_call(swap_kernel, out_shape=jax.ShapeDtypeStruct(block.shape, b...  83.6 us
    pallas_call x1, Pallas kernels, expert_weights_pass(): pl.pallas_call(expert_weights_kernel, grid=(count // tile,), in_specs=[by...  48.2 us
    unnamed x186, local copies, waits for them, and re-layouts  23.1 us
  transfers between devices with their start and end apart: 2, of which 0 were waited for; matrix products, arithmetic and copies ran while one was open for 13% of the time, Pallas kernels for 51%

profile of v3, /device:TPU:0, one launch (start us, length us, event | category | flops | bytes accessed | tf_op | source)
XLA Modules:
  0.0 940.4 jit_solution(8946741336801740681)
XLA Ops:
  11.1 26.5 %shard_map.254 = bf16[192,2048]{1,0:T(8,128)(2,1)} custom-call(bf16[192,2048]{1,0:T(8,128)(2,1)} %fusion.8.src), custom_call_target="tpu_custom_call" | custom-call | tf_op jit(solution)/shard_map/pallas_call | solution.py:696
  38.4 2.6 broadcast_select_fusion.3
  40.9 180.8 %shard_map.255 = (bf16[4,2,2,128,1024]{4,3,2,1,0:T(8,128)(2,1)}, bf16[4,2,2,128,1024]{4,3,2,1,0:T(8,128)(2,1)}, bf16[4,2,2,128,1024]{4,3,2,1,0:T(8,128)(2,1)}, b...) custom-call(bf16[128,1024]{1,0:T(8,128)(2,1)} %refs_0_.1, bf16[128,1024]{1,0:T(8,128)(2,1)} %refs_1_.1, ...), custom_call_target="tpu_custom_call" | custom-call | flops 99999997952 | bytes 100000000 | tf_op jit(solution)/shard_map/pallas_call | solution.py:824
  221.7 4.4 multiply_reduce_fusion.9
  226.2 3.0 multiply_reduce_fusion.8
  229.2 4.9 all-reduce.2
  236.6 3.1 copy.132
  241.7 3.0 copy.133
  244.7 6.7 copy.111
  257.2 2.5 copy-done.79
  269.3 19.4 %shard_map.256 = bf16[192,2048]{1,0:T(8,128)(2,1)} custom-call(bf16[192,2048]{1,0:T(8,128)(2,1)} %dynamic-slice_convert_fusion.1.src), custom_call_target="tpu_custom_call" | custom-call | tf_op jit(solution)/shard_map/pallas_call | solution.py:696
  289.3 2.8 compare_reduce_fusion
  292.2 4.7 reshape.423.hot_ref
  302.2 149.8 %shard_map.257 = (bf16[4,2,2,2,192,2048]{5,4,3,2,1,0:T(8,128)(2,1)}, bf16[4,2,2,384,2048]{4,3,2,1,0:T(8,128)(2,1)}, bf16[4,2,2,384,2176]{4,3,2,1,0:T(8,128)(2,1)...) custom-call(bf16[192,2048]{1,0:T(8,128)(2,1)} %multiply_convert_fusi, ...), custom_call_target="tpu_custom_call" | custom-call | flops 99999997952 | bytes 100000000 | tf_op jit(solution)/shard_map/pallas_call | solution.py:1193
  452.0 137.9 %shard_map.258 = bf16[192,2176]{1,0:T(8,128)(2,1)} custom-call(bf16[4,2,2,2,192,2176]{5,4,3,2,1,0:T(8,128)(2,1)} %bitcast.126), custom_call_target="tpu_custom_call" | custom-call | flops 99999997952 | bytes 100000000 | tf_op jit(solution)/shard_map/pallas_call | solution.py:661
  595.2 19.6 %shard_map.259 = bf16[192,2048]{1,0:T(8,128)(2,1)} custom-call(bf16[192,2048]{1,0:T(8,128)(2,1)} %get-tuple-element.150.src), custom_call_target="tpu_custom_call" | custom-call | tf_op jit(solution)/shard_map/pallas_call | solution.py:696
  617.3 4.5 convolution_convert_fusion.4
  623.1 4.7 multiply_reduce_fusion
  635.6 2.1 copy.130
  637.7 2.7 multiply_reduce_fusion.2
  640.9 5.1 all-reduce.1
  646.0 2.4 subtract_convert_fusion
  662.3 18.2 %shard_map.261 = bf16[192,2048]{1,0:T(8,128)(2,1)} custom-call(bf16[192,2048]{1,0:T(8,128)(2,1)} %dynamic-slice_convert_fusion.src), custom_call_target="tpu_custom_call" | custom-call | tf_op jit(solution)/shard_map/pallas_call | solution.py:696
  680.6 4.4 convolution_convert_fusion
  685.0 4.3 convolution_convert_fusion.1
  689.4 4.7 convolution_convert_fusion.2
  694.1 4.4 convolution_convert_fusion.3
  698.5 48.2 %shard_map.260 = (f32[2048,512]{1,0:T(8,128)}, f32[2048,512]{1,0:T(8,128)}, f32[512,2048]{1,0:T(8,128)}) custom-call(bf16[6144,2048]{1,0:T(8,128)(2,1)} %bitcast.127, bf16[6144,2048]{1,0:T(8,128)(2,1)} %all-gather.2.cloned.1.call-done.g_ref, bf16[6144,512]{1,0:T(8,128)(2,1)} %bitcast.128, bf16[6144,512]{1,0:T(8,128)(2,1)} %bitcast.129, ...), custom_call_target="tpu_custom_call" | custom-call | flops 38654705664 | bytes 62914560 | tf_op jit(solution)/shard_map/pallas_call | solution.py:1251
  746.8 2.1 fusion.13
  750.7 170.3 %shard_map.262 = (f32[128,1024]{1,0:T(8,128)}, f32[128,1024]{1,0:T(8,128)}, f32[128,1024]{1,0:T(8,128)}, f32[128,1024]{1,0:T(8,128)}, f32[24,2048]{1,0:T(8,128)}) custom-call(bf16[4,2,2,128,1024]{4,3,2,1,0:T(8,128)(2,1)} %bitcast.143, bf16[4,2,2,128,1024]{4,3,2,1,0:T(8,128)(2,1)} %bitcast.142, bf16[4,2,2,128,1024]{4,3,2,1,0:T(8,128)(2,1)} %bitcast.141, ...), custom_call_target="tpu_custom_call" | custom-call | flops 99999997952 | bytes 100000000 | tf_op jit(solution)/shard_map/pallas_call | solution.py:969
  924.2 3.2 fusion.12
  927.5 2.3 add_convert_fusion
  (266 shorter events, 69.6 us)
Async XLA Ops:
  7.2 295.0 %all-gather.2.cloned.1.call-start = ((), (), s32[]{:S(2)}) async-start(), calls=%async_computation.1 | async-start | bytes 25952256 | tf_op jit(solution)/shard_map/all_gather | solution.py:1312
  7.9 919.5 %reduce-scatter.2.cloned.1.call-start = ((), (), s32[]{:S(2)}) async-start(), calls=%async_computation.2 | async-start | bytes 25952256 | tf_op jit(solution)/shard_map/reduce_scatter | solution.py:1369
  9.9 28.4 %copy-start.69 = (f32[192]{0:T(256)}, f32[192]{0:T(256)S(1)}, u32[]{:S(2)}) copy-start(f32[192]{0:T(256)S(1)} %get-tuple-element.185) | copy-start | bytes 2308
  9.9 27.6 %copy-start.63 = (s32[384,8]{0,1:T(8,128)S(1)}, s32[384,8]{0,1:T(8,128)}, u32[]{:S(2)}) copy-start(s32[384,8]{0,1:T(8,128)} %param.16) | copy-start | bytes 36868
  9.9 28.4 %copy-start.77 = (f32[2048]{0:T(1024)S(1)}, f32[2048]{0:T(1024)}, u32[]{:S(2)}) copy-start(f32[2048]{0:T(1024)} %param.19) | copy-start | bytes 24580
  38.3 196.4 %copy-start.57 = (f32[1024]{0:T(1024)}, f32[1024]{0:T(1024)S(1)}, u32[]{:S(2)}) copy-start(f32[1024]{0:T(1024)S(1)} %dynamic_slice.21) | copy-start | bytes 12292
  40.9 216.3 %copy-start.32 = (bf16[192,2048]{1,0:T(8,128)(2,1)}, bf16[192,2048]{1,0:T(8,128)(2,1)S(1)}, u32[]{:S(2)}) copy-start(bf16[192,2048]{1,0:T(8,128)(2,1)S(1)} %get-tuple-element.164) | copy-start | bytes 2359300
  221.7 4.5 copy-start.34
  221.7 4.5 copy-start.82
  226.2 8.5 copy-start.6
  234.7 5.1 copy-start.67
  244.7 8.4 copy-start.9
  256.6 5.3 copy-start
  256.6 5.3 copy-start.53
  257.2 4.7 copy-start.61
  292.2 4.7 copy-start.45
  595.2 19.6 %copy-start.14 = (bf16[192,2048]{1,0:T(8,128)(2,1)S(1)}, bf16[192,2048]{1,0:T(8,128)(2,1)}, u32[]{:S(2)}) copy-start(bf16[192,2048]{1,0:T(8,128)(2,1)} %get-tuple-element.150.src) | copy-start | bytes 2359300
  622.2 5.6 slice-start
  623.1 4.7 slice-start.1
  637.7 10.7 %copy-start.73 = (f32[384]{0:T(512)S(1)}, f32[384]{0:T(512)}, u32[]{:S(2)}) copy-start(f32[384]{0:T(512)} %get-tuple-element.203) | copy-start | bytes 4612
  640.4 5.6 copy-start.74
  640.4 10.1 %slice-start.2 = ((s8[4718592]{0:T(1024)(128)(4,1)}), s8[524288]{0:T(1024)(128)(4,1)S(1)}, s32[]{:S(2)}) async-start(s8[4718592]{0:T(1024)(128)(4,1)} %bitcast.96), calls=%async_computation.5 | async-start | bytes 1048576
  661.3 19.2 %copy-start.38 = (bf16[192,2048]{1,0:T(8,128)(2,1)S(1)}, bf16[192,2048]{1,0:T(8,128)(2,1)}, u32[]{:S(2)}) copy-start(bf16[192,2048]{1,0:T(8,128)(2,1)} %copy-done.37) | copy-start | bytes 2359300
  661.3 19.2 %copy-start.40 = (bf16[192,2048]{1,0:T(8,128)(2,1)S(1)}, bf16[192,2048]{1,0:T(8,128)(2,1)}, u32[]{:S(2)}) copy-start(bf16[192,2048]{1,0:T(8,128)(2,1)} %copy-done.39) | copy-start | bytes 2359300
  661.3 19.2 %copy-start.85 = (bf16[8,128,384]{2,1,0:T(8,128)(2,1)S(1)}, bf16[8,128,384]{2,1,0:T(8,128)(2,1)}, u32[]{:S(2)}) copy-start(bf16[8,128,384]{2,1,0:T(8,128)(2,1)} %copy-done.84) | copy-start | bytes 2359300
  689.4 4.7 copy-start.31
  698.5 48.3 %copy-start.5 = (bf16[192,2048]{1,0:T(8,128)(2,1)S(1)}, bf16[192,2048]{1,0:T(8,128)(2,1)}, u32[]{:S(2)}) copy-start(bf16[192,2048]{1,0:T(8,128)(2,1)} %param.15) | copy-start | bytes 2359300
  698.5 48.3 %copy-start.11 = (bf16[192,2048]{1,0:T(8,128)(2,1)S(1)}, bf16[192,2048]{1,0:T(8,128)(2,1)}, u32[]{:S(2)}) copy-start(bf16[192,2048]{1,0:T(8,128)(2,1)} %shard_map.261) | copy-start | bytes 2359300
  698.5 48.3 %copy-start.52 = (f32[2048]{0:T(1024)S(1)}, f32[2048]{0:T(1024)}, u32[]{:S(2)}) copy-start(f32[2048]{0:T(1024)} %param.18) | copy-start | bytes 24580
  698.5 48.3 %copy-start.70 = (f32[192]{0:T(256)S(1)}, f32[192]{0:T(256)}, u32[]{:S(2)}) copy-start(f32[192]{0:T(256)} %copy-done.69) | copy-start | bytes 2308
  750.7 173.5 %copy-start.19 = (f32[192,2048]{1,0:T(8,128)S(1)}, f32[192,2048]{1,0:T(8,128)}, u32[]{:S(2)}) copy-start(f32[192,2048]{1,0:T(8,128)} %get-tuple-element.151) | copy-start | bytes 4718596
  750.7 173.5 %copy-start.75 = (f32[192]{0:T(256)S(1)}, f32[192]{0:T(256)}, u32[]{:S(2)}) copy-start(f32[192]{0:T(256)} %get-tuple-element.184) | copy-start | bytes 2308
  (60 other events, 134.5 us)
Sparse Core Ops, SparseCore 0:
  10.9 235.0 all-gather.1
  590.1 262.9 reduce-scatter.1

commit v4 on v3

--- a/solution.py
+++ b/solution.py
@@ -560,99 +560,153 @@
         lax.fori_loop(0, nz, one, 0)
 
 
-def scatter_kernel(parts, out, total, from_c, half_x, half_y, full_x, full_y, up_buf, down_buf, sent, got, loaded):
-    place = Place()
-    z, x, c, y, nz = place.z, place.x, place.c, place.y, place.z_count
-    rows = total.shape[3]
-    half = rows // 2
+class Fold:
     CD, CX, CY, CO, XH, YH, XF, YF, ZU, ZD = range(10)
-    over_x, over_y, over_c = place.device(x=1 - x), place.device(y=1 - y), place.device(c=1 - c)
-    place.meet()
-
-    def spot(kind):
-        return {CD: (1, 1), CX: (1, 0), CY: (0, 1), CO: (0, 0)}[kind]
-
-    for kind in (CD, CX, CY, CO):
-        dx, dy = spot(kind)
+    SPOT = {CD: (1, 1), CX: (1, 0), CY: (0, 1), CO: (0, 0)}
+
+    def __init__(self, place, parts, total, from_c, half_x, half_y, z_buf, sent, got, loaded):
+        self.place, self.parts, self.total, self.from_c = place, parts, total, from_c
+        self.half_x, self.half_y, self.z_buf = half_x, half_y, z_buf
+        self.sent, self.got, self.loaded = sent, got, loaded
+        self.rows = total.shape[3]
+        self.split = half_x.shape[1]
+        self.low, self.high = pl.ds(0, self.split), pl.ds(self.split, self.rows - self.split)
+        z, x, c, y = place.z, place.x, place.c, place.y
+        self.over_x, self.over_y = place.device(x=1 - x), place.device(y=1 - y)
+        self.over_c = place.device(c=1 - c)
+
+    def push(self, kind, zz, src, dst, device):
+        send(src, dst, self.sent.at[kind, zz], self.got.at[kind, zz], device)
+
+    def arrival(self, kind, zz, ref):
+        pltpu.make_async_copy(ref, ref, self.got.at[kind, zz]).wait()
+
+    def begin(self):
+        x, c, y, nz = self.place.x, self.place.c, self.place.y, self.place.z_count
+
+        def start(kind, i):
+            dx, dy = self.SPOT[kind]
+            zz = self.place.far_first(i)
+            xx, yy = (1 - x if dx else x), (1 - y if dy else y)
+            self.push(
+                kind, zz, self.parts.at[zz, xx, 1 - c, yy], self.from_c.at[dx, dy, zz], self.over_c
+            )
+            pltpu.make_async_copy(
+                self.parts.at[zz, xx, c, yy], self.total.at[dx, dy, zz], self.loaded.at[kind, zz]
+            ).start()
+
         for i in range(nz):
-            zz = place.far_first(i)
-            xx, yy = (1 - x if dx else x), (1 - y if dy else y)
-            send(parts.at[zz, xx, 1 - c, yy], from_c.at[dx, dy, zz], sent.at[kind, zz], got.at[kind, zz], over_c)
-            pltpu.make_async_copy(parts.at[zz, xx, c, yy], total.at[dx, dy, zz], loaded.at[kind, zz]).start()
-
-    def arrival(kind, zz, ref):
-        pltpu.make_async_copy(ref, ref, got.at[kind, zz]).wait()
-
-    def join_cores(kind, zz):
-        dx, dy = spot(kind)
-        here, there = total.at[dx, dy, zz], from_c.at[dx, dy, zz]
-        pltpu.make_async_copy(here, here, loaded.at[kind, zz]).wait()
-        arrival(kind, zz, there)
-        add_rows(here, there, rows)
-
-    low, high = pl.ds(0, half), pl.ds(half, half)
-    for i in range(nz):
-        zz = place.far_first(i)
-        join_cores(CD, zz)
-        send(total.at[1, 1, zz, low], half_x.at[zz], sent.at[XH, zz], got.at[XH, zz], over_x)
-        send(total.at[1, 1, zz, high], half_y.at[zz], sent.at[YH, zz], got.at[YH, zz], over_y)
-    for i in range(nz):
-        zz = place.far_first(i)
-        join_cores(CX, zz)
-        join_cores(CY, zz)
-        arrival(XH, zz, half_x.at[zz])
-        add_rows(total.at[0, 1, zz, low], half_x.at[zz], half)
-        send(total.at[0, 1, zz], full_y.at[zz], sent.at[YF, zz], got.at[YF, zz], over_y)
-        arrival(YH, zz, half_y.at[zz])
-        add_rows(total.at[1, 0, zz, high], half_y.at[zz], half)
-        send(total.at[1, 0, zz], full_x.at[zz], sent.at[XF, zz], got.at[XF, zz], over_x)
-    for i in range(nz):
-        zz = place.far_first(i)
-        mine = total.at[0, 0, zz]
-        join_cores(CO, zz)
-        arrival(XF, zz, full_x.at[zz])
-        add_rows(mine, full_x.at[zz], rows)
-        arrival(YF, zz, full_y.at[zz])
-        add_rows(mine, full_y.at[zz], rows)
+            start(self.CD, i)
+            start(self.CX, i)
+        for kind in (self.CY, self.CO):
+            for i in range(nz):
+                start(kind, i)
+
+    def join_cores(self, kind, zz):
+        dx, dy = self.SPOT[kind]
+        here, there = self.total.at[dx, dy, zz], self.from_c.at[dx, dy, zz]
+        pltpu.make_async_copy(here, here, self.loaded.at[kind, zz]).wait()
+        self.arrival(kind, zz, there)
+        add_rows(here, there, self.rows)
+
+    def halves(self, i):
+        zz = self.place.far_first(i)
+        self.join_cores(self.CD, zz)
+        self.join_cores(self.CX, zz)
+        self.push(self.XH, zz, self.total.at[1, 1, zz, self.low], self.half_x.at[zz], self.over_x)
+        self.push(self.YH, zz, self.total.at[1, 1, zz, self.high], self.half_y.at[zz], self.over_y)
+
+    def columns(self, i):
+        zz = self.place.far_first(i)
+        self.join_cores(self.CY, zz)
+        self.arrival(self.XH, zz, self.half_x.at[zz])
+        add_rows(self.total.at[0, 1, zz, self.low], self.half_x.at[zz], self.split)
+        self.arrival(self.YH, zz, self.half_y.at[zz])
+        add_rows(self.total.at[1, 0, zz, self.high], self.half_y.at[zz], self.rows - self.split)
+        self.push(self.XF, zz, self.total.at[1, 0, zz], self.from_c.at[1, 1, zz], self.over_x)
+        self.push(self.YF, zz, self.total.at[0, 1, zz], self.from_c.at[1, 0, zz], self.over_y)
+
+    def along_z(self, i):
+        z, nz = self.place.z, self.place.z_count
+        zz = self.place.far_first(i)
+        mine = self.total.at[0, 0, zz]
+        self.join_cores(self.CO, zz)
+        self.arrival(self.XF, zz, self.from_c.at[1, 1, zz])
+        add_rows(mine, self.from_c.at[1, 1, zz], self.rows)
+        self.arrival(self.YF, zz, self.from_c.at[1, 0, zz])
+        add_rows(mine, self.from_c.at[1, 0, zz], self.rows)
+        above = jnp.where(zz == z, nz, zz)
 
         @pl.when((z > 0) & (zz >= z))
         def _():
-            arrival(ZU, zz, up_buf.at[zz])
-            add_rows(mine, up_buf.at[zz], rows)
+            self.arrival(self.ZU, zz, self.z_buf.at[zz])
+            add_rows(mine, self.z_buf.at[zz], self.rows)
 
         @pl.when((z < nz - 1) & (zz <= z))
         def _():
-            arrival(ZD, zz, down_buf.at[zz])
-            add_rows(mine, down_buf.at[zz], rows)
+            self.arrival(self.ZD, zz, self.z_buf.at[above])
+            add_rows(mine, self.z_buf.at[above], self.rows)
 
         @pl.when(zz > z)
         def _():
-            send(mine, up_buf.at[zz], sent.at[ZU, zz], got.at[ZU, zz], place.device(z=z + 1))
+            self.push(self.ZU, zz, mine, self.z_buf.at[zz], self.place.device(z=z + 1))
 
         @pl.when(zz < z)
         def _():
-            send(mine, down_buf.at[zz], sent.at[ZD, zz], got.at[ZD, zz], place.device(z=z - 1))
-
-    out[...] = total[0, 0, z]
-
-    def departure(kind, zz, ref):
-        pltpu.make_async_copy(ref, ref, sent.at[kind, zz]).wait()
-
-    for zz in range(nz):
-        for kind in (CD, CX, CY, CO):
-            departure(kind, zz, total.at[0, 0, zz])
-        departure(XH, zz, half_x.at[zz])
-        departure(YH, zz, half_y.at[zz])
-        departure(XF, zz, full_x.at[zz])
-        departure(YF, zz, full_y.at[zz])
-
-        @pl.when(zz > z)
-        def _():
-            departure(ZU, zz, up_buf.at[zz])
-
-        @pl.when(zz < z)
-        def _():
-            departure(ZD, zz, down_buf.at[zz])
+            landing = jnp.where(zz == z - 1, nz, zz)
+            self.push(self.ZD, zz, mine, self.z_buf.at[landing], self.place.device(z=z - 1))
+
+    def result(self):
+        return self.total[0, 0, self.place.z]
+
+    def finish(self):
+        z, nz = self.place.z, self.place.z_count
+
+        def departure(kind, zz, ref):
+            pltpu.make_async_copy(ref, ref, self.sent.at[kind, zz]).wait()
+
+        def one(zz, carry):
+            for kind in (self.CD, self.CX, self.CY, self.CO, self.XF, self.YF):
+                departure(kind, zz, self.total.at[0, 0, zz])
+            departure(self.XH, zz, self.half_x.at[zz])
+            departure(self.YH, zz, self.half_y.at[zz])
+
+            @pl.when(zz > z)
+            def _():
+                departure(self.ZU, zz, self.total.at[0, 0, zz])
+
+            @pl.when(zz < z)
+            def _():
+                departure(self.ZD, zz, self.total.at[0, 0, zz])
+
+            return carry
+
+        lax.fori_loop(0, nz, one, 0)
+
+
+def fold_scratch(nz, rows, cols, split, dt):
+    return [
+        pltpu.VMEM((2, 2, nz, rows, cols), dt),
+        pltpu.VMEM((2, 2, nz, rows, cols), dt),
+        pltpu.VMEM((nz, split, cols), dt),
+        pltpu.VMEM((nz, rows - split, cols), dt),
+        pltpu.VMEM((nz + 1, rows, cols), dt),
+        pltpu.SemaphoreType.DMA((10, nz)),
+        pltpu.SemaphoreType.DMA((10, nz)),
+        pltpu.SemaphoreType.DMA((4, nz)),
+    ]
+
+
+def scatter_kernel(parts, out, *scratch):
+    place = Place()
+    fold = Fold(place, parts, *scratch)
+    place.meet()
+    fold.begin()
+    for step in (fold.halves, fold.columns, fold.along_z):
+        for i in range(place.z_count):
+            step(i)
+    out[...] = fold.result()
+    fold.finish()
 
 
 def scatter_sum(parts, collective):
@@ -663,19 +717,7 @@
         out_shape=jax.ShapeDtypeStruct((rows, cols), dt),
         in_specs=[ANYWHERE],
         out_specs=IN_VMEM,
-        scratch_shapes=[
-            pltpu.VMEM((2, 2, nz, rows, cols), dt),
-            pltpu.VMEM((2, 2, nz, rows, cols), dt),
-            pltpu.VMEM((nz, rows // 2, cols), dt),
-            pltpu.VMEM((nz, rows // 2, cols), dt),
-            pltpu.VMEM((nz, rows, cols), dt),
-            pltpu.VMEM((nz, rows, cols), dt),
-            pltpu.VMEM((nz, rows, cols), dt),
-            pltpu.VMEM((nz, rows, cols), dt),
-            pltpu.SemaphoreType.DMA((10, nz)),
-            pltpu.SemaphoreType.DMA((10, nz)),
-            pltpu.SemaphoreType.DMA((4, nz)),
-        ],
+        scratch_shapes=fold_scratch(nz, rows, cols, rows // 2, dt),
         cost_estimate=LINK_TIME,
         compiler_params=pltpu.CompilerParams(
             collective_id=collective, has_side_effects=True, vmem_limit_bytes=58 << 20
@@ -715,6 +757,201 @@
     other = lax.dynamic_slice_in_dim(part, (1 - index) * rows, rows, 0).astype(jnp.bfloat16)
     mine = lax.dynamic_slice_in_dim(part, index * rows, rows, 0)
     return mine + swap_tensor(other, collective).astype(jnp.float32)
+
+
+def turn(values):
+    return pltpu.roll(values, HEAD // 2, 1)
+
+
+def seen_keys():
+    row = lax.broadcasted_iota(jnp.int32, (GROUP, GROUP), 0)
+    col = lax.broadcasted_iota(jnp.int32, (GROUP, GROUP), 1)
+    return (col <= row) & ((col < PROMPT) | (col >= row - row % CONT))
+
+
+def signed_rope_tables():
+    cosine_table, sine_table = rope_tables()
+    sign = jnp.where(jnp.arange(HEAD) < HEAD // 2, -1.0, 1.0)
+    return cosine_table, sine_table * sign[None, :]
+
+
+def attend_kernel(
+    queries, keys, values, q_inv, k_inv, q_gain, k_gain, cosine, sine, q_rot, k_rot, mixed, log_total
+):
+    visible = seen_keys()
+
+    def head(h, carry):
+        here = pl.ds(pl.multiple_of(h * HEAD, HEAD), HEAD)
+        for raw, inv, gain, rotated in ((queries, q_inv, q_gain, q_rot), (keys, k_inv, k_gain, k_rot)):
+            normal = raw[:, here] * inv[...] * gain[:, here]
+            rotated[:, here] = (normal * cosine[...] + turn(normal) * sine[...]).astype(jnp.bfloat16)
+        scores = dot_nt(q_rot[:, here], k_rot[:, here]) * HEAD**-0.5
+        scores = jnp.where(visible, scores, -1e30)
+        row_max = jnp.max(scores, axis=1, keepdims=True)
+        exponent = jnp.exp(scores - row_max)
+        row_total = jnp.sum(exponent, axis=1, keepdims=True)
+        log_total[h] = row_max + jnp.log(row_total)
+        weights = (exponent / row_total).astype(jnp.bfloat16)
+        mixed[:, here] = dot_nn(weights, values[:, here]).astype(jnp.bfloat16)
+        return carry
+
+    lax.fori_loop(0, queries.shape[1] // HEAD, head, 0)
+
+
+def attend(queries, keys, values, q_inv, k_inv, q_gain, k_gain, tables):
+    rows, cols = queries.shape
+    half = jax.ShapeDtypeStruct((rows, cols), jnp.bfloat16)
+    return pl.pallas_call(
+        attend_kernel,
+        out_shape=[half, half, half, jax.ShapeDtypeStruct((cols // HEAD, rows, 1), jnp.float32)],
+        in_specs=[IN_VMEM] * 9,
+        out_specs=[IN_VMEM] * 4,
+        cost_estimate=pl.CostEstimate(
+            flops=4 * rows * rows * cols, bytes_accessed=16 * rows * cols, transcendentals=rows * rows * 8
+        ),
+        compiler_params=pltpu.CompilerParams(vmem_limit_bytes=40 << 20),
+    )(queries, keys, values, q_inv, k_inv, q_gain, k_gain, *tables)
+
+
+def attend_back_kernel(
+    parts,
+    own_grad,
+    o_all,
+    queries,
+    keys,
+    q_rot,
+    k_rot,
+    values,
+    q_inv,
+    k_inv,
+    log_total,
+    q_gain,
+    k_gain,
+    cosine,
+    sine,
+    mixture,
+    attended_grad,
+    q_grad,
+    k_grad,
+    v_grad,
+    gain_grads,
+    landed,
+    mixed_grad,
+    q_scaled,
+    k_scaled,
+    dots,
+    dots_got,
+    swap_sems,
+    *scratch,
+):
+    place = Place()
+    nz = place.z_count
+    fold = Fold(place, parts, *scratch)
+    place.meet()
+    over_y = place.device(y=1 - place.y)
+    rows = own_grad.shape[0]
+    swap = send(own_grad, landed, swap_sems.at[0, 0], swap_sems.at[1, 0], over_y)
+    fold.begin()
+
+    def take(block, index):
+        where = pl.ds(pl.multiple_of(index * rows, rows), rows)
+        attended_grad[where] = block[...]
+        mixed_grad[where] = dot_nt(block[...], o_all[...]).astype(jnp.bfloat16)
+
+    take(own_grad, place.y)
+    for i in range(nz):
+        fold.halves(i)
+    swap.wait()
+    take(landed, 1 - place.y)
+    visible = seen_keys()
+    lane = lax.broadcasted_iota(jnp.int32, dots.shape, 1)
+    dots[...] = jnp.zeros_like(dots)
+
+    def head(h, carry):
+        here = pl.ds(pl.multiple_of(h * HEAD, HEAD), HEAD)
+        upstream = mixed_grad[:, here]
+        scores = dot_nt(q_rot[:, here], k_rot[:, here]) * HEAD**-0.5
+        probs = jnp.exp(jnp.where(visible, scores, -1e30) - log_total[h])
+        prob_grad = dot_nt(upstream, values[:, here])
+        row_dot = jnp.sum(prob_grad * probs, axis=1, keepdims=True)
+        score_grad = (probs * (prob_grad - row_dot)).astype(jnp.bfloat16)
+        v_grad[:, here] = dot_tn(probs.astype(jnp.bfloat16), upstream).astype(jnp.bfloat16)
+        for index, (rot_grad, raw, inv, gain, scaled) in enumerate(
+            (
+                (dot_nn(score_grad, k_rot[:, here]), queries, q_inv, q_gain, q_scaled),
+                (dot_tn(score_grad, q_rot[:, here]), keys, k_inv, k_gain, k_scaled),
+            )
+        ):
+            rot_grad = rot_grad * HEAD**-0.5
+            norm_grad = rot_grad * cosine[...] - turn(rot_grad) * sine[...]
+            with_raw = norm_grad * raw[:, here]
+            gain_grads[index : index + 1, here] = jnp.sum(with_raw * inv[...], axis=0, keepdims=True)
+            scaled[:, here] = norm_grad * gain[:, here]
+            part = jnp.sum(with_raw * gain[:, here], axis=1, keepdims=True)
+            dots[...] += jnp.where(lane == index, part, 0.0)
+        return carry
+
+    heads = queries.shape[1] // HEAD
+    cuts = [heads * (i + 1) // nz for i in range(nz)]
+    for i in range(nz):
+        fold.columns(i)
+        lax.fori_loop(cuts[i - 1] if i else 0, cuts[i], head, 0)
+    dots_swap = send(dots, dots_got, swap_sems.at[0, 1], swap_sems.at[1, 1], over_y)
+    for i in range(nz):
+        fold.along_z(i)
+    mixture[...] = fold.result()
+    dots_swap.wait()
+
+    def grads(h, carry):
+        here = pl.ds(pl.multiple_of(h * HEAD, HEAD), HEAD)
+        for index, (raw, inv, scaled, grad) in enumerate(
+            ((queries, q_inv, q_scaled, q_grad), (keys, k_inv, k_scaled, k_grad))
+        ):
+            mean = (dots[:, index : index + 1] + dots_got[:, index : index + 1]) / D
+            scale = inv[...]
+            grad[:, here] = (
+                scale * scaled[:, here] - raw[:, here] * (scale * scale * scale * mean)
+            ).astype(jnp.bfloat16)
+        return carry
+
+    lax.fori_loop(0, heads, grads, 0)
+    fold.finish()
+
+
+def attend_back(parts, own_grad, o_all, saved, gains, tables, collective):
+    nz, _, _, _, rows, cols = parts.shape
+    queries = saved[0]
+    group, head_cols = queries.shape
+    half = jax.ShapeDtypeStruct((group, head_cols), jnp.bfloat16)
+    wide = pltpu.VMEM((group, head_cols), jnp.float32)
+    split = rows * 2 // 3
+    return pl.pallas_call(
+        attend_back_kernel,
+        out_shape=[
+            jax.ShapeDtypeStruct((rows, cols), jnp.bfloat16),
+            jax.ShapeDtypeStruct((group, cols), jnp.bfloat16),
+            half,
+            half,
+            half,
+            jax.ShapeDtypeStruct((8, head_cols), jnp.float32),
+        ],
+        in_specs=[ANYWHERE] + [IN_VMEM] * 14,
+        out_specs=[IN_VMEM] * 6,
+        scratch_shapes=[
+            pltpu.VMEM((rows, cols), jnp.bfloat16),
+            pltpu.VMEM((group, head_cols), jnp.bfloat16),
+            wide,
+            wide,
+            pltpu.VMEM((group, LANES), jnp.float32),
+            pltpu.VMEM((group, LANES), jnp.float32),
+            pltpu.SemaphoreType.DMA((2, 2)),
+        ]
+        + fold_scratch(nz, rows, cols, split, parts.dtype),
+        cost_estimate=LINK_TIME,
+        compiler_params=pltpu.CompilerParams(
+            collective_id=collective, has_side_effects=True, vmem_limit_bytes=62 << 20
+        ),
+    )(parts, own_grad, o_all, *saved, *gains, *tables)
 
 
 def plane_gather_kernel(count, *refs):
@@ -837,55 +1074,39 @@
 
 
 def plane_scatter_kernel(count, *refs):
-    parts, small = refs[:count], refs[count]
-    outs, small_out = refs[count + 1 : 2 * count + 1], refs[2 * count + 1]
-    (
-        total,
-        from_c,
-        full_x,
-        up_buf,
-        down_buf,
-        small_sum,
-        small_got,
-        sent,
-        got,
-        loaded,
-        small_sems,
-    ) = refs[2 * count + 2 :]
+    parts, small, row_part = refs[:count], refs[count], refs[count + 1]
+    streams = refs[count + 2 : count + 7]
+    refs = refs[count + 7 :]
+    outs, small_out, row_landed = refs[:count], refs[count], refs[count + 1]
+    wg_grad, wu_grad, wd_grad = refs[count + 2 : count + 5]
+    total, from_c, full_x, z_buf, small_sum, small_got = refs[count + 5 : count + 11]
+    tiles = refs[count + 11 : count + 16]
+    sent, got, loaded, small_sems, row_sems, tile_sems = refs[count + 16 :]
     place = Place()
     z, x, c, nz = place.z, place.x, place.c, place.z_count
     rows = total.shape[3]
     C0, C1, XF, ZU, ZD = range(5)
     over_x, over_c = place.device(x=1 - x), place.device(c=1 - c)
+    over_y = place.device(y=1 - place.y)
     place.meet(all_z=True)
 
-    def arrival(a, kind, zz, ref):
-        pltpu.make_async_copy(ref, ref, got.at[kind, a, zz]).wait()
-
-    for dx, kind in ((1, C1), (0, C0)):
-        for i in range(nz):
-            zz = place.far_first(i)
-            xx = 1 - x if dx else x
-            for a in range(count):
-                send(parts[a].at[zz, xx, 1 - c], from_c.at[dx, zz, a], sent.at[kind, a, zz], got.at[kind, a, zz], over_c)
-                pltpu.make_async_copy(parts[a].at[zz, xx, c], total.at[dx, zz, a], loaded.at[dx, a, zz]).start()
-
-    def join_cores(a, dx, zz):
-        here, there = total.at[dx, zz, a], from_c.at[dx, zz, a]
-        pltpu.make_async_copy(here, here, loaded.at[dx, a, zz]).wait()
-        arrival(a, C1 if dx else C0, zz, there)
-        add_rows(here, there, rows)
-
     small_sum[0] = small[...]
 
-    def small_step(i):
-        if i < 3:
-            partner = (over_c, place.device(y=1 - place.y), over_x)[i]
-            copy = send(small_sum.at[i], small_got.at[i], small_sems.at[0, i], small_sems.at[1, i], partner)
-            copy.wait()
-            small_sum[i + 1] = small_sum[i] + small_got[i]
-            return
-        copies = [
+    def small_start(i):
+        return send(
+            small_sum.at[i],
+            small_got.at[i],
+            small_sems.at[0, i],
+            small_sems.at[1, i],
+            (over_x, over_c, over_y)[i],
+        )
+
+    def small_end(i, copy):
+        copy.wait()
+        small_sum[i + 1] = small_sum[i] + small_got[i]
+
+    def small_z_start():
+        return [
             send(
                 small_sum.at[3],
                 small_got.at[2 + d],
@@ -895,6 +1116,8 @@
             )
             for d in range(1, nz)
         ]
+
+    def small_z_end(copies):
         for copy in copies:
             copy.wait()
         result = jnp.zeros_like(small_out)
@@ -903,14 +1126,68 @@
             result = result + jnp.where(away == 0, small_sum[3], small_got[jnp.maximum(2 + away, 3)])
         small_out[...] = result
 
-    for i in range(nz):
+    count_tiles = streams[0].shape[0]
+
+    def tile_loads(t, slot):
+        return [
+            pltpu.make_async_copy(stream.at[t], tile.at[slot], tile_sems.at[slot, n])
+            for n, (stream, tile) in enumerate(zip(streams, tiles))
+        ]
+
+    def tile_step(t, carry):
+        slot = t % 2
+        for copy in tile_loads(t, slot):
+            copy.wait()
+
+        @pl.when(t + 1 < count_tiles)
+        def _():
+            for copy in tile_loads(t + 1, 1 - slot):
+                copy.start()
+
+        x_tile, g_tile, hidden, gate_pre_grad, up_grad = (tile[slot] for tile in tiles)
+        wg_grad[...] += dot_tn(x_tile, gate_pre_grad)
+        wu_grad[...] += dot_tn(x_tile, up_grad)
+        wd_grad[...] += dot_tn(hidden, g_tile)
+        return carry
+
+    def arrival(a, kind, zz, ref):
+        pltpu.make_async_copy(ref, ref, got.at[kind, a, zz]).wait()
+
+    small_copy = small_start(0)
+    for dx, kind in ((1, C1), (0, C0)):
+        for i in range(nz):
+            zz = place.far_first(i)
+            xx = 1 - x if dx else x
+            for a in range(count):
+                send(
+                    parts[a].at[zz, xx, 1 - c],
+                    from_c.at[dx, zz, a],
+                    sent.at[kind, a, zz],
+                    got.at[kind, a, zz],
+                    over_c,
+                )
+                pltpu.make_async_copy(
+                    parts[a].at[zz, xx, c], total.at[dx, zz, a], loaded.at[dx, a, zz]
+                ).start()
+    for copy in tile_loads(0, 0):
+        copy.start()
+
+    def join_cores(a, dx, zz):
+        here, there = total.at[dx, zz, a], from_c.at[dx, zz, a]
+        pltpu.make_async_copy(here, here, loaded.at[dx, a, zz]).wait()
+        arrival(a, C1 if dx else C0, zz, there)
+        add_rows(here, there, rows)
+
+    def over_the_x(i):
         zz = place.far_first(i)
-        small_step(min(i, 3))
         for a in range(count):
             join_cores(a, 1, zz)
             send(total.at[1, zz, a], full_x.at[zz, a], sent.at[XF, a, zz], got.at[XF, a, zz], over_x)
-    for i in range(nz):
+
+    def along_z(i):
         zz = place.far_first(i)
+        above = jnp.where(zz == z, nz, zz)
+        landing = jnp.where(zz == z - 1, nz, zz)
         for a in range(count):
             mine = total.at[0, zz, a]
             join_cores(a, 0, zz)
@@ -919,21 +1196,54 @@
 
             @pl.when((z > 0) & (zz >= z))
             def _():
-                arrival(a, ZU, zz, up_buf.at[zz, a])
-                add_rows(mine, up_buf.at[zz, a], rows)
+                arrival(a, ZU, zz, z_buf.at[zz, a])
+                add_rows(mine, z_buf.at[zz, a], rows)
 
             @pl.when((z < nz - 1) & (zz <= z))
             def _():
-                arrival(a, ZD, zz, down_buf.at[zz, a])
-                add_rows(mine, down_buf.at[zz, a], rows)
+                arrival(a, ZD, zz, z_buf.at[above, a])
+                add_rows(mine, z_buf.at[above, a], rows)
 
             @pl.when(zz > z)
             def _():
-                send(mine, up_buf.at[zz, a], sent.at[ZU, a, zz], got.at[ZU, a, zz], place.device(z=z + 1))
+                send(
+                    mine,
+                    z_buf.at[zz, a],
+                    sent.at[ZU, a, zz],
+                    got.at[ZU, a, zz],
+                    place.device(z=z + 1),
+                )
 
             @pl.when(zz < z)
             def _():
-                send(mine, down_buf.at[zz, a], sent.at[ZD, a, zz], got.at[ZD, a, zz], place.device(z=z - 1))
+                send(
+                    mine,
+                    z_buf.at[landing, a],
+                    sent.at[ZD, a, zz],
+                    got.at[ZD, a, zz],
+                    place.device(z=z - 1),
+                )
+
+    small_end(0, small_copy)
+    over_the_x(0)
+    small_copy = small_start(1)
+    small_end(1, small_copy)
+    small_copy = small_start(2)
+    row_copy = send(row_part, row_landed, row_sems.at[0], row_sems.at[1], over_y)
+    wg_grad[...] = jnp.zeros_like(wg_grad)
+    wu_grad[...] = jnp.zeros_like(wu_grad)
+    wd_grad[...] = jnp.zeros_like(wd_grad)
+    for i in range(1, nz - 1):
+        over_the_x(i)
+    small_end(2, small_copy)
+    small_copies = small_z_start()
+    over_the_x(nz - 1)
+    for i in range(nz):
+        lax.fori_loop(count_tiles * i // nz, count_tiles * (i + 1) // nz, tile_step, 0)
+        if i == 0:
+            small_z_end(small_copies)
+        along_z(i)
+    row_copy.wait()
 
     for a in range(count):
 
@@ -944,52 +1254,66 @@
 
         lax.fori_loop(0, rows // 16, widen, 0)
 
-    def departure(a, kind, zz, ref):
+    def departure(a, kind, zz):
+        ref = total.at[0, 0, a]
         pltpu.make_async_copy(ref, ref, sent.at[kind, a, zz]).wait()
 
     for a in range(count):
         for zz in range(nz):
-            departure(a, C0, zz, total.at[0, 0, a])
-            departure(a, C1, zz, total.at[0, 0, a])
-            departure(a, XF, zz, total.at[0, 0, a])
+            departure(a, C0, zz)
+            departure(a, C1, zz)
+            departure(a, XF, zz)
 
             @pl.when(zz > z)
             def _():
-                departure(a, ZU, zz, total.at[0, 0, a])
+                departure(a, ZU, zz)
 
             @pl.when(zz < z)
             def _():
-                departure(a, ZD, zz, total.at[0, 0, a])
-
-
-def scatter_in_plane(parts, small, collective):
+                departure(a, ZD, zz)
+
+
+def scatter_in_plane(parts, small, row_part, streams, collective):
     nz, _, _, rows, cols = parts[0].shape
     count = len(parts)
     dt = parts[0].dtype
+    width, units = streams[0].shape[1], streams[2].shape[1]
+    tile = 256 if streams[0].shape[0] % 256 == 0 else GROUP // 2
+    streams = [stream.reshape(-1, tile, stream.shape[1]) for stream in streams]
     return pl.pallas_call(
         functools.partial(plane_scatter_kernel, count),
         out_shape=[jax.ShapeDtypeStruct((rows, cols), jnp.float32)] * count
-        + [jax.ShapeDtypeStruct(small.shape, small.dtype)],
-        in_specs=[ANYWHERE] * count + [IN_VMEM],
-        out_specs=[IN_VMEM] * (count + 1),
+        + [
+            jax.ShapeDtypeStruct(small.shape, small.dtype),
+            jax.ShapeDtypeStruct(row_part.shape, row_part.dtype),
+            jax.ShapeDtypeStruct((width, units), jnp.float32),
+            jax.ShapeDtypeStruct((width, units), jnp.float32),
+            jax.ShapeDtypeStruct((units, width), jnp.float32),
+        ],
+        in_specs=[ANYWHERE] * count + [IN_VMEM] + [ANYWHERE] * 6,
+        out_specs=[IN_VMEM] * (count + 1) + [ANYWHERE] + [IN_VMEM] * 3,
         scratch_shapes=[
             pltpu.VMEM((2, nz, count, rows, cols), dt),
             pltpu.VMEM((2, nz, count, rows, cols), dt),
             pltpu.VMEM((nz, count, rows, cols), dt),
-            pltpu.VMEM((nz, count, rows, cols), dt),
-            pltpu.VMEM((nz, count, rows, cols), dt),
+            pltpu.VMEM((nz + 1, count, rows, cols), dt),
             pltpu.VMEM((4,) + small.shape, small.dtype),
             pltpu.VMEM((2 + nz,) + small.shape, small.dtype),
+        ]
+        + [pltpu.VMEM((2,) + stream.shape[1:], stream.dtype) for stream in streams]
+        + [
             pltpu.SemaphoreType.DMA((5, count, nz)),
             pltpu.SemaphoreType.DMA((5, count, nz)),
             pltpu.SemaphoreType.DMA((2, count, nz)),
             pltpu.SemaphoreType.DMA((2, 2 + nz)),
+            pltpu.SemaphoreType.DMA((2,)),
+            pltpu.SemaphoreType.DMA((2, 5)),
         ],
         cost_estimate=LINK_TIME,
         compiler_params=pltpu.CompilerParams(
-            collective_id=collective, has_side_effects=True, vmem_limit_bytes=58 << 20
+            collective_id=collective, has_side_effects=True, vmem_limit_bytes=62 << 20
         ),
-    )(*parts, small)
+    )(*parts, small, row_part, *streams)
 
 
 def dot_nn(a, b):
@@ -1221,48 +1545,6 @@
     )(block, upstream.reshape(out + (width,)), hot, router, lanes, w_gate, w_up, w_down)
 
 
-def expert_weights_kernel(
-    x_ref, g_ref, hidden_ref, gate_pre_grad_ref, up_grad_ref, wg_grad_ref, wu_grad_ref, wd_grad_ref
-):
-    @pl.when(pl.program_id(0) == 0)
-    def _():
-        wg_grad_ref[...] = jnp.zeros_like(wg_grad_ref)
-        wu_grad_ref[...] = jnp.zeros_like(wu_grad_ref)
-        wd_grad_ref[...] = jnp.zeros_like(wd_grad_ref)
-
-    rows = x_ref[...]
-    wg_grad_ref[...] += dot_tn(rows, gate_pre_grad_ref[...])
-    wu_grad_ref[...] += dot_tn(rows, up_grad_ref[...])
-    wd_grad_ref[...] += dot_tn(hidden_ref[...], g_ref[...])
-
-
-def expert_weights_pass(rows, upstream, hidden, gate_pre_grad, up_grad):
-    count, width = rows.shape
-    units = hidden.shape[1]
-    tile = 512 if count % 512 == 0 else GROUP // 2
-
-    def by_row(cols):
-        return pl.BlockSpec((tile, cols), lambda i: (i, 0))
-
-    def whole(first, second):
-        return pl.BlockSpec((first, second), lambda i: (0, 0), pipeline_mode=pl.Buffered(1))
-
-    shapes = [(width, units), (width, units), (units, width)]
-    return pl.pallas_call(
-        expert_weights_kernel,
-        grid=(count // tile,),
-        in_specs=[by_row(width)] * 2 + [by_row(units)] * 3,
-        out_specs=[whole(*shape) for shape in shapes],
-        out_shape=[jax.ShapeDtypeStruct(shape, jnp.float32) for shape in shapes],
-        cost_estimate=pl.CostEstimate(
-            flops=6 * count * width * units,
-            bytes_accessed=4 * count * width + 12 * width * units,
-            transcendentals=0,
-        ),
-        compiler_params=pltpu.CompilerParams(vmem_limit_bytes=60 << 20),
-    )(rows, upstream, hidden, gate_pre_grad, up_grad)
-
-
 def dense_body(
     tokens,
     routes,
@@ -1283,17 +1565,18 @@
     rank_index = lax.axis_index("tensor")
     own_rows = tokens.shape[0]
     head_cols = w_query.shape[1]
-    local_heads = head_cols // HEAD
     col_start = rank_index * head_cols
     row_start = rank_index * own_rows
     experts = router.shape[1]
-    attn_scale = HEAD ** (-0.5)
-    head_shape = (GROUP, local_heads, HEAD)
     q_gain_local = lax.dynamic_slice_in_dim(q_gain, col_start, head_cols)
     k_gain_local = lax.dynamic_slice_in_dim(k_gain, col_start, head_cols)
+    inputs_both = both_rows(tokens, 5).astype(jnp.float32)
+    unit_both = inputs_both * lax.rsqrt(
+        jnp.mean(inputs_both * inputs_both, axis=1, keepdims=True) + EPSILON
+    )
+    normed = (unit_both * attn_gain).astype(jnp.bfloat16)
     inputs = tokens.astype(jnp.float32)
     attn_inv = lax.rsqrt(jnp.mean(inputs * inputs, axis=1, keepdims=True) + EPSILON)
-    normed = both_rows((inputs * attn_inv * attn_gain).astype(jnp.bfloat16), 5)
     q_all, k_all, v_all, o_all, routes_all = gather_in_plane(
         (w_query, w_key, w_value, w_out, routes), 1
     )
@@ -1318,35 +1601,12 @@
     )
     query_inv = lax.rsqrt(query_sq / D + EPSILON)[:, None]
     key_inv = lax.rsqrt(key_sq / D + EPSILON)[:, None]
-    cosine_table, sine_table = rope_tables()
-    query_rot = rotate(
-        (queries * query_inv * q_gain_local).reshape(head_shape), cosine_table, sine_table
-    ).astype(jnp.bfloat16)
-    key_rot = rotate(
-        (keys_raw * key_inv * k_gain_local).reshape(head_shape), cosine_table, sine_table
-    ).astype(jnp.bfloat16)
-    value_heads = values_raw.astype(jnp.bfloat16).reshape(head_shape)
-    visible = visible_keys()[None]
-
-    def masked_scores():
-        raw_scores = (
-            jnp.einsum("qhd,khd->hqk", query_rot, key_rot, preferred_element_type=jnp.float32)
-            * attn_scale
-        )
-        return jnp.where(visible, raw_scores, -1e30)
-
-    scores = masked_scores()
-    row_max = jnp.max(scores, axis=2, keepdims=True)
-    exponent = jnp.exp(scores - row_max)
-    row_total = jnp.sum(exponent, axis=2, keepdims=True)
-    log_total = row_max + jnp.log(row_total)
-    mixed_heads = jnp.einsum(
-        "hqk,khd->qhd",
-        (exponent / row_total).astype(jnp.bfloat16),
-        value_heads,
-        preferred_element_type=jnp.float32,
-    )
-    mixed_heads = mixed_heads.reshape(GROUP, head_cols).astype(jnp.bfloat16)
+    tables = signed_rope_tables()
+    values = values_raw.astype(jnp.bfloat16)
+    gains = (q_gain_local[None], k_gain_local[None])
+    query_rot, key_rot, mixed_heads, log_total = attend(
+        queries, keys_raw, values, query_inv, key_inv, *gains, tables
+    )
     attended = own_rows_sum(matmul(mixed_heads, o_all), 6)
     hidden_one = inputs + attended
     mlp_inv = lax.rsqrt(jnp.mean(hidden_one * hidden_one, axis=1, keepdims=True) + EPSILON)
@@ -1362,11 +1622,6 @@
     for_weights = [array.reshape(rows_all.shape[0], -1) for array in for_weights]
     blocks = (lax.axis_size("dp") // 4, 2, 2, 2, own_rows)
     returned = scatter_sum(r_part.reshape(*blocks, D + LANES), 3)
-    y_part, returned, for_weights = lax.optimization_barrier((y_part, returned, for_weights))
-    gate_weight_grad, up_weight_grad, down_weight_grad = expert_weights_pass(
-        rows_all, upstream_all, *for_weights
-    )
-    mixture = lax.psum_scatter(y_part, EVERY, scatter_dimension=0, tiled=True)
     expert_grad = jnp.sum(
         returned[:, D : D + 4 * experts].astype(jnp.float32).reshape(own_rows, 4, experts), axis=1
     )
@@ -1385,61 +1640,18 @@
         - hidden_one * mlp_inv**3 * jnp.mean(hidden_one * scaled_grad, axis=1, keepdims=True)
     )
     mlp_gain_grad = jnp.sum(normed_two_grad * hidden_one * mlp_inv, axis=0)
-    attended_grad = both_rows(hidden_one_grad.astype(jnp.bfloat16), 7)
-    mixed_grad = jnp.einsum("gd,cd->gc", attended_grad, o_all, preferred_element_type=jnp.float32)
-    mixed_grad = mixed_grad.astype(jnp.bfloat16).reshape(head_shape)
-    attn_probs = jnp.exp(masked_scores() - log_total)
-    prob_grad = jnp.einsum(
-        "qhd,khd->hqk", mixed_grad, value_heads, preferred_element_type=jnp.float32
-    )
-    row_dot = jnp.sum(prob_grad * attn_probs, axis=2, keepdims=True)
-    score_grad = (attn_probs * (prob_grad - row_dot)).astype(jnp.bfloat16)
-    query_rot_grad = (
-        jnp.einsum("hqk,khd->qhd", score_grad, key_rot, preferred_element_type=jnp.float32)
-        * attn_scale
-    )
-    key_rot_grad = (
-        jnp.einsum("hqk,qhd->khd", score_grad, query_rot, preferred_element_type=jnp.float32)
-        * attn_scale
-    )
-    value_grad = (
-        jnp.einsum(
-            "hqk,qhd->khd",
-            attn_probs.astype(jnp.bfloat16),
-            mixed_grad,
-            preferred_element_type=jnp.float32,
-        )
-        .reshape(GROUP, head_cols)
-        .astype(jnp.bfloat16)
-    )
-    query_norm_grad = unrotate(query_rot_grad, cosine_table, sine_table).reshape(GROUP, head_cols)
-    key_norm_grad = unrotate(key_rot_grad, cosine_table, sine_table).reshape(GROUP, head_cols)
-    query_scaled = query_norm_grad * q_gain_local
-    key_scaled = key_norm_grad * k_gain_local
-    query_dot, key_dot = tensor_total(
-        (jnp.sum(queries * query_scaled, axis=1), jnp.sum(keys_raw * key_scaled, axis=1))
-    )
-    query_grad = (
-        query_inv * query_scaled - queries * query_inv**3 * (query_dot / D)[:, None]
-    ).astype(jnp.bfloat16)
-    key_grad = (key_inv * key_scaled - keys_raw * key_inv**3 * (key_dot / D)[:, None]).astype(
-        jnp.bfloat16
-    )
-    q_gain_part = jnp.sum(query_norm_grad * queries * query_inv, axis=0)
-    k_gain_part = jnp.sum(key_norm_grad * keys_raw * key_inv, axis=0)
+    saved = (queries, keys_raw, query_rot, key_rot, values, query_inv, key_inv, log_total)
+    mixture, attended_grad, query_grad, key_grad, value_grad, gain_grads = attend_back(
+        y_part.reshape(*blocks, D), hidden_one_grad.astype(jnp.bfloat16), o_all, saved, gains, tables, 7
+    )
+    layer_out = (hidden_one + mixture.astype(jnp.float32)).astype(jnp.bfloat16)
+    q_gain_part, k_gain_part = gain_grads[0], gain_grads[1]
     normed_part = (
         jnp.einsum("gc,rc->gr", query_grad, q_all, preferred_element_type=jnp.float32)
         + jnp.einsum("gc,rc->gr", key_grad, k_all, preferred_element_type=jnp.float32)
         + jnp.einsum("gc,rc->gr", value_grad, v_all, preferred_element_type=jnp.float32)
     )
-    normed_grad = own_rows_sum(normed_part, 8)
-    scaled_input = normed_grad * attn_gain
-    tokens_grad = (
-        hidden_one_grad
-        + attn_inv * scaled_input
-        - inputs * attn_inv**3 * jnp.mean(inputs * scaled_input, axis=1, keepdims=True)
-    )
-    attn_gain_grad = jnp.sum(normed_grad * inputs * attn_inv, axis=0)
+    attn_gain_grad = jnp.sum(normed_part * unit_both, axis=0)
     zero_width = jnp.zeros((D,), jnp.float32)
     q_gain_full = lax.dynamic_update_slice_in_dim(zero_width, q_gain_part, col_start, 0)
     k_gain_full = lax.dynamic_update_slice_in_dim(zero_width, k_gain_part, col_start, 0)
@@ -1461,12 +1673,23 @@
             (attended_grad, mixed_heads),
         )
     ]
-    products, gate_weight_grad = lax.optimization_barrier((products, gate_weight_grad))
-    *weight_sums, small_sums = scatter_in_plane(products, small_grads, 4)
+    row_part = lax.dynamic_slice_in_dim(
+        normed_part, (1 - rank_index) * own_rows, own_rows, 0
+    ).astype(jnp.bfloat16)
+    own_part = lax.dynamic_slice_in_dim(normed_part, row_start, own_rows, 0)
+    streams = [rows_all, upstream_all, *for_weights]
+    *weight_sums, small_sums, other_part, gate_weight_grad, up_weight_grad, down_weight_grad = (
+        scatter_in_plane(products, small_grads, row_part, streams, 4)
+    )
+    normed_grad = own_part + other_part.astype(jnp.float32)
+    scaled_input = normed_grad * attn_gain
+    tokens_grad = (
+        hidden_one_grad
+        + attn_inv * scaled_input
+        - inputs * attn_inv**3 * jnp.mean(inputs * scaled_input, axis=1, keepdims=True)
+    )
     attn_gain_grad, q_gain_grad, k_gain_grad, mlp_gain_grad = (small_sums[i] for i in range(4))
     router_grad = jnp.transpose(small_sums[8:])
-    mixture, weight_sums = lax.optimization_barrier((mixture, weight_sums))
-    layer_out = (hidden_one + mixture.astype(jnp.float32)).astype(jnp.bfloat16)
     return (
         layer_out,
         tokens_grad,

time: 950 us -> 907 us (0.955)
  other arithmetic: 40.4 us -> 18.9 us
    pallas_call x1 -> x2, Pallas kernels: 48.2 us -> 148 us  [the longest x1 141 us: attend_back(): pl.pallas_call(attend_back_kernel, out_shape=[jax.ShapeDtypeStruct((rows,...]
    pallas_call x1, Pallas kernels: 170 us -> 119 us  [scatter_in_plane(): pl.pallas_call(functools.partial(plane_scatter_kernel, count), out_shape=...]
    pallas_call x4 -> x2, Pallas kernels: 83.6 us -> 45.4 us  [swap_tensor(): pl.pallas_call(swap_kernel, out_shape=jax.ShapeDtypeStruct(block.shape, b...]
    dot_general x7 -> x0, matrix products: 13.9 us -> none  [the longest x1 4.71 us: dense_body(): jnp.einsum('qhd,khd->hqk', mixed_grad, value_heads, preferred_element_typ...]
    reshape x5 -> x0, local copies, waits for them, and re-layouts: 10.2 us -> none  [the longest x1 3.14 us: dense_body(): (queries * query_inv * q_gain_local).reshape(head_shape)]
    unnamed x186 -> x140, local copies, waits for them, and re-layouts: 23.1 us -> 24.4 us
  transfers between devices with their start and end apart: 2 -> 1, of which waited for: 0 -> 0; matrix products, arithmetic and copies ran while one was open for 13% -> 5% of each run, Pallas kernels for 51% -> 26%
where the time goes in v4:
time: 907 us; the launch traced here: 902 us
  Pallas kernels  772 us (85%)
  local copies, waits for them, and re-layouts  45.5 us (5%)
  matrix products  44.2 us (5%)
  other arithmetic  18.9 us (2%)
  between operations  15.4 us (2%)
    pallas_call x1, Pallas kernels, gather_in_plane(): pl.pallas_call(functools.partial(plane_gather_kernel, count), out_shape=[...  181 us
    pallas_call x1, Pallas kernels, expert_pass(): pl.pallas_call(functools.partial(expert_kernel, nz), in_specs=[ANYWHERE]...  149 us
    pallas_call x1, Pallas kernels, attend_back(): pl.pallas_call(attend_back_kernel, out_shape=[jax.ShapeDtypeStruct((rows,...  141 us
    pallas_call x1, Pallas kernels, scatter_sum(): pl.pallas_call(scatter_kernel, out_shape=jax.ShapeDtypeStruct((rows, cols...  130 us
    pallas_call x1, Pallas kernels, scatter_in_plane(): pl.pallas_call(functools.partial(plane_scatter_kernel, count), out_shape=...  119 us
    pallas_call x2, Pallas kernels, swap_tensor(): pl.pallas_call(swap_kernel, out_shape=jax.ShapeDtypeStruct(block.shape, b...  45.4 us
    unnamed x140, local copies, waits for them, and re-layouts  24.4 us
  transfers between devices with their start and end apart: 1, of which 0 were waited for; matrix products, arithmetic and copies ran while one was open for 5% of the time, Pallas kernels for 26%

profile of v4, /device:TPU:0, one launch (start us, length us, event | category | flops | bytes accessed | tf_op | source)
XLA Modules:
  0.0 902.1 jit_solution(1093183594149875070)
XLA Ops:
  7.9 25.8 %shard_map.254 = bf16[192,2048]{1,0:T(8,128)(2,1)} custom-call(bf16[192,2048]{1,0:T(8,128)(2,1)} %src.1), custom_call_target="tpu_custom_call" | custom-call | tf_op jit(solution)/shard_map/pallas_call | solution.py:738
  37.1 180.6 %shard_map.255 = (bf16[4,2,2,128,1024]{4,3,2,1,0:T(8,128)(2,1)}, bf16[4,2,2,128,1024]{4,3,2,1,0:T(8,128)(2,1)}, bf16[4,2,2,128,1024]{4,3,2,1,0:T(8,128)(2,1)}, b...) custom-call(bf16[128,1024]{1,0:T(8,128)(2,1)} %refs_0_.1, bf16[128,1024]{1,0:T(8,128)(2,1)} %refs_1_.1, ...), custom_call_target="tpu_custom_call" | custom-call | flops 99999997952 | bytes 100000000 | tf_op jit(solution)/shard_map/pallas_call | solution.py:1061
  217.8 4.3 multiply_reduce_fusion.3
  222.1 3.9 multiply_reduce_fusion.4
  226.0 5.6 all-reduce.1
  233.3 4.9 copy.58
  238.2 2.0 copy-done.19
  240.2 4.1 copy.68
  245.3 4.6 convolution_convert_fusion.4.values
  250.1 7.1 shard_map.256
  261.9 19.7 %shard_map.257 = bf16[192,2048]{1,0:T(8,128)(2,1)} custom-call(bf16[192,2048]{1,0:T(8,128)(2,1)} %dynamic-slice_convert_fusion.1.src), custom_call_target="tpu_custom_call" | custom-call | tf_op jit(solution)/shard_map/pallas_call | solution.py:738
  283.3 4.7 reshape.218.hot_ref
  294.0 148.7 %shard_map.258 = (bf16[4,2,2,2,192,2048]{5,4,3,2,1,0:T(8,128)(2,1)}, bf16[4,2,2,384,2048]{4,3,2,1,0:T(8,128)(2,1)}, bf16[4,2,2,384,2176]{4,3,2,1,0:T(8,128)(2,1)...) custom-call(bf16[192,2048]{1,0:T(8,128)(2,1)} %copy-done.23, ...), custom_call_target="tpu_custom_call" | custom-call | flops 99999997952 | bytes 100000000 | tf_op jit(solution)/shard_map/pallas_call | solution.py:1517
  442.8 129.9 %shard_map.259 = bf16[192,2176]{1,0:T(8,128)(2,1)} custom-call(bf16[4,2,2,2,192,2176]{5,4,3,2,1,0:T(8,128)(2,1)} %bitcast.85), custom_call_target="tpu_custom_call" | custom-call | flops 99999997952 | bytes 100000000 | tf_op jit(solution)/shard_map/pallas_call | solution.py:715
  573.9 2.4 multiply_reduce_fusion
  576.8 1.9 fusion.27
  578.8 140.6 %shard_map.260 = (bf16[192,2048]{1,0:T(8,128)(2,1)}, bf16[384,2048]{1,0:T(8,128)(2,1)}, bf16[384,1024]{1,0:T(8,128)(2,1)}, bf16[384,1024]{1,0:T(8,128)(2,1)}, bf...) custom-call(bf16[4,2,2,2,192,2048]{5,4,3,2,1,0:T(8,128)(2,1)} %bitcast.87, bf16[192,2048]{1,0:T(8,128)(2,1)} %get-tuple-element.136.own_grad, ...), custom_call_target="tpu_custom_call" | custom-call | flops 99999997952 | bytes 100000000 | tf_op jit(solution)/shard_map/pallas_call | solution.py:928
  719.4 4.4 fusion.31
  723.9 4.5 convolution_convert_fusion.2
  728.4 1.8 fusion.30
  730.3 4.5 convolution_convert_fusion.3
  734.8 4.5 convolution_convert_fusion.1
  739.3 2.3 fusion.3
  744.5 4.4 convolution_convert_fusion
  750.3 119.4 %shard_map.261 = (f32[128,1024]{1,0:T(8,128)}, f32[128,1024]{1,0:T(8,128)}, f32[128,1024]{1,0:T(8,128)}, f32[128,1024]{1,0:T(8,128)}, f32[24,2048]{1,0:T(8,128)}...) custom-call(bf16[4,2,2,128,1024]{4,3,2,1,0:T(8,128)(2,1)} %bitcast.96, ...), custom_call_target="tpu_custom_call" | custom-call | flops 99999997952 | bytes 100000000 | tf_op jit(solution)/shard_map/pallas_call | solution.py:1283
  873.1 2.2 fusion.5
  875.4 2.0 copy.64
  877.4 2.3 add_convert_fusion
  879.8 3.3 fusion.7
  885.4 2.1 copy.81
  889.1 2.1 copy.82
  892.8 2.0 copy.83
  (184 shorter events, 33.7 us)
Async XLA Ops:
  7.2 286.8 %all-gather.2.cloned.1.call-start = ((), (), s32[]{:S(2)}) async-start(), calls=%async_computation | async-start | bytes 25952256 | tf_op jit(solution)/shard_map/all_gather | solution.py:1595
  36.7 181.1 %copy-start.25 = (bf16[192,2048]{1,0:T(8,128)(2,1)}, bf16[192,2048]{1,0:T(8,128)(2,1)S(1)}, u32[]{:S(2)}) copy-start(bf16[192,2048]{1,0:T(8,128)(2,1)S(1)} %get-tuple-element.140) | copy-start | bytes 2359300
  36.7 181.1 %copy-start.27 = (bf16[192,2048]{1,0:T(8,128)(2,1)}, bf16[192,2048]{1,0:T(8,128)(2,1)S(1)}, u32[]{:S(2)}) copy-start(bf16[192,2048]{1,0:T(8,128)(2,1)S(1)} %get-tuple-element.141) | copy-start | bytes 2359300
  37.1 185.0 %copy-start.57 = (f32[384]{0:T(512)}, f32[384]{0:T(512)S(1)}, u32[]{:S(2)}) copy-start(f32[384]{0:T(512)S(1)} %add_rsqrt_fusion.2) | copy-start | bytes 4612
  37.1 180.7 %copy-start.50 = (f32[2048]{0:T(1024)S(1)}, f32[2048]{0:T(1024)}, u32[]{:S(2)}) copy-start(f32[2048]{0:T(1024)} %param.18) | copy-start | bytes 24580
  222.1 27.9 %copy-start = (f32[384,1024]{1,0:T(8,128)}, f32[384,1024]{1,0:T(8,128)S(1)}, u32[]{:S(2)}) copy-start(f32[384,1024]{1,0:T(8,128)S(1)} %get-tuple-element.155.keys) | copy-start | bytes 4718596
  226.0 24.0 %copy-start.1 = (f32[384,1024]{1,0:T(8,128)}, f32[384,1024]{1,0:T(8,128)S(1)}, u32[]{:S(2)}) copy-start(f32[384,1024]{1,0:T(8,128)S(1)} %get-tuple-element.153.queries) | copy-start | bytes 4718596
  231.7 18.3 %copy-start.2 = (f32[384,1]{1,0:T(8,128)}, f32[384,1]{1,0:T(8,128)S(1)}, u32[]{:S(2)}) copy-start(f32[384,1]{1,0:T(8,128)S(1)} %broadcast_in_dim.69.q_inv) | copy-start | bytes 4612
  231.9 18.2 %copy-start.3 = (f32[384,1]{1,0:T(8,128)}, f32[384,1]{1,0:T(8,128)S(1)}, u32[]{:S(2)}) copy-start(f32[384,1]{1,0:T(8,128)S(1)} %broadcast_in_dim.70.k_inv) | copy-start | bytes 4612
  232.6 17.4 %copy-start.7 = (f32[1024]{0:T(1024)}, f32[1024]{0:T(1024)S(1)}, u32[]{:S(2)}) copy-start(f32[1024]{0:T(1024)S(1)} %dynamic_slice.21) | copy-start | bytes 12292
  233.3 16.8 %copy-start.8 = (f32[1024]{0:T(1024)}, f32[1024]{0:T(1024)S(1)}, u32[]{:S(2)}) copy-start(f32[1024]{0:T(1024)S(1)} %dynamic_slice.22) | copy-start | bytes 12292
  250.0 9.1 %copy-start.6 = (bf16[384,1024]{1,0:T(8,128)(2,1)}, bf16[384,1024]{1,0:T(8,128)(2,1)S(1)}, u32[]{:S(2)}) copy-start(bf16[384,1024]{1,0:T(8,128)(2,1)S(1)} %convolution_convert_fusion.4.values) | copy-start | bytes 2359300
  250.0 7.3 copy-start.20
  260.9 21.4 %copy-start.35 = (s32[4,2,2,384,8]{4,3,2,1,0:T(8,128)S(1)}, s32[4,2,2,384,8]{4,3,2,1,0:T(8,128)}, u32[]{:S(2)}) copy-start(s32[4,2,2,384,8]{4,3,2,1,0:T(8,128)} %get-tuple-element.49) | copy-start | bytes 589828
  282.3 5.7 copy-start.39
  283.2 6.0 copy-start.49
  283.2 6.0 copy-start.17
  283.2 6.0 copy-start.36
  292.8 149.9 %copy-start.44 = (f32[192,16]{0,1:T(8,128)}, f32[192,16]{0,1:T(8,128)S(1)}, u32[]{:S(2)}) copy-start(f32[192,16]{0,1:T(8,128)S(1)} %get-tuple-element.157) | copy-start | bytes 36868
  292.8 149.9 %copy-start.52 = (f32[192]{0:T(256)}, f32[192]{0:T(256)S(1)}, u32[]{:S(2)}) copy-start(f32[192]{0:T(256)S(1)} %get-tuple-element.156) | copy-start | bytes 2308
  442.7 131.1 %copy-start.45 = (f32[192,16]{0,1:T(8,128)S(1)}, f32[192,16]{0,1:T(8,128)}, u32[]{:S(2)}) copy-start(f32[192,16]{0,1:T(8,128)} %copy-done.44) | copy-start | bytes 36868
  442.7 131.1 %copy-start.48 = (pred[192,16]{0,1:T(8,128)(4,1)S(1)}, pred[192,16]{0,1:T(8,128)(4,1)}, u32[]{:S(2)}) copy-start(pred[192,16]{0,1:T(8,128)(4,1)} %fusion.10) | copy-start | bytes 9220
  442.8 131.1 %copy-start.53 = (f32[192]{0:T(256)S(1)}, f32[192]{0:T(256)}, u32[]{:S(2)}) copy-start(f32[192]{0:T(256)} %copy-done.52) | copy-start | bytes 2308
  442.8 131.1 %copy-start.56 = (f32[192]{0:T(256)S(1)}, f32[192]{0:T(256)}, u32[]{:S(2)}) copy-start(f32[192]{0:T(256)} %fusion.12) | copy-start | bytes 2308
  442.8 131.1 %copy-start.15 = (f32[192,2048]{1,0:T(8,128)S(1)}, f32[192,2048]{1,0:T(8,128)}, u32[]{:S(2)}) copy-start(f32[192,2048]{1,0:T(8,128)} %copy-done.14) | copy-start | bytes 4718596
  442.8 131.1 %copy-start.40 = (bf16[2048,16]{0,1:T(8,128)(2,1)S(1)}, bf16[2048,16]{0,1:T(8,128)(2,1)}, u32[]{:S(2)}) copy-start(bf16[2048,16]{0,1:T(8,128)(2,1)} %param.26) | copy-start | bytes 196612
  442.8 131.1 %copy-start.47 = (f32[2048]{0:T(1024)S(1)}, f32[2048]{0:T(1024)}, u32[]{:S(2)}) copy-start(f32[2048]{0:T(1024)} %param.25) | copy-start | bytes 24580
  442.8 131.1 %copy-start.55 = (f32[192]{0:T(256)S(1)}, f32[192]{0:T(256)}, u32[]{:S(2)}) copy-start(f32[192]{0:T(256)} %copy-done.54) | copy-start | bytes 2308
  741.5 7.4 copy-start.21
  750.3 122.9 %copy-start.18 = (bf16[192,2048]{1,0:T(8,128)(2,1)S(1)}, bf16[192,2048]{1,0:T(8,128)(2,1)}, u32[]{:S(2)}) copy-start(bf16[192,2048]{1,0:T(8,128)(2,1)} %src.1) | copy-start | bytes 2359300
  869.7 7.7 copy-start.16
  873.1 6.6 copy-start.34
  (34 other events, 122.8 us)
Sparse Core Ops, SparseCore 0:
  10.9 232.4 all-gather.1

commit v5 on v4

--- a/solution.py
+++ b/solution.py
@@ -433,10 +433,11 @@
 class Spread:
     ZU, ZD, XF, YF, XH, YH, CO, CX, CY, CA, CB = range(11)
 
-    def __init__(self, place, src, whole, sent, got, kept):
+    def __init__(self, place, src, whole, sent, got, kept, split=None):
         self.place, self.src, self.whole, self.sent, self.got = place, src, whole, sent, got
-        half = src.shape[0] // 2
-        self.low, self.high = pl.ds(0, half), pl.ds(half, half)
+        rows = src.shape[0]
+        split = rows // 2 if split is None else split
+        self.low, self.high = pl.ds(0, split), pl.ds(split, rows - split)
         z, x, c, y = place.z, place.x, place.c, place.y
         self.up, self.down = place.device(z=z + 1), place.device(z=z - 1)
         self.over_x, self.over_y = place.device(x=1 - x), place.device(y=1 - y)
@@ -462,7 +463,7 @@
         ref = self.whole.at[zz, xx, self.place.c, yy, rows]
         pltpu.make_async_copy(ref, ref, self.sent.at[kind, zz]).wait()
 
-    def spread_own(self, zz, origin=None):
+    def column(self, zz, origin=None):
         x, y, every = self.place.x, self.place.y, slice(None)
         self.push(self.XF, zz, x, y, every, self.over_x, origin)
         self.push(self.YF, zz, x, y, every, self.over_y, origin)
@@ -479,7 +480,7 @@
         def _():
             self.push(self.ZD, z, x, y, slice(None), self.down, self.src)
 
-        self.spread_own(z, self.src)
+        self.column(z, self.src)
         self.keep.start()
 
     def along_z(self, d):
@@ -494,8 +495,6 @@
             def _():
                 self.push(self.ZU, below, x, y, slice(None), self.up)
 
-            self.spread_own(below)
-
         @pl.when(above < nz)
         def _():
             self.arrival(self.ZD, above, x, y)
@@ -503,8 +502,6 @@
             @pl.when(z > 0)
             def _():
                 self.push(self.ZD, above, x, y, slice(None), self.down)
-
-            self.spread_own(above)
 
     def relay(self, zz):
         x, y, every = self.place.x, self.place.y, slice(None)
@@ -697,66 +694,79 @@
     ]
 
 
-def scatter_kernel(parts, out, *scratch):
+def scatter_kernel(parts, *refs):
+    streams, refs = refs[:5], refs[5:]
+    out, wg_grad, wu_grad, wd_grad = refs[:4]
+    tiles, tile_sems, scratch = refs[4:9], refs[9], refs[10:]
     place = Place()
+    nz = place.z_count
     fold = Fold(place, parts, *scratch)
+    count = streams[0].shape[0]
     place.meet()
     fold.begin()
-    for step in (fold.halves, fold.columns, fold.along_z):
-        for i in range(place.z_count):
-            step(i)
+
+    def loads(t, slot):
+        return [
+            pltpu.make_async_copy(stream.at[t], tile.at[slot], tile_sems.at[slot, n])
+            for n, (stream, tile) in enumerate(zip(streams, tiles))
+        ]
+
+    def tile_step(t, carry):
+        slot = t % 2
+        for copy in loads(t, slot):
+            copy.wait()
+
+        @pl.when(t + 1 < count)
+        def _():
+            for copy in loads(t + 1, 1 - slot):
+                copy.start()
+
+        x_tile, g_tile, hidden, gate_pre_grad, up_grad = (tile[slot] for tile in tiles)
+        wg_grad[...] += dot_tn(x_tile, gate_pre_grad)
+        wu_grad[...] += dot_tn(x_tile, up_grad)
+        wd_grad[...] += dot_tn(hidden, g_tile)
+        return carry
+
+    for copy in loads(0, 0):
+        copy.start()
+    for grad in (wg_grad, wu_grad, wd_grad):
+        grad[...] = jnp.zeros_like(grad)
+    for i in range(nz):
+        fold.halves(i)
+    steps = [functools.partial(fold.columns, i) for i in range(nz)]
+    steps += [functools.partial(fold.along_z, i) for i in range(nz)]
+    done = 0
+    for n, step in enumerate(steps):
+        share = (n + 1) / (2 * nz) if n < nz else 0.5 + (n - nz + 1) / (2 * nz)
+        until = min(count, round(count * share))
+        lax.fori_loop(done, until, tile_step, 0)
+        done = until
+        step()
     out[...] = fold.result()
     fold.finish()
 
 
-def scatter_sum(parts, collective):
+def scatter_sum(parts, streams, collective):
     nz, _, _, _, rows, cols = parts.shape
     dt = parts.dtype
+    width, units = streams[0].shape[1], streams[2].shape[1]
+    tile = 256 if streams[0].shape[0] % 256 == 0 else GROUP // 2
+    streams = [stream.reshape(-1, tile, stream.shape[1]) for stream in streams]
+    shapes = [(width, units), (width, units), (units, width)]
     return pl.pallas_call(
         scatter_kernel,
-        out_shape=jax.ShapeDtypeStruct((rows, cols), dt),
-        in_specs=[ANYWHERE],
-        out_specs=IN_VMEM,
-        scratch_shapes=fold_scratch(nz, rows, cols, rows // 2, dt),
+        out_shape=[jax.ShapeDtypeStruct((rows, cols), dt)]
+        + [jax.ShapeDtypeStruct(shape, jnp.float32) for shape in shapes],
+        in_specs=[ANYWHERE] * 6,
+        out_specs=[IN_VMEM] * 4,
+        scratch_shapes=[pltpu.VMEM((2,) + stream.shape[1:], stream.dtype) for stream in streams]
+        + [pltpu.SemaphoreType.DMA((2, 5))]
+        + fold_scratch(nz, rows, cols, rows // 2, dt),
         cost_estimate=LINK_TIME,
         compiler_params=pltpu.CompilerParams(
-            collective_id=collective, has_side_effects=True, vmem_limit_bytes=58 << 20
+            collective_id=collective, has_side_effects=True, vmem_limit_bytes=62 << 20
         ),
-    )(parts)
-
-
-def swap_kernel(src, out, sent, got):
-    dp, y = lax.axis_index("dp"), lax.axis_index("tensor")
-    other = (dp, 1 - y)
-    barrier = pltpu.get_barrier_semaphore()
-    pl.semaphore_signal(barrier, inc=1, device_id=other, device_id_type=MESH_ID)
-    pl.semaphore_wait(barrier, 1)
-    send(src, out, sent, got, other).wait()
-
-
-def swap_tensor(block, collective):
-    return pl.pallas_call(
-        swap_kernel,
-        out_shape=jax.ShapeDtypeStruct(block.shape, block.dtype),
-        in_specs=[ANYWHERE],
-        out_specs=ANYWHERE,
-        scratch_shapes=[pltpu.SemaphoreType.DMA, pltpu.SemaphoreType.DMA],
-        compiler_params=pltpu.CompilerParams(collective_id=collective, has_side_effects=True),
-    )(block)
-
-
-def both_rows(block, collective):
-    other = swap_tensor(block, collective)
-    first = lax.axis_index("tensor") == 0
-    return jnp.concatenate([jnp.where(first, block, other), jnp.where(first, other, block)], axis=0)
-
-
-def own_rows_sum(part, collective):
-    rows = part.shape[0] // 2
-    index = lax.axis_index("tensor")
-    other = lax.dynamic_slice_in_dim(part, (1 - index) * rows, rows, 0).astype(jnp.bfloat16)
-    mine = lax.dynamic_slice_in_dim(part, index * rows, rows, 0)
-    return mine + swap_tensor(other, collective).astype(jnp.float32)
+    )(parts, *streams)
 
 
 def turn(values):
@@ -776,8 +786,71 @@
 
 
 def attend_kernel(
-    queries, keys, values, q_inv, k_inv, q_gain, k_gain, cosine, sine, q_rot, k_rot, mixed, log_total
+    src,
+    normed,
+    w_query,
+    w_key,
+    w_value,
+    w_out,
+    q_gain,
+    k_gain,
+    cosine,
+    sine,
+    whole,
+    queries,
+    keys,
+    values,
+    q_rot,
+    k_rot,
+    mixed,
+    q_inv,
+    k_inv,
+    log_total,
+    attended,
+    stats,
+    stats_got,
+    leaving,
+    landed,
+    swap_sems,
+    sent,
+    got,
+    kept,
 ):
+    place = Place()
+    nz = place.z_count
+    rows = leaving.shape[0]
+    spread = Spread(place, src, whole, sent, got, kept, src.shape[0] // 3)
+    place.meet()
+    over_y = place.device(y=1 - place.y)
+    spread.begin()
+
+    def near(k):
+        return place.far_first(nz - 1 - k)
+
+    lane = lax.broadcasted_iota(jnp.int32, stats.shape, 1)
+    stats[...] = jnp.zeros_like(stats)
+    chunk = 2 * HEAD
+
+    def project(i, carry):
+        here = pl.ds(pl.multiple_of(i * chunk, chunk), chunk)
+        for index, (weight, raw) in enumerate(((w_query, queries), (w_key, keys))):
+            product = dot_nn(normed[...], weight[:, here])
+            raw[:, here] = product
+            squares = jnp.sum(product * product, axis=1, keepdims=True)
+            stats[...] += jnp.where(lane == index, squares, 0.0)
+        values[:, here] = dot_nn(normed[...], w_value[:, here]).astype(jnp.bfloat16)
+        return carry
+
+    lax.fori_loop(0, queries.shape[1] // chunk, project, 0)
+    stats_swap = send(stats, stats_got, swap_sems.at[0, 0], swap_sems.at[1, 0], over_y)
+    if nz > 1:
+        spread.along_z(1)
+        spread.column(near(1))
+    spread.relay(near(0))
+    stats_swap.wait()
+    for index, inv in enumerate((q_inv, k_inv)):
+        total = stats[:, index : index + 1] + stats_got[:, index : index + 1]
+        inv[...] = lax.rsqrt(total / D + EPSILON)
     visible = seen_keys()
 
     def head(h, carry):
@@ -795,28 +868,91 @@
         mixed[:, here] = dot_nn(weights, values[:, here]).astype(jnp.bfloat16)
         return carry
 
-    lax.fori_loop(0, queries.shape[1] // HEAD, head, 0)
-
-
-def attend(queries, keys, values, q_inv, k_inv, q_gain, k_gain, tables):
-    rows, cols = queries.shape
-    half = jax.ShapeDtypeStruct((rows, cols), jnp.bfloat16)
+    heads = queries.shape[1] // HEAD
+    lax.fori_loop(0, heads // 2, head, 0)
+    if nz > 2:
+        spread.along_z(2)
+        spread.column(near(2))
+    lax.fori_loop(heads // 2, heads, head, 0)
+
+    def joined(target, index):
+        where = pl.ds(pl.multiple_of(index * rows, rows), rows)
+
+        def columns(b, carry):
+            here = pl.ds(pl.multiple_of(b * w_out.shape[2], w_out.shape[2]), w_out.shape[2])
+            target[:, here] = dot_nn(mixed[where], w_out[b]).astype(target.dtype)
+            return carry
+
+        lax.fori_loop(0, w_out.shape[0], columns, 0)
+
+    joined(leaving, 1 - place.y)
+    swap = send(leaving, landed, swap_sems.at[0, 1], swap_sems.at[1, 1], over_y)
+    if nz > 1:
+        spread.relay(near(1))
+    joined(attended, place.y)
+    for d in range(3, nz):
+        spread.along_z(d)
+        spread.column(near(d))
+    spread.diagonal(near(0))
+    for k in range(2, nz):
+        spread.relay(near(k))
+        spread.diagonal(near(k - 1))
+    if nz > 1:
+        spread.diagonal(near(nz - 1))
+    swap.wait()
+    attended[...] += landed[...].astype(jnp.float32)
+    spread.keep.wait()
+    for zz in range(nz):
+        spread.sibling_near(zz)
+        spread.sibling_far(zz)
+    spread.finish()
+
+
+def attend(block, normed, weights, gains, tables, collective):
+    nz = lax.axis_size("dp") // 4
+    rows, width = block.shape
+    group, cols = normed.shape[0], weights[0].shape[1]
+    half = jax.ShapeDtypeStruct((group, cols), jnp.bfloat16)
+    wide = jax.ShapeDtypeStruct((group, cols), jnp.float32)
+    thin = jax.ShapeDtypeStruct((group, 1), jnp.float32)
     return pl.pallas_call(
         attend_kernel,
-        out_shape=[half, half, half, jax.ShapeDtypeStruct((cols // HEAD, rows, 1), jnp.float32)],
-        in_specs=[IN_VMEM] * 9,
-        out_specs=[IN_VMEM] * 4,
-        cost_estimate=pl.CostEstimate(
-            flops=4 * rows * rows * cols, bytes_accessed=16 * rows * cols, transcendentals=rows * rows * 8
+        out_shape=[
+            jax.ShapeDtypeStruct((nz, 2, 2, 2, rows, width), block.dtype),
+            wide,
+            wide,
+            half,
+            half,
+            half,
+            half,
+            thin,
+            thin,
+            jax.ShapeDtypeStruct((cols // HEAD, group, 1), jnp.float32),
+            jax.ShapeDtypeStruct((rows, width), jnp.float32),
+        ],
+        in_specs=[ANYWHERE] + [IN_VMEM] * 9,
+        out_specs=[ANYWHERE] + [IN_VMEM] * 10,
+        scratch_shapes=[
+            pltpu.VMEM((group, LANES), jnp.float32),
+            pltpu.VMEM((group, LANES), jnp.float32),
+            pltpu.VMEM((rows, width), jnp.bfloat16),
+            pltpu.VMEM((rows, width), jnp.bfloat16),
+            pltpu.SemaphoreType.DMA((2, 2)),
+            pltpu.SemaphoreType.DMA((11, nz)),
+            pltpu.SemaphoreType.DMA((11, nz)),
+            pltpu.SemaphoreType.DMA,
+        ],
+        cost_estimate=LINK_TIME,
+        compiler_params=pltpu.CompilerParams(
+            collective_id=collective, has_side_effects=True, vmem_limit_bytes=60 << 20
         ),
-        compiler_params=pltpu.CompilerParams(vmem_limit_bytes=40 << 20),
-    )(queries, keys, values, q_inv, k_inv, q_gain, k_gain, *tables)
+    )(block, normed, *weights, *gains, *tables)
 
 
 def attend_back_kernel(
     parts,
     own_grad,
-    o_all,
+    w_out,
     queries,
     keys,
     q_rot,
@@ -856,7 +992,15 @@
     def take(block, index):
         where = pl.ds(pl.multiple_of(index * rows, rows), rows)
         attended_grad[where] = block[...]
-        mixed_grad[where] = dot_nt(block[...], o_all[...]).astype(jnp.bfloat16)
+        step = w_out.shape[2]
+
+        def columns(b, total):
+            here = pl.ds(pl.multiple_of(b * step, step), step)
+            return total + dot_nt(block[:, here], w_out[b])
+
+        total = jnp.zeros((rows, mixed_grad.shape[1]), jnp.float32)
+        total = lax.fori_loop(0, w_out.shape[0], columns, total)
+        mixed_grad[where] = total.astype(jnp.bfloat16)
 
     take(own_grad, place.y)
     for i in range(nz):
@@ -918,7 +1062,7 @@
     fold.finish()
 
 
-def attend_back(parts, own_grad, o_all, saved, gains, tables, collective):
+def attend_back(parts, own_grad, w_out, saved, gains, tables, collective):
     nz, _, _, _, rows, cols = parts.shape
     queries = saved[0]
     group, head_cols = queries.shape
@@ -951,19 +1095,21 @@
         compiler_params=pltpu.CompilerParams(
             collective_id=collective, has_side_effects=True, vmem_limit_bytes=62 << 20
         ),
-    )(parts, own_grad, o_all, *saved, *gains, *tables)
+    )(parts, own_grad, w_out, *saved, *gains, *tables)
 
 
 def plane_gather_kernel(count, *refs):
-    srcs, outs = refs[:count], refs[count : 2 * count]
-    sent, got, kept = refs[2 * count :]
+    srcs, block = refs[:count], refs[count]
+    outs, landed = refs[count + 1 : 2 * count + 1], refs[2 * count + 1]
+    sent, got, kept, swap_sems = refs[2 * count + 2 :]
     place = Place()
     z, x, c, nz = place.z, place.x, place.c, place.z_count
     ZU, ZD, XF, CO, CX = range(5)
     up, down = place.device(z=z + 1), place.device(z=z - 1)
     over_x, over_c = place.device(x=1 - x), place.device(c=1 - c)
-    place.meet(use_y=False)
+    place.meet()
     every = range(count)
+    swap = send(block, landed, swap_sems.at[0], swap_sems.at[1], place.device(y=1 - place.y))
 
     def push(a, kind, zz, xx, device, own=False):
         ref = outs[a].at[zz, xx, c]
@@ -1054,34 +1200,36 @@
             def _():
                 departure(a, ZD, zz, x)
 
-
-def gather_in_plane(shards, collective):
+    swap.wait()
+
+
+def gather_in_plane(shards, block, collective):
     nz = lax.axis_size("dp") // 4
     count = len(shards)
     return pl.pallas_call(
         functools.partial(plane_gather_kernel, count),
-        out_shape=[jax.ShapeDtypeStruct((nz, 2, 2) + s.shape, s.dtype) for s in shards],
-        in_specs=[ANYWHERE] * count,
-        out_specs=[ANYWHERE] * count,
+        out_shape=[jax.ShapeDtypeStruct((nz, 2, 2) + s.shape, s.dtype) for s in shards]
+        + [jax.ShapeDtypeStruct(block.shape, block.dtype)],
+        in_specs=[ANYWHERE] * (count + 1),
+        out_specs=[ANYWHERE] * (count + 1),
         scratch_shapes=[
             pltpu.SemaphoreType.DMA((5, count, nz)),
             pltpu.SemaphoreType.DMA((5, count, nz)),
             pltpu.SemaphoreType.DMA((count,)),
+            pltpu.SemaphoreType.DMA((2,)),
         ],
         cost_estimate=LINK_TIME,
         compiler_params=pltpu.CompilerParams(collective_id=collective, has_side_effects=True),
-    )(*shards)
+    )(*shards, block)
 
 
 def plane_scatter_kernel(count, *refs):
-    parts, small, row_part = refs[:count], refs[count], refs[count + 1]
-    streams = refs[count + 2 : count + 7]
-    refs = refs[count + 7 :]
+    lefts, rights = refs[:count], refs[count : 2 * count]
+    small, row_part = refs[2 * count : 2 * count + 2]
+    refs = refs[2 * count + 2 :]
     outs, small_out, row_landed = refs[:count], refs[count], refs[count + 1]
-    wg_grad, wu_grad, wd_grad = refs[count + 2 : count + 5]
-    total, from_c, full_x, z_buf, small_sum, small_got = refs[count + 5 : count + 11]
-    tiles = refs[count + 11 : count + 16]
-    sent, got, loaded, small_sems, row_sems, tile_sems = refs[count + 16 :]
+    total, leaving, from_c, full_x, z_buf, small_sum, small_got = refs[count + 2 : count + 9]
+    sent, got, small_sems, row_sems = refs[count + 9 :]
     place = Place()
     z, x, c, nz = place.z, place.x, place.c, place.z_count
     rows = total.shape[3]
@@ -1126,57 +1274,35 @@
             result = result + jnp.where(away == 0, small_sum[3], small_got[jnp.maximum(2 + away, 3)])
         small_out[...] = result
 
-    count_tiles = streams[0].shape[0]
-
-    def tile_loads(t, slot):
-        return [
-            pltpu.make_async_copy(stream.at[t], tile.at[slot], tile_sems.at[slot, n])
-            for n, (stream, tile) in enumerate(zip(streams, tiles))
-        ]
-
-    def tile_step(t, carry):
-        slot = t % 2
-        for copy in tile_loads(t, slot):
-            copy.wait()
-
-        @pl.when(t + 1 < count_tiles)
-        def _():
-            for copy in tile_loads(t + 1, 1 - slot):
-                copy.start()
-
-        x_tile, g_tile, hidden, gate_pre_grad, up_grad = (tile[slot] for tile in tiles)
-        wg_grad[...] += dot_tn(x_tile, gate_pre_grad)
-        wu_grad[...] += dot_tn(x_tile, up_grad)
-        wd_grad[...] += dot_tn(hidden, g_tile)
-        return carry
-
     def arrival(a, kind, zz, ref):
         pltpu.make_async_copy(ref, ref, got.at[kind, a, zz]).wait()
 
     small_copy = small_start(0)
-    for dx, kind in ((1, C1), (0, C0)):
-        for i in range(nz):
-            zz = place.far_first(i)
-            xx = 1 - x if dx else x
-            for a in range(count):
-                send(
-                    parts[a].at[zz, xx, 1 - c],
-                    from_c.at[dx, zz, a],
-                    sent.at[kind, a, zz],
-                    got.at[kind, a, zz],
-                    over_c,
-                )
-                pltpu.make_async_copy(
-                    parts[a].at[zz, xx, c], total.at[dx, zz, a], loaded.at[dx, a, zz]
-                ).start()
-    for copy in tile_loads(0, 0):
-        copy.start()
+
+    def make(dx, i):
+        zz = place.far_first(i)
+        xx = 1 - x if dx else x
+        for a in range(count):
+
+            def product(cc):
+                shard = (zz * 2 + xx) * 2 + cc
+                here = pl.ds(pl.multiple_of(shard * rows, rows), rows)
+                return dot_tn(lefts[a][:, here], rights[a][...]).astype(total.dtype)
+
+            leaving[dx, zz, a] = product(1 - c)
+            send(
+                leaving.at[dx, zz, a],
+                from_c.at[dx, zz, a],
+                sent.at[C1 if dx else C0, a, zz],
+                got.at[C1 if dx else C0, a, zz],
+                over_c,
+            )
+            total[dx, zz, a] = product(c)
 
     def join_cores(a, dx, zz):
-        here, there = total.at[dx, zz, a], from_c.at[dx, zz, a]
-        pltpu.make_async_copy(here, here, loaded.at[dx, a, zz]).wait()
+        there = from_c.at[dx, zz, a]
         arrival(a, C1 if dx else C0, zz, there)
-        add_rows(here, there, rows)
+        add_rows(total.at[dx, zz, a], there, rows)
 
     def over_the_x(i):
         zz = place.far_first(i)
@@ -1224,25 +1350,29 @@
                     place.device(z=z - 1),
                 )
 
+    make(1, 0)
+    row_copy = send(row_part, row_landed, row_sems.at[0], row_sems.at[1], over_y)
     small_end(0, small_copy)
-    over_the_x(0)
     small_copy = small_start(1)
-    small_end(1, small_copy)
-    small_copy = small_start(2)
-    row_copy = send(row_part, row_landed, row_sems.at[0], row_sems.at[1], over_y)
-    wg_grad[...] = jnp.zeros_like(wg_grad)
-    wu_grad[...] = jnp.zeros_like(wu_grad)
-    wd_grad[...] = jnp.zeros_like(wd_grad)
-    for i in range(1, nz - 1):
-        over_the_x(i)
+    for i in range(1, nz):
+        make(1, i)
+        over_the_x(i - 1)
+        if i == 1:
+            small_end(1, small_copy)
+            small_copy = small_start(2)
+    over_the_x(nz - 1)
+
+    def own_chips(i, carry):
+        make(0, i)
+        return carry
+
+    lax.fori_loop(0, nz, own_chips, 0)
     small_end(2, small_copy)
     small_copies = small_z_start()
-    over_the_x(nz - 1)
     for i in range(nz):
-        lax.fori_loop(count_tiles * i // nz, count_tiles * (i + 1) // nz, tile_step, 0)
+        along_z(i)
         if i == 0:
             small_z_end(small_copies)
-        along_z(i)
     row_copy.wait()
 
     for a in range(count):
@@ -1273,47 +1403,39 @@
                 departure(a, ZD, zz)
 
 
-def scatter_in_plane(parts, small, row_part, streams, collective):
-    nz, _, _, rows, cols = parts[0].shape
-    count = len(parts)
-    dt = parts[0].dtype
-    width, units = streams[0].shape[1], streams[2].shape[1]
-    tile = 256 if streams[0].shape[0] % 256 == 0 else GROUP // 2
-    streams = [stream.reshape(-1, tile, stream.shape[1]) for stream in streams]
+def scatter_in_plane(lefts, rights, small, row_part, collective):
+    count = len(lefts)
+    nz = lax.axis_size("dp") // 4
+    cols, dt = rights[0].shape[1], rights[0].dtype
+    rows = lefts[0].shape[1] // (4 * nz)
+    blocks = pltpu.VMEM((2, nz, count, rows, cols), dt)
     return pl.pallas_call(
         functools.partial(plane_scatter_kernel, count),
         out_shape=[jax.ShapeDtypeStruct((rows, cols), jnp.float32)] * count
         + [
             jax.ShapeDtypeStruct(small.shape, small.dtype),
             jax.ShapeDtypeStruct(row_part.shape, row_part.dtype),
-            jax.ShapeDtypeStruct((width, units), jnp.float32),
-            jax.ShapeDtypeStruct((width, units), jnp.float32),
-            jax.ShapeDtypeStruct((units, width), jnp.float32),
         ],
-        in_specs=[ANYWHERE] * count + [IN_VMEM] + [ANYWHERE] * 6,
-        out_specs=[IN_VMEM] * (count + 1) + [ANYWHERE] + [IN_VMEM] * 3,
+        in_specs=[IN_VMEM] * (2 * count + 1) + [ANYWHERE],
+        out_specs=[IN_VMEM] * (count + 1) + [ANYWHERE],
         scratch_shapes=[
-            pltpu.VMEM((2, nz, count, rows, cols), dt),
-            pltpu.VMEM((2, nz, count, rows, cols), dt),
+            blocks,
+            blocks,
+            blocks,
             pltpu.VMEM((nz, count, rows, cols), dt),
             pltpu.VMEM((nz + 1, count, rows, cols), dt),
             pltpu.VMEM((4,) + small.shape, small.dtype),
             pltpu.VMEM((2 + nz,) + small.shape, small.dtype),
-        ]
-        + [pltpu.VMEM((2,) + stream.shape[1:], stream.dtype) for stream in streams]
-        + [
             pltpu.SemaphoreType.DMA((5, count, nz)),
             pltpu.SemaphoreType.DMA((5, count, nz)),
-            pltpu.SemaphoreType.DMA((2, count, nz)),
             pltpu.SemaphoreType.DMA((2, 2 + nz)),
             pltpu.SemaphoreType.DMA((2,)),
-            pltpu.SemaphoreType.DMA((2, 5)),
         ],
         cost_estimate=LINK_TIME,
         compiler_params=pltpu.CompilerParams(
             collective_id=collective, has_side_effects=True, vmem_limit_bytes=62 << 20
         ),
-    )(*parts, small, row_part, *streams)
+    )(*lefts, *rights, small, row_part)
 
 
 def dot_nn(a, b):
@@ -1413,14 +1535,13 @@
             for n, (here, there) in enumerate(stores)
         ]
 
-    z_done, steps = 0, {}
+    steps = {}
     for position, (k, dx) in enumerate(pairs):
         todo = []
         if dx == 0:
+            if k + 1 < z_count:
+                todo += [("z", k + 1), ("column", k + 1)]
             todo.append(("relay", k))
-            while z_done < min(k + 1, z_count - 1):
-                z_done += 1
-                todo.insert(0, ("z", z_done))
         else:
             todo.append(("diagonal", k))
         steps[2 * position] = todo
@@ -1436,6 +1557,8 @@
                     for kind, number in steps[position]:
                         if kind == "z":
                             spread.along_z(number)
+                        elif kind == "column":
+                            spread.column(near(number))
                         elif kind == "relay":
                             spread.relay(near(number))
                         else:
@@ -1461,12 +1584,13 @@
                 copy.wait()
 
         zz, xx, cc = tile_at(i)
-        first_row = pl.multiple_of(((zz * 2 + xx) * 2 + cc) * tile, tile)
         rows = x_tile[slot]
         logits = jnp.where(lanes_ref[1:2] > 0.0, dot_nn(rows, router_ref[...]), -1e30)
         weights = jnp.exp(logits - jnp.max(logits, axis=1, keepdims=True))
         own_weight = jnp.sum(weights * lanes_ref[0:1], axis=1, keepdims=True)
-        gate = hot_ref[pl.ds(first_row, tile)] * own_weight / jnp.sum(weights, axis=1, keepdims=True)
+        named = jnp.transpose(hot_ref[(zz * 2 + xx) * 2 + cc].astype(jnp.float32))
+        hot = jnp.sum(named * lanes_ref[0:1, : named.shape[1]], axis=1, keepdims=True)
+        gate = hot * own_weight / jnp.sum(weights, axis=1, keepdims=True)
         gate_pre = dot_nn(rows, wg_ref[...])
         up_pre = dot_nn(rows, wu_ref[...])
         raw_grad = dot_nt(g_tile[slot], wd_ref[...])
@@ -1570,21 +1694,25 @@
     experts = router.shape[1]
     q_gain_local = lax.dynamic_slice_in_dim(q_gain, col_start, head_cols)
     k_gain_local = lax.dynamic_slice_in_dim(k_gain, col_start, head_cols)
-    inputs_both = both_rows(tokens, 5).astype(jnp.float32)
+    expert_ids = jnp.arange(experts, dtype=jnp.int32)
+    named = jnp.any(routes[None] == expert_ids[:, None, None], axis=2).astype(jnp.bfloat16)
+    q_all, k_all, v_all, o_all, hot, other_tokens = gather_in_plane(
+        (w_query, w_key, w_value, w_out, named), tokens, 1
+    )
+    hot = hot.reshape(-1, *named.shape)
+    q_all, k_all, v_all = (w.reshape(D, head_cols) for w in (q_all, k_all, v_all))
+    o_all = o_all.reshape(-1, *w_out.shape)
+    first = rank_index == 0
+    inputs_both = jnp.concatenate(
+        [jnp.where(first, tokens, other_tokens), jnp.where(first, other_tokens, tokens)], axis=0
+    ).astype(jnp.float32)
     unit_both = inputs_both * lax.rsqrt(
         jnp.mean(inputs_both * inputs_both, axis=1, keepdims=True) + EPSILON
     )
     normed = (unit_both * attn_gain).astype(jnp.bfloat16)
     inputs = tokens.astype(jnp.float32)
     attn_inv = lax.rsqrt(jnp.mean(inputs * inputs, axis=1, keepdims=True) + EPSILON)
-    q_all, k_all, v_all, o_all, routes_all = gather_in_plane(
-        (w_query, w_key, w_value, w_out, routes), 1
-    )
-    q_all, k_all, v_all = (w.reshape(D, head_cols) for w in (q_all, k_all, v_all))
-    o_all = jnp.transpose(o_all.reshape(-1, *w_out.shape), (1, 0, 2)).reshape(head_cols, D)
-    routes_all = routes_all.reshape(-1, TOPK)
     own_expert = lax.axis_index("dp")
-    hot = jnp.any(routes_all == own_expert, axis=1, keepdims=True).astype(jnp.float32)
     lane = jnp.arange(LANES)
     marked = own_expert + experts * rank_index
     lanes = jnp.stack(
@@ -1592,27 +1720,26 @@
         + [lane < 0] * 4
     ).astype(jnp.float32)
     router_wide = jnp.pad(router, ((0, 0), (0, LANES - experts)))
-    upstream_all = lax.all_gather(cotangent, EVERY, axis=0, tiled=True)
-    queries = matmul(normed, q_all)
-    keys_raw = matmul(normed, k_all)
-    values_raw = matmul(normed, v_all)
-    query_sq, key_sq = tensor_total(
-        (jnp.sum(queries * queries, axis=1), jnp.sum(keys_raw * keys_raw, axis=1))
-    )
-    query_inv = lax.rsqrt(query_sq / D + EPSILON)[:, None]
-    key_inv = lax.rsqrt(key_sq / D + EPSILON)[:, None]
     tables = signed_rope_tables()
-    values = values_raw.astype(jnp.bfloat16)
     gains = (q_gain_local[None], k_gain_local[None])
-    query_rot, key_rot, mixed_heads, log_total = attend(
-        queries, keys_raw, values, query_inv, key_inv, *gains, tables
-    )
-    attended = own_rows_sum(matmul(mixed_heads, o_all), 6)
+    (
+        upstream_all,
+        queries,
+        keys_raw,
+        values,
+        query_rot,
+        key_rot,
+        mixed_heads,
+        query_inv,
+        key_inv,
+        log_total,
+        attended,
+    ) = attend(cotangent, normed, (q_all, k_all, v_all, o_all), gains, tables, 6)
+    upstream_all = upstream_all.reshape(-1, D)
     hidden_one = inputs + attended
     mlp_inv = lax.rsqrt(jnp.mean(hidden_one * hidden_one, axis=1, keepdims=True) + EPSILON)
     normed_two = (hidden_one * mlp_inv * mlp_gain).astype(jnp.bfloat16)
     own_routes = lax.dynamic_slice_in_dim(routes, row_start, own_rows, 0)
-    expert_ids = jnp.arange(experts, dtype=jnp.int32)
     own_hot = jnp.any(own_routes[:, :, None] == expert_ids[None, None, :], axis=1)
     own_probs = jax.nn.softmax(matmul(normed_two, router), axis=1)
     rows_all, y_part, r_part, *for_weights = expert_pass(
@@ -1621,7 +1748,9 @@
     rows_all, y_part = rows_all.reshape(-1, D), y_part.reshape(-1, D)
     for_weights = [array.reshape(rows_all.shape[0], -1) for array in for_weights]
     blocks = (lax.axis_size("dp") // 4, 2, 2, 2, own_rows)
-    returned = scatter_sum(r_part.reshape(*blocks, D + LANES), 3)
+    returned, gate_weight_grad, up_weight_grad, down_weight_grad = scatter_sum(
+        r_part.reshape(*blocks, D + LANES), [rows_all, upstream_all, *for_weights], 3
+    )
     expert_grad = jnp.sum(
         returned[:, D : D + 4 * experts].astype(jnp.float32).reshape(own_rows, 4, experts), axis=1
     )
@@ -1663,23 +1792,16 @@
         ],
         axis=0,
     )
-    shard = (lax.axis_size("dp") // 4, 2, 2, w_query.shape[0], head_cols)
-    products = [
-        dot_tn(first, second).astype(jnp.bfloat16).reshape(shard)
-        for first, second in (
-            (normed, query_grad),
-            (normed, key_grad),
-            (normed, value_grad),
-            (attended_grad, mixed_heads),
-        )
-    ]
     row_part = lax.dynamic_slice_in_dim(
         normed_part, (1 - rank_index) * own_rows, own_rows, 0
     ).astype(jnp.bfloat16)
     own_part = lax.dynamic_slice_in_dim(normed_part, row_start, own_rows, 0)
-    streams = [rows_all, upstream_all, *for_weights]
-    *weight_sums, small_sums, other_part, gate_weight_grad, up_weight_grad, down_weight_grad = (
-        scatter_in_plane(products, small_grads, row_part, streams, 4)
+    *weight_sums, small_sums, other_part = scatter_in_plane(
+        (normed, normed, normed, attended_grad),
+        (query_grad, key_grad, value_grad, mixed_heads),
+        small_grads,
+        row_part,
+        4,
     )
     normed_grad = own_part + other_part.astype(jnp.float32)
     scaled_input = normed_grad * attn_gain

time: 907 us -> 820 us (0.904)
  matrix products: 44.2 us -> 11.7 us
  Pallas kernels: 772 us -> 752 us
  local copies, waits for them, and re-layouts: 45.5 us -> 28 us
  between operations: 15.4 us -> 1.61 us
    pallas_call x1, Pallas kernels: 181 us -> 99.4 us  [gather_in_plane(): pl.pallas_call(functools.partial(plane_gather_kernel, count), out_shape=[...]
    pallas_call x4 -> x2, Pallas kernels: 183 us -> 262 us  [the longest x1 131 us: attend(): pl.pallas_call(attend_kernel, out_shape=[jax.ShapeDtypeStruct((nz, 2, 2,...]
    dot_general x4 -> x0, matrix products: 17.9 us -> none  [dot_tn(): lax.dot_general(a, b, (((0,), (0,)), ((), ())), preferred_element_type=jn...]
    dot_general x5 -> x1, matrix products: 15 us -> 1.46 us  [matmul(): return jnp.dot(first_op, second_op, preferred_element_type=jnp.float32)]
    unnamed x140 -> x88, local copies, waits for them, and re-layouts: 24.4 us -> 18.5 us
  transfers between devices with their start and end apart: 1 -> 0, of which waited for: 0 -> 0; matrix products, arithmetic and copies ran while one was open for 5% -> 0% of each run, Pallas kernels for 26% -> 0%
where the time goes in v5:
time: 820 us; the launch traced here: 813 us
  Pallas kernels  752 us (92%)
  local copies, waits for them, and re-layouts  28 us (3%)
  other arithmetic  19.9 us (2%)
  matrix products  11.7 us (1%)
    pallas_call x1, Pallas kernels, expert_pass(): pl.pallas_call(functools.partial(expert_kernel, nz), in_specs=[ANYWHERE]...  145 us
    pallas_call x1, Pallas kernels, attend_back(): pl.pallas_call(attend_back_kernel, out_shape=[jax.ShapeDtypeStruct((rows,...  133 us
    pallas_call x1, Pallas kernels, attend(): pl.pallas_call(attend_kernel, out_shape=[jax.ShapeDtypeStruct((nz, 2, 2,...  131 us
    pallas_call x1, Pallas kernels, scatter_sum(): pl.pallas_call(scatter_kernel, out_shape=[jax.ShapeDtypeStruct((rows, col...  131 us
    pallas_call x1, Pallas kernels, scatter_in_plane(): pl.pallas_call(functools.partial(plane_scatter_kernel, count), out_shape=...  113 us
    pallas_call x1, Pallas kernels, gather_in_plane(): pl.pallas_call(functools.partial(plane_gather_kernel, count), out_shape=[...  99.4 us
    unnamed x88, local copies, waits for them, and re-layouts  18.5 us

profile of v5, /device:TPU:0, one launch (start us, length us, event | category | flops | bytes accessed | tf_op | source)
XLA Modules:
  0.0 812.9 jit_solution(1226875470963040922)
XLA Ops:
  2.0 99.4 %shard_map.254 = (bf16[4,2,2,128,1024]{4,3,2,1,0:T(8,128)(2,1)}, bf16[4,2,2,128,1024]{4,3,2,1,0:T(8,128)(2,1)}, bf16[4,2,2,128,1024]{4,3,2,1,0:T(8,128)(2,1)}, b...) custom-call(bf16[128,1024]{1,0:T(8,128)(2,1)} %refs_0_.1, ...), custom_call_target="tpu_custom_call" | custom-call | flops 99999997952 | bytes 100000000 | tf_op jit(solution)/shard_map/pallas_call | solution.py:1209
  101.5 1.2 broadcast_select_fusion.1
  104.5 1.6 fusion.2.normed.refs_0_.refs_1_.refs_2_
  107.4 1.5 sine_multiply_fusion
  109.0 131.2 %shard_map.255 = (bf16[4,2,2,2,192,2048]{5,4,3,2,1,0:T(8,128)(2,1)}, f32[384,1024]{1,0:T(8,128)}, f32[384,1024]{1,0:T(8,128)}, bf16[384,1024]{1,0:T(8,128)(2,1)}...) custom-call(bf16[192,2048]{1,0:T(8,128)(2,1)} %src.1, ...), custom_call_target="tpu_custom_call" | custom-call | flops 99999997952 | bytes 100000000 | tf_op jit(solution)/shard_map/pallas_call | solution.py:918
  240.2 1.7 multiply_reduce_fusion.2
  243.1 1.1 multiply_convert_fusion.src
  245.1 0.9 pad.4.router_ref
  246.0 144.6 %shard_map.256 = (bf16[4,2,2,2,192,2048]{5,4,3,2,1,0:T(8,128)(2,1)}, bf16[4,2,2,384,2048]{4,3,2,1,0:T(8,128)(2,1)}, bf16[4,2,2,384,2176]{4,3,2,1,0:T(8,128)(2,1)...) custom-call(bf16[192,2048]{1,0:T(8,128)(2,1)} %multiply_convert_fusi, ...), custom_call_target="tpu_custom_call" | custom-call | flops 99999997952 | bytes 100000000 | tf_op jit(solution)/shard_map/pallas_call | solution.py:1641
  390.6 131.1 %shard_map.257 = (bf16[192,2176]{1,0:T(8,128)(2,1)}, f32[2048,512]{1,0:T(8,128)}, f32[2048,512]{1,0:T(8,128)}, f32[512,2048]{1,0:T(8,128)}) custom-call(bf16[4,2,2,2,192,2176]{5,4,3,2,1,0:T(8,128)(2,1)} %bitcast.61, bf16[24,256,2048]{2,1,0:T(8,128)(2,1)} %bitcast.65, bf16[24,256,2048]{2,1,0:T(8,128)(2,1)} %bitcast.63, bf16[24,256,512]{2,1,0:T(8,128)(2,1)} %bitcast.66, ...), custom_call_target="tpu_custom_call" | custom-call | flops 99999997952 | bytes 100000000 | tf_op jit(solution)/shard_map/pallas_call | solution.py:756
  522.8 1.5 fusion.21
  524.5 1.3 multiply_reduce_fusion
  525.9 1.9 fusion.19
  527.8 132.7 %shard_map.258 = (bf16[192,2048]{1,0:T(8,128)(2,1)}, bf16[384,2048]{1,0:T(8,128)(2,1)}, bf16[384,1024]{1,0:T(8,128)(2,1)}, bf16[384,1024]{1,0:T(8,128)(2,1)}, bf...) custom-call(bf16[4,2,2,2,192,2048]{5,4,3,2,1,0:T(8,128)(2,1)} %bitcast.64, bf16[192,2048]{1,0:T(8,128)(2,1)} %get-tuple-element.152.own_grad, ...), custom_call_target="tpu_custom_call" | custom-call | flops 99999997952 | bytes 100000000 | tf_op jit(solution)/shard_map/pallas_call | solution.py:1072
  660.5 4.4 fusion.23
  665.0 1.8 fusion.22
  667.8 2.3 fusion.3
  670.1 1.7 copy-done.3
  671.7 1.0 dynamic-slice_convert_fusion.refs_9_
  675.1 1.4 concatenate.11.refs_8_
  676.5 112.6 %shard_map.259 = (f32[128,1024]{1,0:T(8,128)}, f32[128,1024]{1,0:T(8,128)}, f32[128,1024]{1,0:T(8,128)}, f32[128,1024]{1,0:T(8,128)}, f32[24,2048]{1,0:T(8,128)}, /*index=5*/bf16[192,2048]{1,0:T(8,128)(2,1)}) custom-call(bf16[384,2048]{1,0:T(8,128)(2,1)} %fusion.2.normed.refs_0_.refs_1_.refs_2_, bf16[384,2048]{1,0:T(8,128)(2,1)} %fusion.2.normed.refs_0_.refs_1_.refs_2_, ...), custom_call_target="tpu_custom_call" | custom-call | flops 99999997952 | bytes 100000000 | tf_op jit(solution)/shard_map/pallas_call | solution.py:1412
  789.1 2.3 fusion.5
  791.7 3.5 fusion.7
  795.2 1.0 copy.43
  796.2 1.6 slice_bitcast_fusion
  797.8 1.6 fusion.20
  799.5 1.1 add_convert_fusion
  803.0 2.1 copy.56
  805.2 1.6 copy-done.13
  806.7 2.1 copy.57
  808.9 1.6 copy-done.12
  810.4 2.0 copy.58
  (113 shorter events, 13.9 us)
Async XLA Ops:
  2.0 99.5 %copy-start.5 = (bf16[192,2048]{1,0:T(8,128)(2,1)S(1)}, bf16[192,2048]{1,0:T(8,128)(2,1)}, u32[]{:S(2)}) copy-start(bf16[192,2048]{1,0:T(8,128)(2,1)} %refs_5_.1) | copy-start | bytes 2359300
  102.8 1.8 copy-start.28
  104.5 2.2 copy-start.37
  240.2 2.9 copy-start.26
  241.9 2.9 copy-start.20
  242.5 1.6 copy-start.33
  390.6 132.2 %copy-start.21 = (bf16[2048,16]{0,1:T(8,128)(2,1)S(1)}, bf16[2048,16]{0,1:T(8,128)(2,1)}, u32[]{:S(2)}) copy-start(bf16[2048,16]{0,1:T(8,128)(2,1)} %param.26) | copy-start | bytes 196612
  390.6 133.7 %copy-start.30 = (s32[384,8]{0,1:T(8,128)S(1)}, s32[384,8]{0,1:T(8,128)}, u32[]{:S(2)}) copy-start(s32[384,8]{0,1:T(8,128)} %param.16) | copy-start | bytes 36868
  390.6 133.8 %copy-start.1 = (f32[192,2048]{1,0:T(8,128)S(1)}, f32[192,2048]{1,0:T(8,128)}, u32[]{:S(2)}) copy-start(f32[192,2048]{1,0:T(8,128)} %copy-done) | copy-start | bytes 4718596
  390.6 133.8 %copy-start.27 = (f32[2048]{0:T(1024)S(1)}, f32[2048]{0:T(1024)}, u32[]{:S(2)}) copy-start(f32[2048]{0:T(1024)} %param.25) | copy-start | bytes 24580
  390.6 133.8 %copy-start.34 = (f32[192]{0:T(256)S(1)}, f32[192]{0:T(256)}, u32[]{:S(2)}) copy-start(f32[192]{0:T(256)} %copy-done.33) | copy-start | bytes 2308
  521.8 2.7 copy-start.16
  660.5 4.4 copy-start.38
  660.5 4.4 copy-start.39
  664.9 1.9 copy-start.8
  664.9 1.9 copy-start.10
  665.0 2.7 copy-start.15
  665.0 2.8 copy-start.19
  665.0 2.8 copy-start.32
  670.0 1.7 copy-start.3
  676.5 112.6 %copy-start.6 = (bf16[192,2048]{1,0:T(8,128)(2,1)S(1)}, bf16[192,2048]{1,0:T(8,128)(2,1)}, u32[]{:S(2)}) copy-start(bf16[192,2048]{1,0:T(8,128)(2,1)} %refs_5_.1) | copy-start | bytes 2359300
  676.5 112.6 %copy-start.29 = (f32[2048]{0:T(1024)S(1)}, f32[2048]{0:T(1024)}, u32[]{:S(2)}) copy-start(f32[2048]{0:T(1024)} %param.18) | copy-start | bytes 24580
  789.1 2.6 copy-start.4
  791.7 3.5 copy-start.25
  791.7 7.7 copy-start.2
  795.2 4.2 copy-start.18
  795.2 5.3 copy-start.24
  796.2 5.1 copy-start.23
  799.4 3.6 copy-start.14
  800.5 1.7 copy-start.22
  803.0 3.7 copy-start.13
  806.7 3.7 copy-start.12
  (8 other events, 9.5 us)

commit v6 on v5

--- a/solution.py
+++ b/solution.py
@@ -413,6 +413,10 @@
         return jnp.where(self.z * 2 < self.z_count, low, high)
 
 
+    def near_first(self, step):
+        return self.far_first(self.z_count - 1 - step)
+
+
 def send(src, dst, send_sem, recv_sem, device):
     copy = pltpu.make_async_remote_copy(
         src_ref=src, dst_ref=dst, send_sem=send_sem, recv_sem=recv_sem, device_id=device, device_id_type=MESH_ID
@@ -431,13 +435,17 @@
 
 
 class Spread:
-    ZU, ZD, XF, YF, XH, YH, CO, CX, CY, CA, CB = range(11)
-
-    def __init__(self, place, src, whole, sent, got, kept, split=None):
+    KINDS = 14
+    ZU, ZD, XF, YF, XH, YH, CO, CX, CY, CA, CB, CC, DU, DD = range(KINDS)
+
+    def __init__(self, place, src, whole, sent, got, kept, own_split, through_z, other_split):
         self.place, self.src, self.whole, self.sent, self.got = place, src, whole, sent, got
         rows = src.shape[0]
-        split = rows // 2 if split is None else split
-        self.low, self.high = pl.ds(0, split), pl.ds(split, rows - split)
+        self.parts = {
+            True: (pl.ds(0, own_split), pl.ds(own_split, rows - own_split)),
+            False: (pl.ds(through_z, other_split), pl.ds(through_z + other_split, rows - through_z - other_split)),
+        }
+        self.deep = pl.ds(0, through_z)
         z, x, c, y = place.z, place.x, place.c, place.y
         self.up, self.down = place.device(z=z + 1), place.device(z=z - 1)
         self.over_x, self.over_y = place.device(x=1 - x), place.device(y=1 - y)
@@ -463,8 +471,9 @@
         ref = self.whole.at[zz, xx, self.place.c, yy, rows]
         pltpu.make_async_copy(ref, ref, self.sent.at[kind, zz]).wait()
 
-    def column(self, zz, origin=None):
+    def column(self, k, origin=None):
         x, y, every = self.place.x, self.place.y, slice(None)
+        zz = self.place.near_first(k)
         self.push(self.XF, zz, x, y, every, self.over_x, origin)
         self.push(self.YF, zz, x, y, every, self.over_y, origin)
         self.push(self.CO, zz, x, y, every, self.over_c, origin)
@@ -480,97 +489,155 @@
         def _():
             self.push(self.ZD, z, x, y, slice(None), self.down, self.src)
 
-        self.column(z, self.src)
+        self.column(0, self.src)
         self.keep.start()
 
-    def along_z(self, d):
-        z, x, y, nz = self.place.z, self.place.x, self.place.y, self.place.z_count
+    def move_z(self, d, up_kind, down_kind, xx, yy, rows, hand_over):
+        z, nz = self.place.z, self.place.z_count
         below, above = z - d, z + d
 
         @pl.when(below >= 0)
         def _():
-            self.arrival(self.ZU, below, x, y)
+            self.arrival(up_kind, below, xx, yy, rows)
 
             @pl.when(z < nz - 1)
             def _():
-                self.push(self.ZU, below, x, y, slice(None), self.up)
+                self.push(up_kind, below, xx, yy, rows, self.up)
+
+            if hand_over:
+                self.push(self.CC, below, xx, yy, rows, self.over_c)
 
         @pl.when(above < nz)
         def _():
-            self.arrival(self.ZD, above, x, y)
+            self.arrival(down_kind, above, xx, yy, rows)
 
             @pl.when(z > 0)
             def _():
-                self.push(self.ZD, above, x, y, slice(None), self.down)
-
-    def relay(self, zz):
+                self.push(down_kind, above, xx, yy, rows, self.down)
+
+            if hand_over:
+                self.push(self.CC, above, xx, yy, rows, self.over_c)
+
+    def along_z(self, d):
+        self.move_z(d, self.ZU, self.ZD, self.place.x, self.place.y, slice(None), False)
+
+    def diagonal_along_z(self, d):
+        self.move_z(d, self.DU, self.DD, 1 - self.place.x, 1 - self.place.y, self.deep, True)
+
+    def relay(self, k):
         x, y, every = self.place.x, self.place.y, slice(None)
+        zz = self.place.near_first(k)
+        low, high = self.parts[k == 0]
         self.arrival(self.XF, zz, 1 - x, y)
-        self.push(self.YH, zz, 1 - x, y, self.low, self.over_y)
+        if low.size:
+            self.push(self.YH, zz, 1 - x, y, low, self.over_y)
         self.push(self.CX, zz, 1 - x, y, every, self.over_c)
         self.arrival(self.YF, zz, x, 1 - y)
-        self.push(self.XH, zz, x, 1 - y, self.high, self.over_x)
+        self.push(self.XH, zz, x, 1 - y, high, self.over_x)
         self.push(self.CY, zz, x, 1 - y, every, self.over_c)
 
-    def diagonal(self, zz):
+    def diagonal(self, k):
+        z, nz = self.place.z, self.place.z_count
+        xx, yy = 1 - self.place.x, 1 - self.place.y
+        zz = self.place.near_first(k)
+        low, high = self.parts[k == 0]
+        self.arrival(self.XH, zz, xx, yy, high)
+        if low.size:
+            self.arrival(self.YH, zz, xx, yy, low)
+        if k == 0:
+
+            @pl.when(z < nz - 1)
+            def _():
+                self.push(self.DU, z, xx, yy, self.deep, self.up)
+
+            @pl.when(z > 0)
+            def _():
+                self.push(self.DD, z, xx, yy, self.deep, self.down)
+
+        self.push(self.CB, zz, xx, yy, high, self.over_c)
+        if low.size:
+            self.push(self.CA, zz, xx, yy, low, self.over_c)
+
+    def sibling_near(self, k):
         x, y = self.place.x, self.place.y
-        self.arrival(self.XH, zz, 1 - x, 1 - y, self.high)
-        self.push(self.CB, zz, 1 - x, 1 - y, self.high, self.over_c)
-        self.arrival(self.YH, zz, 1 - x, 1 - y, self.low)
-        self.push(self.CA, zz, 1 - x, 1 - y, self.low, self.over_c)
-
-    def sibling_near(self, zz):
-        x, y = self.place.x, self.place.y
+        zz = self.place.near_first(k)
         self.arrival(self.CO, zz, x, y, sibling=True)
         self.arrival(self.CY, zz, x, 1 - y, sibling=True)
 
-    def sibling_far(self, zz):
+    def sibling_far(self, k):
         x, y = self.place.x, self.place.y
+        zz = self.place.near_first(k)
+        low, high = self.parts[k == 0]
         self.arrival(self.CX, zz, 1 - x, y, sibling=True)
-        self.arrival(self.CA, zz, 1 - x, 1 - y, self.low, sibling=True)
-        self.arrival(self.CB, zz, 1 - x, 1 - y, self.high, sibling=True)
+        self.arrival(self.CB, zz, 1 - x, 1 - y, high, sibling=True)
+        if low.size:
+            self.arrival(self.CA, zz, 1 - x, 1 - y, low, sibling=True)
+        if k > 0:
+            self.arrival(self.CC, zz, 1 - x, 1 - y, self.deep, sibling=True)
 
     def finish(self):
         z, x, y, nz = self.place.z, self.place.x, self.place.y, self.place.z_count
-
-        def one(zz, carry):
+        for k in range(nz):
+            zz = self.place.near_first(k)
+            low, high = self.parts[k == 0]
             self.departure(self.XF, zz, x, y)
             self.departure(self.YF, zz, x, y)
             self.departure(self.CO, zz, x, y)
             self.departure(self.CX, zz, 1 - x, y)
             self.departure(self.CY, zz, x, 1 - y)
-            self.departure(self.YH, zz, 1 - x, y, self.low)
-            self.departure(self.XH, zz, x, 1 - y, self.high)
-            self.departure(self.CA, zz, 1 - x, 1 - y, self.low)
-            self.departure(self.CB, zz, 1 - x, 1 - y, self.high)
+            self.departure(self.XH, zz, x, 1 - y, high)
+            self.departure(self.CB, zz, 1 - x, 1 - y, high)
+            if low.size:
+                self.departure(self.YH, zz, 1 - x, y, low)
+                self.departure(self.CA, zz, 1 - x, 1 - y, low)
+            if k > 0:
+                self.departure(self.CC, zz, 1 - x, 1 - y, self.deep)
 
             @pl.when((zz <= z) & (z < nz - 1))
             def _():
                 self.departure(self.ZU, zz, x, y)
+                self.departure(self.DU, zz, 1 - x, 1 - y, self.deep)
 
             @pl.when((zz >= z) & (z > 0))
             def _():
                 self.departure(self.ZD, zz, x, y)
-
-            return carry
-
-        lax.fori_loop(0, nz, one, 0)
+                self.departure(self.DD, zz, 1 - x, 1 - y, self.deep)
 
 
 class Fold:
-    CD, CX, CY, CO, XH, YH, XF, YF, ZU, ZD = range(10)
+    KINDS = 12
+    CD, CX, CY, CO, XH, YH, XF, YF, ZU, ZD, DU, DD = range(KINDS)
     SPOT = {CD: (1, 1), CX: (1, 0), CY: (0, 1), CO: (0, 0)}
 
-    def __init__(self, place, parts, total, from_c, half_x, half_y, z_buf, sent, got, loaded):
+    def __init__(
+        self, place, split, parts, total, from_c, half_x, half_y, z_buf, d_buf, sent, got, loaded
+    ):
         self.place, self.parts, self.total, self.from_c = place, parts, total, from_c
-        self.half_x, self.half_y, self.z_buf = half_x, half_y, z_buf
+        self.half_x, self.half_y, self.z_buf, self.d_buf = half_x, half_y, z_buf, d_buf
         self.sent, self.got, self.loaded = sent, got, loaded
         self.rows = total.shape[3]
-        self.split = half_x.shape[1]
-        self.low, self.high = pl.ds(0, self.split), pl.ds(self.split, self.rows - self.split)
+        self.own_split, self.through_z, self.other_split = split
+        self.deep = pl.ds(0, self.through_z)
         z, x, c, y = place.z, place.x, place.c, place.y
         self.over_x, self.over_y = place.device(x=1 - x), place.device(y=1 - y)
         self.over_c = place.device(c=1 - c)
+
+    def diagonal_parts(self, zz, own):
+        if own:
+            low = pl.ds(0, self.own_split)
+            high = pl.ds(self.own_split, self.rows - self.own_split)
+            return low, high, self.half_y.at[low], self.half_x.at[pl.ds(0, high.size)]
+        low = pl.ds(self.through_z, self.other_split)
+        start = self.through_z + self.other_split
+        high = pl.ds(start, self.rows - start)
+        y_start = pl.multiple_of(self.own_split + zz * low.size, 16)
+        x_start = pl.multiple_of(self.rows - self.own_split + zz * high.size, 16)
+        return (
+            low,
+            high,
+            self.half_y.at[pl.ds(y_start, low.size)],
+            self.half_x.at[pl.ds(x_start, high.size)],
+        )
 
     def push(self, kind, zz, src, dst, device):
         send(src, dst, self.sent.at[kind, zz], self.got.at[kind, zz], device)
@@ -595,9 +662,9 @@
         for i in range(nz):
             start(self.CD, i)
             start(self.CX, i)
-        for kind in (self.CY, self.CO):
-            for i in range(nz):
-                start(kind, i)
+            start(self.CY, i)
+        for i in range(nz):
+            start(self.CO, i)
 
     def join_cores(self, kind, zz):
         dx, dy = self.SPOT[kind]
@@ -606,20 +673,81 @@
         self.arrival(kind, zz, there)
         add_rows(here, there, self.rows)
 
+    def deep_push(self, zz):
+        z, nz = self.place.z, self.place.z_count
+        mine = self.total.at[1, 1, zz, self.deep]
+
+        @pl.when(zz > z)
+        def _():
+            self.push(self.DU, zz, mine, self.d_buf.at[zz], self.place.device(z=z + 1))
+
+        @pl.when(zz < z)
+        def _():
+            landing = jnp.where(zz == z - 1, nz, zz)
+            self.push(self.DD, zz, mine, self.d_buf.at[landing], self.place.device(z=z - 1))
+
+    def at_end(self):
+        return (self.place.z == 0) | (self.place.z == self.place.z_count - 1)
+
     def halves(self, i):
+        own = i == self.place.z_count - 1
         zz = self.place.far_first(i)
         self.join_cores(self.CD, zz)
         self.join_cores(self.CX, zz)
-        self.push(self.XH, zz, self.total.at[1, 1, zz, self.low], self.half_x.at[zz], self.over_x)
-        self.push(self.YH, zz, self.total.at[1, 1, zz, self.high], self.half_y.at[zz], self.over_y)
+        if own:
+            return
+        self.push_halves(zz, False)
+
+        @pl.when(self.at_end())
+        def _():
+            self.deep_push(zz)
+
+    def push_halves(self, zz, own):
+        low, high, land_y, land_x = self.diagonal_parts(zz, own)
+        self.push(self.XH, zz, self.total.at[1, 1, zz, high], land_x, self.over_x)
+        self.push(self.YH, zz, self.total.at[1, 1, zz, low], land_y, self.over_y)
+
+    def deep_on(self, i):
+        z = self.place.z
+        zz = self.place.far_first(i)
+
+        @pl.when(jnp.logical_not(self.at_end()))
+        def _():
+            @pl.when(zz > z)
+            def _():
+                self.arrival(self.DU, zz, self.d_buf.at[zz])
+
+            @pl.when(zz < z)
+            def _():
+                self.arrival(self.DD, zz, self.d_buf.at[zz])
+
+            add_rows(self.total.at[1, 1, zz, self.deep], self.d_buf.at[zz], self.through_z)
+            self.deep_push(zz)
+
+    def own_halves(self):
+        z, nz = self.place.z, self.place.z_count
+        mine = self.total.at[1, 1, z, self.deep]
+
+        @pl.when(z > 0)
+        def _():
+            self.arrival(self.DU, z, self.d_buf.at[z])
+            add_rows(mine, self.d_buf.at[z], self.through_z)
+
+        @pl.when(z < nz - 1)
+        def _():
+            self.arrival(self.DD, z, self.d_buf.at[nz])
+            add_rows(mine, self.d_buf.at[nz], self.through_z)
+
+        self.push_halves(z, True)
 
     def columns(self, i):
         zz = self.place.far_first(i)
+        low, high, land_y, land_x = self.diagonal_parts(zz, i == self.place.z_count - 1)
         self.join_cores(self.CY, zz)
-        self.arrival(self.XH, zz, self.half_x.at[zz])
-        add_rows(self.total.at[0, 1, zz, self.low], self.half_x.at[zz], self.split)
-        self.arrival(self.YH, zz, self.half_y.at[zz])
-        add_rows(self.total.at[1, 0, zz, self.high], self.half_y.at[zz], self.rows - self.split)
+        self.arrival(self.XH, zz, land_x)
+        add_rows(self.total.at[0, 1, zz, high], land_x, high.size)
+        self.arrival(self.YH, zz, land_y)
+        add_rows(self.total.at[1, 0, zz, low], land_y, low.size)
         self.push(self.XF, zz, self.total.at[1, 0, zz], self.from_c.at[1, 1, zz], self.over_x)
         self.push(self.YF, zz, self.total.at[0, 1, zz], self.from_c.at[1, 0, zz], self.over_y)
 
@@ -653,6 +781,19 @@
             landing = jnp.where(zz == z - 1, nz, zz)
             self.push(self.ZD, zz, mine, self.z_buf.at[landing], self.place.device(z=z - 1))
 
+    def opening(self):
+        last = self.place.z_count - 1
+        return [functools.partial(self.halves, i) for i in range(last)] + [
+            functools.partial(self.columns, i) for i in range(min(1, last))
+        ]
+
+    def middle(self):
+        last = self.place.z_count - 1
+        steps = [functools.partial(self.deep_on, i) for i in range(last)]
+        steps.insert(1, functools.partial(self.halves, last))
+        steps.append(self.own_halves)
+        return steps + [functools.partial(self.columns, i) for i in range(min(1, last), last + 1)]
+
     def result(self):
         return self.total[0, 0, self.place.z]
 
@@ -662,34 +803,41 @@
         def departure(kind, zz, ref):
             pltpu.make_async_copy(ref, ref, self.sent.at[kind, zz]).wait()
 
-        def one(zz, carry):
+        for i in range(nz):
+            zz = self.place.far_first(i)
+            low, high, land_y, land_x = self.diagonal_parts(zz, i == nz - 1)
             for kind in (self.CD, self.CX, self.CY, self.CO, self.XF, self.YF):
                 departure(kind, zz, self.total.at[0, 0, zz])
-            departure(self.XH, zz, self.half_x.at[zz])
-            departure(self.YH, zz, self.half_y.at[zz])
+            departure(self.XH, zz, land_x)
+            departure(self.YH, zz, land_y)
 
             @pl.when(zz > z)
             def _():
                 departure(self.ZU, zz, self.total.at[0, 0, zz])
+                departure(self.DU, zz, self.d_buf.at[zz])
 
             @pl.when(zz < z)
             def _():
                 departure(self.ZD, zz, self.total.at[0, 0, zz])
-
-            return carry
-
-        lax.fori_loop(0, nz, one, 0)
+                departure(self.DD, zz, self.d_buf.at[zz])
+
+
+def half_rows(rows, split):
+    own, deep, other = split
+    return (own, other), (rows - own, rows - deep - other)
 
 
 def fold_scratch(nz, rows, cols, split, dt):
+    (y_own, y_other), (x_own, x_other) = half_rows(rows, split)
     return [
         pltpu.VMEM((2, 2, nz, rows, cols), dt),
         pltpu.VMEM((2, 2, nz, rows, cols), dt),
-        pltpu.VMEM((nz, split, cols), dt),
-        pltpu.VMEM((nz, rows - split, cols), dt),
+        pltpu.VMEM((x_own + nz * x_other, cols), dt),
+        pltpu.VMEM((y_own + nz * y_other, cols), dt),
         pltpu.VMEM((nz + 1, rows, cols), dt),
-        pltpu.SemaphoreType.DMA((10, nz)),
-        pltpu.SemaphoreType.DMA((10, nz)),
+        pltpu.VMEM((nz + 1, split[1], cols), dt),
+        pltpu.SemaphoreType.DMA((Fold.KINDS, nz)),
+        pltpu.SemaphoreType.DMA((Fold.KINDS, nz)),
         pltpu.SemaphoreType.DMA((4, nz)),
     ]
 
@@ -700,7 +848,7 @@
     tiles, tile_sems, scratch = refs[4:9], refs[9], refs[10:]
     place = Place()
     nz = place.z_count
-    fold = Fold(place, parts, *scratch)
+    fold = Fold(place, row_split(out.shape[0]), parts, *scratch)
     count = streams[0].shape[0]
     place.meet()
     fold.begin()
@@ -731,19 +879,20 @@
         copy.start()
     for grad in (wg_grad, wu_grad, wd_grad):
         grad[...] = jnp.zeros_like(grad)
-    for i in range(nz):
-        fold.halves(i)
-    steps = [functools.partial(fold.columns, i) for i in range(nz)]
+    steps = fold.opening() + fold.middle()
     steps += [functools.partial(fold.along_z, i) for i in range(nz)]
     done = 0
     for n, step in enumerate(steps):
-        share = (n + 1) / (2 * nz) if n < nz else 0.5 + (n - nz + 1) / (2 * nz)
-        until = min(count, round(count * share))
+        until = min(count, round(count * n / (len(steps) - 1)))
         lax.fori_loop(done, until, tile_step, 0)
         done = until
         step()
     out[...] = fold.result()
     fold.finish()
+
+
+def row_split(rows):
+    return rows // 2, rows // 2, rows // 4
 
 
 def scatter_sum(parts, streams, collective):
@@ -761,7 +910,7 @@
         out_specs=[IN_VMEM] * 4,
         scratch_shapes=[pltpu.VMEM((2,) + stream.shape[1:], stream.dtype) for stream in streams]
         + [pltpu.SemaphoreType.DMA((2, 5))]
-        + fold_scratch(nz, rows, cols, rows // 2, dt),
+        + fold_scratch(nz, rows, cols, row_split(rows), dt),
         cost_estimate=LINK_TIME,
         compiler_params=pltpu.CompilerParams(
             collective_id=collective, has_side_effects=True, vmem_limit_bytes=62 << 20
@@ -819,13 +968,10 @@
     place = Place()
     nz = place.z_count
     rows = leaving.shape[0]
-    spread = Spread(place, src, whole, sent, got, kept, src.shape[0] // 3)
+    spread = Spread(place, src, whole, sent, got, kept, rows // 4, rows * 3 // 4, 0)
     place.meet()
     over_y = place.device(y=1 - place.y)
     spread.begin()
-
-    def near(k):
-        return place.far_first(nz - 1 - k)
 
     lane = lax.broadcasted_iota(jnp.int32, stats.shape, 1)
     stats[...] = jnp.zeros_like(stats)
@@ -843,10 +989,10 @@
 
     lax.fori_loop(0, queries.shape[1] // chunk, project, 0)
     stats_swap = send(stats, stats_got, swap_sems.at[0, 0], swap_sems.at[1, 0], over_y)
+    spread.relay(0)
     if nz > 1:
         spread.along_z(1)
-        spread.column(near(1))
-    spread.relay(near(0))
+        spread.column(1)
     stats_swap.wait()
     for index, inv in enumerate((q_inv, k_inv)):
         total = stats[:, index : index + 1] + stats_got[:, index : index + 1]
@@ -870,9 +1016,10 @@
 
     heads = queries.shape[1] // HEAD
     lax.fori_loop(0, heads // 2, head, 0)
+    spread.diagonal(0)
     if nz > 2:
         spread.along_z(2)
-        spread.column(near(2))
+        spread.column(2)
     lax.fori_loop(heads // 2, heads, head, 0)
 
     def joined(target, index):
@@ -888,23 +1035,22 @@
     joined(leaving, 1 - place.y)
     swap = send(leaving, landed, swap_sems.at[0, 1], swap_sems.at[1, 1], over_y)
     if nz > 1:
-        spread.relay(near(1))
+        spread.relay(1)
     joined(attended, place.y)
-    for d in range(3, nz):
-        spread.along_z(d)
-        spread.column(near(d))
-    spread.diagonal(near(0))
-    for k in range(2, nz):
-        spread.relay(near(k))
-        spread.diagonal(near(k - 1))
-    if nz > 1:
-        spread.diagonal(near(nz - 1))
+    for k in range(1, nz):
+        spread.diagonal_along_z(k)
+        if k + 2 < nz:
+            spread.along_z(k + 2)
+            spread.column(k + 2)
+        if k + 1 < nz:
+            spread.relay(k + 1)
+        spread.diagonal(k)
     swap.wait()
     attended[...] += landed[...].astype(jnp.float32)
     spread.keep.wait()
-    for zz in range(nz):
-        spread.sibling_near(zz)
-        spread.sibling_far(zz)
+    for k in range(nz):
+        spread.sibling_near(k)
+        spread.sibling_far(k)
     spread.finish()
 
 
@@ -938,8 +1084,8 @@
             pltpu.VMEM((rows, width), jnp.bfloat16),
             pltpu.VMEM((rows, width), jnp.bfloat16),
             pltpu.SemaphoreType.DMA((2, 2)),
-            pltpu.SemaphoreType.DMA((11, nz)),
-            pltpu.SemaphoreType.DMA((11, nz)),
+            pltpu.SemaphoreType.DMA((Spread.KINDS, nz)),
+            pltpu.SemaphoreType.DMA((Spread.KINDS, nz)),
             pltpu.SemaphoreType.DMA,
         ],
         cost_estimate=LINK_TIME,
@@ -947,6 +1093,10 @@
             collective_id=collective, has_side_effects=True, vmem_limit_bytes=60 << 20
         ),
     )(block, normed, *weights, *gains, *tables)
+
+
+def busy_y_split(rows):
+    return rows // 2, rows // 2, rows // 6
 
 
 def attend_back_kernel(
@@ -982,7 +1132,7 @@
 ):
     place = Place()
     nz = place.z_count
-    fold = Fold(place, parts, *scratch)
+    fold = Fold(place, busy_y_split(own_grad.shape[0]), parts, *scratch)
     place.meet()
     over_y = place.device(y=1 - place.y)
     rows = own_grad.shape[0]
@@ -1003,8 +1153,8 @@
         mixed_grad[where] = total.astype(jnp.bfloat16)
 
     take(own_grad, place.y)
-    for i in range(nz):
-        fold.halves(i)
+    for step in fold.opening():
+        step()
     swap.wait()
     take(landed, 1 - place.y)
     visible = seen_keys()
@@ -1036,10 +1186,10 @@
         return carry
 
     heads = queries.shape[1] // HEAD
-    cuts = [heads * (i + 1) // nz for i in range(nz)]
-    for i in range(nz):
-        fold.columns(i)
-        lax.fori_loop(cuts[i - 1] if i else 0, cuts[i], head, 0)
+    steps = fold.middle()
+    for n, step in enumerate(steps):
+        step()
+        lax.fori_loop(heads * n // len(steps), heads * (n + 1) // len(steps), head, 0)
     dots_swap = send(dots, dots_got, swap_sems.at[0, 1], swap_sems.at[1, 1], over_y)
     for i in range(nz):
         fold.along_z(i)
@@ -1068,7 +1218,6 @@
     group, head_cols = queries.shape
     half = jax.ShapeDtypeStruct((group, head_cols), jnp.bfloat16)
     wide = pltpu.VMEM((group, head_cols), jnp.float32)
-    split = rows * 2 // 3
     return pl.pallas_call(
         attend_back_kernel,
         out_shape=[
@@ -1090,7 +1239,7 @@
             pltpu.VMEM((group, LANES), jnp.float32),
             pltpu.SemaphoreType.DMA((2, 2)),
         ]
-        + fold_scratch(nz, rows, cols, split, parts.dtype),
+        + fold_scratch(nz, rows, cols, busy_y_split(rows), parts.dtype),
         cost_estimate=LINK_TIME,
         compiler_params=pltpu.CompilerParams(
             collective_id=collective, has_side_effects=True, vmem_limit_bytes=62 << 20
@@ -1485,22 +1634,21 @@
 ):
     place = Place()
     place.meet()
-    spread = Spread(place, src, x_all, sent, got, kept)
+    third = src.shape[0] // 3
+    spread = Spread(place, src, x_all, sent, got, kept, src.shape[0] // 2, 2 * third, third // 2)
     spread.begin()
     width = src.shape[1]
     tile = x_tile.shape[1]
     pairs = sorted(
-        ((k, dx) for k in range(z_count) for dx in (0, 1)), key=lambda p: p[0] + 1.3 * p[1]
+        ((k, dx) for k in range(z_count) for dx in (0, 1)),
+        key=lambda p: p[0] + (1.3 if p[0] else 0.5) * p[1],
     )
     tiles = 2 * len(pairs)
     near_table, across_table = [p[0] for p in pairs], [p[1] for p in pairs]
 
-    def near(k):
-        return place.far_first(z_count - 1 - k)
-
     def tile_at(i):
         pair, second = i // 2, i % 2
-        zz = near(pick(near_table, pair))
+        zz = place.near_first(pick(near_table, pair))
         xx = jnp.where(pick(across_table, pair) == 1, 1 - place.x, place.x)
         cc = jnp.where(second == 1, 1 - place.c, place.c)
         return zz, xx, cc
@@ -1539,11 +1687,18 @@
     for position, (k, dx) in enumerate(pairs):
         todo = []
         if dx == 0:
+            if k == 0:
+                todo.append((spread.relay, 0))
+            elif k > 1:
+                todo.append((spread.diagonal_along_z, k - 1))
             if k + 1 < z_count:
-                todo += [("z", k + 1), ("column", k + 1)]
-            todo.append(("relay", k))
+                todo += [(spread.along_z, k + 1), (spread.column, k + 1)]
+            if k > 0:
+                todo.append((spread.relay, k))
         else:
-            todo.append(("diagonal", k))
+            if k == z_count - 1 and k > 0:
+                todo.append((spread.diagonal_along_z, k))
+            todo.append((spread.diagonal, k))
         steps[2 * position] = todo
 
     def prepare(i):
@@ -1554,21 +1709,14 @@
             @pl.when(i == position)
             def _():
                 if position % 2 == 0:
-                    for kind, number in steps[position]:
-                        if kind == "z":
-                            spread.along_z(number)
-                        elif kind == "column":
-                            spread.column(near(number))
-                        elif kind == "relay":
-                            spread.relay(near(number))
-                        else:
-                            spread.diagonal(near(number))
+                    for step, number in steps[position]:
+                        step(number)
                     if position == 0:
                         spread.keep.wait()
                 elif dx == 0:
-                    spread.sibling_near(near(k))
+                    spread.sibling_near(k)
                 else:
-                    spread.sibling_far(near(k))
+                    spread.sibling_far(k)
 
         for copy in loads(i, i % 2):
             copy.start()
@@ -1582,6 +1730,10 @@
         def _():
             for copy in store(i - 2, slot):
                 copy.wait()
+
+        @pl.when(i < tiles - 1)
+        def _():
+            prepare(i + 1)
 
         zz, xx, cc = tile_at(i)
         rows = x_tile[slot]
@@ -1594,10 +1746,6 @@
         gate_pre = dot_nn(rows, wg_ref[...])
         up_pre = dot_nn(rows, wu_ref[...])
         raw_grad = dot_nt(g_tile[slot], wd_ref[...])
-
-        @pl.when(i < tiles - 1)
-        def _():
-            prepare(i + 1)
 
         sigmoid = jax.nn.sigmoid(gate_pre)
         silu = gate_pre * sigmoid
@@ -1658,8 +1806,8 @@
             pltpu.VMEM((2, tile, units), jnp.bfloat16),
             pltpu.SemaphoreType.DMA((2, 3)),
             pltpu.SemaphoreType.DMA((2, 5)),
-            pltpu.SemaphoreType.DMA((11, nz)),
-            pltpu.SemaphoreType.DMA((11, nz)),
+            pltpu.SemaphoreType.DMA((Spread.KINDS, nz)),
+            pltpu.SemaphoreType.DMA((Spread.KINDS, nz)),
             pltpu.SemaphoreType.DMA,
         ],
         cost_estimate=LINK_TIME,

time: 820 us -> 768 us (0.937)
  Pallas kernels: 752 us -> 700 us
    pallas_call x1, Pallas kernels: 131 us -> 113 us  [scatter_sum(): pl.pallas_call(scatter_kernel, out_shape=[jax.ShapeDtypeStruct((rows, col...]
    pallas_call x1, Pallas kernels: 131 us -> 115 us  [attend(): pl.pallas_call(attend_kernel, out_shape=[jax.ShapeDtypeStruct((nz, 2, 2,...]
    pallas_call x1, Pallas kernels: 133 us -> 118 us  [attend_back(): pl.pallas_call(attend_back_kernel, out_shape=[jax.ShapeDtypeStruct((rows,...]
where the time goes in v6:
time: 768 us; the launch traced here: 761 us
  Pallas kernels  700 us (91%)
  local copies, waits for them, and re-layouts  28 us (4%)
  other arithmetic  19.9 us (3%)
  matrix products  11.7 us (2%)
    pallas_call x1, Pallas kernels, expert_pass(): pl.pallas_call(functools.partial(expert_kernel, nz), in_specs=[ANYWHERE]...  141 us
    pallas_call x1, Pallas kernels, attend_back(): pl.pallas_call(attend_back_kernel, out_shape=[jax.ShapeDtypeStruct((rows,...  118 us
    pallas_call x1, Pallas kernels, attend(): pl.pallas_call(attend_kernel, out_shape=[jax.ShapeDtypeStruct((nz, 2, 2,...  115 us
    pallas_call x1, Pallas kernels, scatter_in_plane(): pl.pallas_call(functools.partial(plane_scatter_kernel, count), out_shape=...  113 us
    pallas_call x1, Pallas kernels, scatter_sum(): pl.pallas_call(scatter_kernel, out_shape=[jax.ShapeDtypeStruct((rows, col...  113 us
    pallas_call x1, Pallas kernels, gather_in_plane(): pl.pallas_call(functools.partial(plane_gather_kernel, count), out_shape=[...  99.4 us
    unnamed x88, local copies, waits for them, and re-layouts  18.5 us

profile of v6, /device:TPU:0, one launch (start us, length us, event | category | flops | bytes accessed | tf_op | source)
XLA Modules:
  0.0 760.9 jit_solution(631720643964678622)
XLA Ops:
  2.0 99.4 %shard_map.254 = (bf16[4,2,2,128,1024]{4,3,2,1,0:T(8,128)(2,1)}, bf16[4,2,2,128,1024]{4,3,2,1,0:T(8,128)(2,1)}, bf16[4,2,2,128,1024]{4,3,2,1,0:T(8,128)(2,1)}, b...) custom-call(bf16[128,1024]{1,0:T(8,128)(2,1)} %refs_0_.1, ...), custom_call_target="tpu_custom_call" | custom-call | flops 99999997952 | bytes 100000000 | tf_op jit(solution)/shard_map/pallas_call | solution.py:1358
  101.5 1.2 broadcast_select_fusion.1
  104.5 1.6 fusion.2.normed.refs_0_.refs_1_.refs_2_
  107.4 1.5 sine_multiply_fusion
  109.0 115.1 %shard_map.255 = (bf16[4,2,2,2,192,2048]{5,4,3,2,1,0:T(8,128)(2,1)}, f32[384,1024]{1,0:T(8,128)}, f32[384,1024]{1,0:T(8,128)}, bf16[384,1024]{1,0:T(8,128)(2,1)}...) custom-call(bf16[192,2048]{1,0:T(8,128)(2,1)} %src.1, ...), custom_call_target="tpu_custom_call" | custom-call | flops 99999997952 | bytes 100000000 | tf_op jit(solution)/shard_map/pallas_call | solution.py:1064
  224.1 1.7 multiply_reduce_fusion.2
  226.9 1.1 multiply_convert_fusion.src
  228.9 0.9 pad.4.router_ref
  229.9 140.8 %shard_map.256 = (bf16[4,2,2,2,192,2048]{5,4,3,2,1,0:T(8,128)(2,1)}, bf16[4,2,2,384,2048]{4,3,2,1,0:T(8,128)(2,1)}, bf16[4,2,2,384,2176]{4,3,2,1,0:T(8,128)(2,1)...) custom-call(bf16[192,2048]{1,0:T(8,128)(2,1)} %multiply_convert_fusi, ...), custom_call_target="tpu_custom_call" | custom-call | flops 99999997952 | bytes 100000000 | tf_op jit(solution)/shard_map/pallas_call | solution.py:1789
  370.7 113.2 %shard_map.257 = (bf16[192,2176]{1,0:T(8,128)(2,1)}, f32[2048,512]{1,0:T(8,128)}, f32[2048,512]{1,0:T(8,128)}, f32[512,2048]{1,0:T(8,128)}) custom-call(bf16[4,2,2,2,192,2176]{5,4,3,2,1,0:T(8,128)(2,1)} %bitcast.61, bf16[24,256,2048]{2,1,0:T(8,128)(2,1)} %bitcast.65, bf16[24,256,2048]{2,1,0:T(8,128)(2,1)} %bitcast.63, bf16[24,256,512]{2,1,0:T(8,128)(2,1)} %bitcast.66, ...), custom_call_target="tpu_custom_call" | custom-call | flops 99999997952 | bytes 100000000 | tf_op jit(solution)/shard_map/pallas_call | solution.py:905
  484.9 1.5 fusion.21
  486.6 1.3 multiply_reduce_fusion
  488.0 1.9 fusion.19
  489.9 118.1 %shard_map.258 = (bf16[192,2048]{1,0:T(8,128)(2,1)}, bf16[384,2048]{1,0:T(8,128)(2,1)}, bf16[384,1024]{1,0:T(8,128)(2,1)}, bf16[384,1024]{1,0:T(8,128)(2,1)}, bf...) custom-call(bf16[4,2,2,2,192,2048]{5,4,3,2,1,0:T(8,128)(2,1)} %bitcast.64, bf16[192,2048]{1,0:T(8,128)(2,1)} %get-tuple-element.152.own_grad, ...), custom_call_target="tpu_custom_call" | custom-call | flops 99999997952 | bytes 100000000 | tf_op jit(solution)/shard_map/pallas_call | solution.py:1221
  608.0 4.4 fusion.23
  612.5 1.8 fusion.22
  615.3 2.3 fusion.3
  617.6 1.7 copy-done.3
  619.2 1.0 dynamic-slice_convert_fusion.refs_9_
  622.6 1.4 concatenate.11.refs_8_
  624.0 113.4 %shard_map.259 = (f32[128,1024]{1,0:T(8,128)}, f32[128,1024]{1,0:T(8,128)}, f32[128,1024]{1,0:T(8,128)}, f32[128,1024]{1,0:T(8,128)}, f32[24,2048]{1,0:T(8,128)}, /*index=5*/bf16[192,2048]{1,0:T(8,128)(2,1)}) custom-call(bf16[384,2048]{1,0:T(8,128)(2,1)} %fusion.2.normed.refs_0_.refs_1_.refs_2_, bf16[384,2048]{1,0:T(8,128)(2,1)} %fusion.2.normed.refs_0_.refs_1_.refs_2_, ...), custom_call_target="tpu_custom_call" | custom-call | flops 99999997952 | bytes 100000000 | tf_op jit(solution)/shard_map/pallas_call | solution.py:1561
  737.4 2.3 fusion.5
  740.0 3.5 fusion.7
  743.5 1.0 copy.43
  744.5 1.6 slice_bitcast_fusion
  746.1 1.6 fusion.20
  747.7 1.1 add_convert_fusion
  751.3 2.1 copy.56
  753.4 1.6 copy-done.13
  755.0 2.1 copy.57
  757.1 1.6 copy-done.12
  758.7 2.0 copy.58
  (113 shorter events, 13.9 us)
Async XLA Ops:
  2.0 99.5 %copy-start.5 = (bf16[192,2048]{1,0:T(8,128)(2,1)S(1)}, bf16[192,2048]{1,0:T(8,128)(2,1)}, u32[]{:S(2)}) copy-start(bf16[192,2048]{1,0:T(8,128)(2,1)} %refs_5_.1) | copy-start | bytes 2359300
  102.8 1.8 copy-start.28
  104.5 2.2 copy-start.37
  224.1 2.9 copy-start.26
  225.8 2.9 copy-start.20
  226.4 1.6 copy-start.33
  370.7 114.2 %copy-start.21 = (bf16[2048,16]{0,1:T(8,128)(2,1)S(1)}, bf16[2048,16]{0,1:T(8,128)(2,1)}, u32[]{:S(2)}) copy-start(bf16[2048,16]{0,1:T(8,128)(2,1)} %param.26) | copy-start | bytes 196612
  370.7 115.7 %copy-start.30 = (s32[384,8]{0,1:T(8,128)S(1)}, s32[384,8]{0,1:T(8,128)}, u32[]{:S(2)}) copy-start(s32[384,8]{0,1:T(8,128)} %param.16) | copy-start | bytes 36868
  370.7 115.9 %copy-start.1 = (f32[192,2048]{1,0:T(8,128)S(1)}, f32[192,2048]{1,0:T(8,128)}, u32[]{:S(2)}) copy-start(f32[192,2048]{1,0:T(8,128)} %copy-done) | copy-start | bytes 4718596
  370.7 115.9 %copy-start.27 = (f32[2048]{0:T(1024)S(1)}, f32[2048]{0:T(1024)}, u32[]{:S(2)}) copy-start(f32[2048]{0:T(1024)} %param.25) | copy-start | bytes 24580
  370.7 115.9 %copy-start.34 = (f32[192]{0:T(256)S(1)}, f32[192]{0:T(256)}, u32[]{:S(2)}) copy-start(f32[192]{0:T(256)} %copy-done.33) | copy-start | bytes 2308
  483.9 2.7 copy-start.16
  608.0 4.4 copy-start.38
  608.0 4.4 copy-start.39
  612.4 1.9 copy-start.8
  612.4 1.9 copy-start.10
  612.5 2.7 copy-start.15
  612.5 2.8 copy-start.19
  612.5 2.8 copy-start.32
  617.5 1.7 copy-start.3
  624.0 113.4 %copy-start.6 = (bf16[192,2048]{1,0:T(8,128)(2,1)S(1)}, bf16[192,2048]{1,0:T(8,128)(2,1)}, u32[]{:S(2)}) copy-start(bf16[192,2048]{1,0:T(8,128)(2,1)} %refs_5_.1) | copy-start | bytes 2359300
  624.0 113.4 %copy-start.29 = (f32[2048]{0:T(1024)S(1)}, f32[2048]{0:T(1024)}, u32[]{:S(2)}) copy-start(f32[2048]{0:T(1024)} %param.18) | copy-start | bytes 24580
  737.4 2.6 copy-start.4
  740.0 3.5 copy-start.25
  740.0 7.7 %copy-start.2 = (f32[192,2048]{1,0:T(8,128)S(1)}, f32[192,2048]{1,0:T(8,128)}, u32[]{:S(2)}) copy-start(f32[192,2048]{1,0:T(8,128)} %copy-done) | copy-start | bytes 4718596
  743.5 4.2 copy-start.18
  743.5 5.3 copy-start.24
  744.5 5.1 copy-start.23
  747.7 3.6 copy-start.14
  748.8 1.7 copy-start.22
  751.3 3.7 copy-start.13
  755.0 3.7 copy-start.12
  (8 other events, 9.5 us)

commit v7 on v6

--- a/solution.py
+++ b/solution.py
@@ -425,6 +425,16 @@
     return copy
 
 
+def fetch(sources, targets, sems):
+    copies = [
+        pltpu.make_async_copy(source, target, sems.at[n])
+        for n, (source, target) in enumerate(zip(sources, targets))
+    ]
+    for copy in copies:
+        copy.start()
+    return copies
+
+
 def add_rows(total, part, rows, step=16):
     def chunk(i, carry):
         here = pl.ds(pl.multiple_of(i * step, step), step)
@@ -936,11 +946,11 @@
 
 def attend_kernel(
     src,
-    normed,
-    w_query,
-    w_key,
-    w_value,
-    w_out,
+    normed_source,
+    w_query_source,
+    w_key_source,
+    w_value_source,
+    w_out_source,
     q_gain,
     k_gain,
     cosine,
@@ -960,11 +970,19 @@
     stats_got,
     leaving,
     landed,
+    normed,
+    w_query,
+    w_key,
+    w_value,
+    w_out,
+    fetch_sems,
     swap_sems,
     sent,
     got,
     kept,
 ):
+    sources = (normed_source, w_query_source, w_key_source, w_value_source, w_out_source)
+    fetched = fetch(sources, (normed, w_query, w_key, w_value, w_out), fetch_sems)
     place = Place()
     nz = place.z_count
     rows = leaving.shape[0]
@@ -987,6 +1005,8 @@
         values[:, here] = dot_nn(normed[...], w_value[:, here]).astype(jnp.bfloat16)
         return carry
 
+    for copy in fetched[:4]:
+        copy.wait()
     lax.fori_loop(0, queries.shape[1] // chunk, project, 0)
     stats_swap = send(stats, stats_got, swap_sems.at[0, 0], swap_sems.at[1, 0], over_y)
     spread.relay(0)
@@ -1032,6 +1052,7 @@
 
         lax.fori_loop(0, w_out.shape[0], columns, 0)
 
+    fetched[4].wait()
     joined(leaving, 1 - place.y)
     swap = send(leaving, landed, swap_sems.at[0, 1], swap_sems.at[1, 1], over_y)
     if nz > 1:
@@ -1076,13 +1097,17 @@
             jax.ShapeDtypeStruct((cols // HEAD, group, 1), jnp.float32),
             jax.ShapeDtypeStruct((rows, width), jnp.float32),
         ],
-        in_specs=[ANYWHERE] + [IN_VMEM] * 9,
+        in_specs=[ANYWHERE] * 6 + [IN_VMEM] * 4,
         out_specs=[ANYWHERE] + [IN_VMEM] * 10,
         scratch_shapes=[
             pltpu.VMEM((group, LANES), jnp.float32),
             pltpu.VMEM((group, LANES), jnp.float32),
             pltpu.VMEM((rows, width), jnp.bfloat16),
             pltpu.VMEM((rows, width), jnp.bfloat16),
+        ]
+        + [pltpu.VMEM(array.shape, array.dtype) for array in (normed, *weights)]
+        + [
+            pltpu.SemaphoreType.DMA((5,)),
             pltpu.SemaphoreType.DMA((2, 2)),
             pltpu.SemaphoreType.DMA((Spread.KINDS, nz)),
             pltpu.SemaphoreType.DMA((Spread.KINDS, nz)),
@@ -1102,15 +1127,15 @@
 def attend_back_kernel(
     parts,
     own_grad,
-    w_out,
-    queries,
-    keys,
-    q_rot,
-    k_rot,
-    values,
+    w_out_source,
+    queries_source,
+    keys_source,
+    q_rot_source,
+    k_rot_source,
+    values_source,
     q_inv,
     k_inv,
-    log_total,
+    log_total_source,
     q_gain,
     k_gain,
     cosine,
@@ -1127,9 +1152,28 @@
     k_scaled,
     dots,
     dots_got,
+    w_out,
+    queries,
+    keys,
+    q_rot,
+    k_rot,
+    values,
+    log_total,
+    fetch_sems,
     swap_sems,
     *scratch,
 ):
+    sources = (
+        w_out_source,
+        queries_source,
+        keys_source,
+        q_rot_source,
+        k_rot_source,
+        values_source,
+        log_total_source,
+    )
+    targets = (w_out, queries, keys, q_rot, k_rot, values, log_total)
+    fetched = fetch(sources, targets, fetch_sems)
     place = Place()
     nz = place.z_count
     fold = Fold(place, busy_y_split(own_grad.shape[0]), parts, *scratch)
@@ -1152,11 +1196,14 @@
         total = lax.fori_loop(0, w_out.shape[0], columns, total)
         mixed_grad[where] = total.astype(jnp.bfloat16)
 
+    fetched[0].wait()
     take(own_grad, place.y)
     for step in fold.opening():
         step()
     swap.wait()
     take(landed, 1 - place.y)
+    for copy in fetched[1:]:
+        copy.wait()
     visible = seen_keys()
     lane = lax.broadcasted_iota(jnp.int32, dots.shape, 1)
     dots[...] = jnp.zeros_like(dots)
@@ -1228,7 +1275,7 @@
             half,
             jax.ShapeDtypeStruct((8, head_cols), jnp.float32),
         ],
-        in_specs=[ANYWHERE] + [IN_VMEM] * 14,
+        in_specs=[ANYWHERE, IN_VMEM] + [ANYWHERE] * 6 + [IN_VMEM] * 2 + [ANYWHERE] + [IN_VMEM] * 4,
         out_specs=[IN_VMEM] * 6,
         scratch_shapes=[
             pltpu.VMEM((rows, cols), jnp.bfloat16),
@@ -1237,8 +1284,9 @@
             wide,
             pltpu.VMEM((group, LANES), jnp.float32),
             pltpu.VMEM((group, LANES), jnp.float32),
-            pltpu.SemaphoreType.DMA((2, 2)),
         ]
+        + [pltpu.VMEM(array.shape, array.dtype) for array in (w_out, *saved[:5], saved[7])]
+        + [pltpu.SemaphoreType.DMA((7,)), pltpu.SemaphoreType.DMA((2, 2))]
         + fold_scratch(nz, rows, cols, busy_y_split(rows), parts.dtype),
         cost_estimate=LINK_TIME,
         compiler_params=pltpu.CompilerParams(
@@ -1610,9 +1658,9 @@
     hot_ref,
     router_ref,
     lanes_ref,
-    wg_ref,
-    wu_ref,
-    wd_ref,
+    wg_source,
+    wu_source,
+    wd_source,
     x_all,
     y_all,
     r_all,
@@ -1626,12 +1674,17 @@
     hidden_tile,
     gate_pre_grad_tile,
     up_grad_tile,
+    wg_ref,
+    wu_ref,
+    wd_ref,
+    fetch_sems,
     load_sems,
     store_sems,
     sent,
     got,
     kept,
 ):
+    fetched = fetch((wg_source, wu_source, wd_source), (wg_ref, wu_ref, wd_ref), fetch_sems)
     place = Place()
     place.meet()
     third = src.shape[0] // 3
@@ -1773,6 +1826,8 @@
         return carry
 
     prepare(0)
+    for copy in fetched:
+        copy.wait()
     lax.fori_loop(0, tiles, compute, 0)
     for i in (tiles - 2, tiles - 1):
         for copy in store(i, i % 2):
@@ -1788,7 +1843,7 @@
     out = (nz, 2, 2, tile)
     return pl.pallas_call(
         functools.partial(expert_kernel, nz),
-        in_specs=[ANYWHERE] * 2 + [IN_VMEM] * 6,
+        in_specs=[ANYWHERE] * 2 + [IN_VMEM] * 3 + [ANYWHERE] * 3,
         out_specs=[ANYWHERE] * 6,
         out_shape=[
             jax.ShapeDtypeStruct((nz, 2, 2, 2, rows, width), jnp.bfloat16),
@@ -1804,6 +1859,10 @@
             pltpu.VMEM((2, tile, units), jnp.bfloat16),
             pltpu.VMEM((2, tile, units), jnp.bfloat16),
             pltpu.VMEM((2, tile, units), jnp.bfloat16),
+            pltpu.VMEM(w_gate.shape, w_gate.dtype),
+            pltpu.VMEM(w_up.shape, w_up.dtype),
+            pltpu.VMEM(w_down.shape, w_down.dtype),
+            pltpu.SemaphoreType.DMA((3,)),
             pltpu.SemaphoreType.DMA((2, 3)),
             pltpu.SemaphoreType.DMA((2, 5)),
             pltpu.SemaphoreType.DMA((Spread.KINDS, nz)),

time: 768 us -> 757 us (0.986)
  Pallas kernels: 700 us -> 690 us
where the time goes in v7:
time: 757 us; the launch traced here: 751 us
  Pallas kernels  690 us (91%)
  local copies, waits for them, and re-layouts  28 us (4%)
  other arithmetic  19.9 us (3%)
  matrix products  11.7 us (2%)
    pallas_call x1, Pallas kernels, expert_pass(): pl.pallas_call(functools.partial(expert_kernel, nz), in_specs=[ANYWHERE]...  139 us
    pallas_call x1, Pallas kernels, attend_back(): pl.pallas_call(attend_back_kernel, out_shape=[jax.ShapeDtypeStruct((rows,...  115 us
    pallas_call x1, Pallas kernels, scatter_in_plane(): pl.pallas_call(functools.partial(plane_scatter_kernel, count), out_shape=...  113 us
    pallas_call x1, Pallas kernels, scatter_sum(): pl.pallas_call(scatter_kernel, out_shape=[jax.ShapeDtypeStruct((rows, col...  113 us
    pallas_call x1, Pallas kernels, attend(): pl.pallas_call(attend_kernel, out_shape=[jax.ShapeDtypeStruct((nz, 2, 2,...  110 us
    pallas_call x1, Pallas kernels, gather_in_plane(): pl.pallas_call(functools.partial(plane_gather_kernel, count), out_shape=[...  99.4 us
    unnamed x88, local copies, waits for them, and re-layouts  18.5 us

profile of v7, /device:TPU:0, one launch (start us, length us, event | category | flops | bytes accessed | tf_op | source)
XLA Modules:
  0.0 750.6 jit_solution(11602380380061844240)
XLA Ops:
  2.0 99.4 %shard_map.254 = (bf16[4,2,2,128,1024]{4,3,2,1,0:T(8,128)(2,1)}, bf16[4,2,2,128,1024]{4,3,2,1,0:T(8,128)(2,1)}, bf16[4,2,2,128,1024]{4,3,2,1,0:T(8,128)(2,1)}, b...) custom-call(bf16[128,1024]{1,0:T(8,128)(2,1)} %refs_0_.1, ...), custom_call_target="tpu_custom_call" | custom-call | flops 99999997952 | bytes 100000000 | tf_op jit(solution)/shard_map/pallas_call | solution.py:1406
  101.5 1.2 broadcast_select_fusion.1
  104.5 1.6 fusion.2.normed_source.refs_0_.refs_1_.refs_2_
  107.4 1.5 sine_multiply_fusion
  109.0 109.8 %shard_map.255 = (bf16[4,2,2,2,192,2048]{5,4,3,2,1,0:T(8,128)(2,1)}, f32[384,1024]{1,0:T(8,128)}, f32[384,1024]{1,0:T(8,128)}, bf16[384,1024]{1,0:T(8,128)(2,1)}...) custom-call(bf16[192,2048]{1,0:T(8,128)(2,1)} %src.1, ...), custom_call_target="tpu_custom_call" | custom-call | flops 99999997952 | bytes 100000000 | tf_op jit(solution)/shard_map/pallas_call | solution.py:1085
  218.8 1.7 multiply_reduce_fusion.2
  221.6 1.1 multiply_convert_fusion.src
  223.7 0.9 pad.4.router_ref
  224.6 138.8 %shard_map.256 = (bf16[4,2,2,2,192,2048]{5,4,3,2,1,0:T(8,128)(2,1)}, bf16[4,2,2,384,2048]{4,3,2,1,0:T(8,128)(2,1)}, bf16[4,2,2,384,2176]{4,3,2,1,0:T(8,128)(2,1)...) custom-call(bf16[192,2048]{1,0:T(8,128)(2,1)} %multiply_convert_fusi, ...), custom_call_target="tpu_custom_call" | custom-call | flops 99999997952 | bytes 100000000 | tf_op jit(solution)/shard_map/pallas_call | solution.py:1844
  363.5 113.2 %shard_map.257 = (bf16[192,2176]{1,0:T(8,128)(2,1)}, f32[2048,512]{1,0:T(8,128)}, f32[2048,512]{1,0:T(8,128)}, f32[512,2048]{1,0:T(8,128)}) custom-call(bf16[4,2,2,2,192,2176]{5,4,3,2,1,0:T(8,128)(2,1)} %bitcast.61, bf16[24,256,2048]{2,1,0:T(8,128)(2,1)} %bitcast.65, bf16[24,256,2048]{2,1,0:T(8,128)(2,1)} %bitcast.63, bf16[24,256,512]{2,1,0:T(8,128)(2,1)} %bitcast.66, ...), custom_call_target="tpu_custom_call" | custom-call | flops 99999997952 | bytes 100000000 | tf_op jit(solution)/shard_map/pallas_call | solution.py:915
  477.6 1.5 fusion.21
  479.3 1.3 multiply_reduce_fusion
  480.7 1.9 fusion.19
  482.6 115.0 %shard_map.258 = (bf16[192,2048]{1,0:T(8,128)(2,1)}, bf16[384,2048]{1,0:T(8,128)(2,1)}, bf16[384,1024]{1,0:T(8,128)(2,1)}, bf16[384,1024]{1,0:T(8,128)(2,1)}, bf...) custom-call(bf16[4,2,2,2,192,2048]{5,4,3,2,1,0:T(8,128)(2,1)} %bitcast.64, bf16[192,2048]{1,0:T(8,128)(2,1)} %get-tuple-element.152.own_grad, ...), custom_call_target="tpu_custom_call" | custom-call | flops 99999997952 | bytes 100000000 | tf_op jit(solution)/shard_map/pallas_call | solution.py:1268
  597.7 4.4 fusion.23
  602.1 1.8 fusion.22
  604.9 2.3 fusion.3
  607.2 1.7 copy-done.3
  608.9 1.0 dynamic-slice_convert_fusion.refs_9_
  612.3 1.4 concatenate.11.refs_8_
  613.6 113.4 %shard_map.259 = (f32[128,1024]{1,0:T(8,128)}, f32[128,1024]{1,0:T(8,128)}, f32[128,1024]{1,0:T(8,128)}, f32[128,1024]{1,0:T(8,128)}, f32[24,2048]{1,0:T(8,128)}, /*index=5*/bf16[192,2048]{1,0:T(8,128)(2,1)}) custom-call(bf16[384,2048]{1,0:T(8,128)(2,1)} %fusion.2.normed_source.refs_0_.refs_1_.refs_2_, ...), custom_call_target="tpu_custom_call" | custom-call | flops 99999997952 | bytes 100000000 | tf_op jit(solution)/shard_map/pallas_call | solution.py:1609
  727.1 2.3 fusion.5
  729.7 3.5 fusion.7
  733.1 1.0 copy.43
  734.1 1.6 slice_bitcast_fusion
  735.8 1.6 fusion.20
  737.4 1.1 add_convert_fusion
  741.0 2.1 copy.56
  743.1 1.6 copy-done.13
  744.7 2.1 copy.57
  746.8 1.6 copy-done.12
  748.4 2.0 copy.58
  (113 shorter events, 13.9 us)
Async XLA Ops:
  2.0 99.5 %copy-start.5 = (bf16[192,2048]{1,0:T(8,128)(2,1)S(1)}, bf16[192,2048]{1,0:T(8,128)(2,1)}, u32[]{:S(2)}) copy-start(bf16[192,2048]{1,0:T(8,128)(2,1)} %refs_5_.1) | copy-start | bytes 2359300
  102.8 1.8 copy-start.28
  104.5 2.2 copy-start.37
  218.8 2.9 copy-start.26
  220.5 2.9 copy-start.20
  221.1 1.6 copy-start.33
  363.4 114.2 %copy-start.21 = (bf16[2048,16]{0,1:T(8,128)(2,1)S(1)}, bf16[2048,16]{0,1:T(8,128)(2,1)}, u32[]{:S(2)}) copy-start(bf16[2048,16]{0,1:T(8,128)(2,1)} %param.26) | copy-start | bytes 196612
  363.4 115.7 %copy-start.30 = (s32[384,8]{0,1:T(8,128)S(1)}, s32[384,8]{0,1:T(8,128)}, u32[]{:S(2)}) copy-start(s32[384,8]{0,1:T(8,128)} %param.16) | copy-start | bytes 36868
  363.4 115.9 %copy-start.1 = (f32[192,2048]{1,0:T(8,128)S(1)}, f32[192,2048]{1,0:T(8,128)}, u32[]{:S(2)}) copy-start(f32[192,2048]{1,0:T(8,128)} %copy-done) | copy-start | bytes 4718596
  363.4 115.9 %copy-start.27 = (f32[2048]{0:T(1024)S(1)}, f32[2048]{0:T(1024)}, u32[]{:S(2)}) copy-start(f32[2048]{0:T(1024)} %param.25) | copy-start | bytes 24580
  363.4 115.9 %copy-start.34 = (f32[192]{0:T(256)S(1)}, f32[192]{0:T(256)}, u32[]{:S(2)}) copy-start(f32[192]{0:T(256)} %copy-done.33) | copy-start | bytes 2308
  476.6 2.7 copy-start.16
  597.6 4.4 copy-start.38
  597.7 4.4 copy-start.39
  602.1 1.9 copy-start.8
  602.1 1.9 copy-start.10
  602.1 2.7 copy-start.15
  602.1 2.8 copy-start.19
  602.1 2.8 copy-start.32
  607.2 1.7 copy-start.3
  613.6 113.4 %copy-start.6 = (bf16[192,2048]{1,0:T(8,128)(2,1)S(1)}, bf16[192,2048]{1,0:T(8,128)(2,1)}, u32[]{:S(2)}) copy-start(bf16[192,2048]{1,0:T(8,128)(2,1)} %refs_5_.1) | copy-start | bytes 2359300
  613.6 113.4 %copy-start.29 = (f32[2048]{0:T(1024)S(1)}, f32[2048]{0:T(1024)}, u32[]{:S(2)}) copy-start(f32[2048]{0:T(1024)} %param.18) | copy-start | bytes 24580
  727.1 2.6 copy-start.4
  729.7 3.5 copy-start.25
  729.7 7.7 %copy-start.2 = (f32[192,2048]{1,0:T(8,128)S(1)}, f32[192,2048]{1,0:T(8,128)}, u32[]{:S(2)}) copy-start(f32[192,2048]{1,0:T(8,128)} %copy-done) | copy-start | bytes 4718596
  733.1 4.2 copy-start.18
  733.1 5.3 copy-start.24
  734.1 5.1 copy-start.23
  737.4 3.6 copy-start.14
  738.5 1.7 copy-start.22
  741.0 3.7 copy-start.13
  744.7 3.7 copy-start.12
  (8 other events, 9.5 us)

commit v8 on v7

--- a/solution.py
+++ b/solution.py
@@ -1301,23 +1301,33 @@
     sent, got, kept, swap_sems = refs[2 * count + 2 :]
     place = Place()
     z, x, c, nz = place.z, place.x, place.c, place.z_count
-    ZU, ZD, XF, CO, CX = range(5)
+    ZU, ZD, XF, CO, CX, EU, ED, CE = range(8)
     up, down = place.device(z=z + 1), place.device(z=z - 1)
     over_x, over_c = place.device(x=1 - x), place.device(c=1 - c)
     place.meet()
     every = range(count)
     swap = send(block, landed, swap_sems.at[0], swap_sems.at[1], place.device(y=1 - place.y))
 
-    def push(a, kind, zz, xx, device, own=False):
-        ref = outs[a].at[zz, xx, c]
+    lengths = [src.shape[0] for src in srcs]
+    deep = [3 * n // 4 if n == max(lengths) else 0 for n in lengths]
+
+    def rest(a, own):
+        return slice(None) if own or not deep[a] else pl.ds(deep[a], lengths[a] - deep[a])
+
+    def view(a, zz, xx, cc, rows):
+        block = outs[a].at[zz, xx, cc]
+        return block if rows == slice(None) else block.at[rows]
+
+    def push(a, kind, zz, xx, device, own=False, rows=slice(None)):
+        ref = view(a, zz, xx, c, rows)
         send(srcs[a] if own else ref, ref, sent.at[kind, a, zz], got.at[kind, a, zz], device)
 
-    def arrival(a, kind, zz, xx, cc):
-        ref = outs[a].at[zz, xx, cc]
+    def arrival(a, kind, zz, xx, cc, rows=slice(None)):
+        ref = view(a, zz, xx, cc, rows)
         pltpu.make_async_copy(ref, ref, got.at[kind, a, zz]).wait()
 
-    def departure(a, kind, zz, xx):
-        ref = outs[a].at[zz, xx, c]
+    def departure(a, kind, zz, xx, rows=slice(None)):
+        ref = view(a, zz, xx, c, rows)
         pltpu.make_async_copy(ref, ref, sent.at[kind, a, zz]).wait()
 
     keeps = []
@@ -1337,9 +1347,44 @@
         keep.start()
         keeps.append(keep)
 
-    def relay(a, zz):
-        arrival(a, XF, zz, 1 - x, c)
-        push(a, CX, zz, 1 - x, over_c)
+    def relay(a, zz, own):
+        rows = rest(a, own)
+        arrival(a, XF, zz, 1 - x, c, rows)
+        if own and deep[a]:
+            some = pl.ds(0, deep[a])
+
+            @pl.when(z < nz - 1)
+            def _():
+                push(a, EU, z, 1 - x, up, rows=some)
+
+            @pl.when(z > 0)
+            def _():
+                push(a, ED, z, 1 - x, down, rows=some)
+
+        push(a, CX, zz, 1 - x, over_c, rows=rows)
+
+    def deep_along_z(a, d):
+        some = pl.ds(0, deep[a])
+
+        @pl.when(z - d >= 0)
+        def _():
+            arrival(a, EU, z - d, 1 - x, c, some)
+
+            @pl.when(z < nz - 1)
+            def _():
+                push(a, EU, z - d, 1 - x, up, rows=some)
+
+            push(a, CE, z - d, 1 - x, over_c, rows=some)
+
+        @pl.when(z + d < nz)
+        def _():
+            arrival(a, ED, z + d, 1 - x, c, some)
+
+            @pl.when(z > 0)
+            def _():
+                push(a, ED, z + d, 1 - x, down, rows=some)
+
+            push(a, CE, z + d, 1 - x, over_c, rows=some)
 
     for d in range(nz):
         below, above = z - d - 1, z + d + 1
@@ -1353,7 +1398,7 @@
                     def _():
                         push(a, ZU, below, x, up)
 
-                    push(a, XF, below, x, over_x)
+                    push(a, XF, below, x, over_x, rows=rest(a, False))
                     push(a, CO, below, x, over_c)
 
                 @pl.when(above < nz)
@@ -1364,38 +1409,50 @@
                     def _():
                         push(a, ZD, above, x, down)
 
-                    push(a, XF, above, x, over_x)
+                    push(a, XF, above, x, over_x, rows=rest(a, False))
                     push(a, CO, above, x, over_c)
 
     for d in range(nz):
         for a in every:
             if d == 0:
-                relay(a, z)
+                relay(a, z, True)
             else:
                 @pl.when(z - d >= 0)
                 def _():
-                    relay(a, z - d)
+                    relay(a, z - d, False)
 
                 @pl.when(z + d < nz)
                 def _():
-                    relay(a, z + d)
+                    relay(a, z + d, False)
+
+                if deep[a]:
+                    deep_along_z(a, d)
 
     for a in every:
         keeps[a].wait()
-        for zz in range(nz):
+        for near in range(nz):
+            zz = place.near_first(near)
+            rows, some = rest(a, near == 0), pl.ds(0, deep[a])
             arrival(a, CO, zz, x, 1 - c)
-            arrival(a, CX, zz, 1 - x, 1 - c)
-            departure(a, XF, zz, x)
+            arrival(a, CX, zz, 1 - x, 1 - c, rows)
+            departure(a, XF, zz, x, rows)
             departure(a, CO, zz, x)
-            departure(a, CX, zz, 1 - x)
+            departure(a, CX, zz, 1 - x, rows)
+            if near and deep[a]:
+                arrival(a, CE, zz, 1 - x, 1 - c, some)
+                departure(a, CE, zz, 1 - x, some)
 
             @pl.when((zz <= z) & (z < nz - 1))
             def _():
                 departure(a, ZU, zz, x)
+                if deep[a]:
+                    departure(a, EU, zz, 1 - x, some)
 
             @pl.when((zz >= z) & (z > 0))
             def _():
                 departure(a, ZD, zz, x)
+                if deep[a]:
+                    departure(a, ED, zz, 1 - x, some)
 
     swap.wait()
 
@@ -1410,8 +1467,8 @@
         in_specs=[ANYWHERE] * (count + 1),
         out_specs=[ANYWHERE] * (count + 1),
         scratch_shapes=[
-            pltpu.SemaphoreType.DMA((5, count, nz)),
-            pltpu.SemaphoreType.DMA((5, count, nz)),
+            pltpu.SemaphoreType.DMA((8, count, nz)),
+            pltpu.SemaphoreType.DMA((8, count, nz)),
             pltpu.SemaphoreType.DMA((count,)),
             pltpu.SemaphoreType.DMA((2,)),
         ],

time: 757 us -> 753 us (level)
  no operation moved by 1% of the time
where the time goes in v8:
time: 753 us; the launch traced here: 747 us
  Pallas kernels  686 us (91%)
  local copies, waits for them, and re-layouts  28 us (4%)
  other arithmetic  19.9 us (3%)
  matrix products  11.7 us (2%)
    pallas_call x1, Pallas kernels, expert_pass(): pl.pallas_call(functools.partial(expert_kernel, nz), in_specs=[ANYWHERE]...  138 us
    pallas_call x1, Pallas kernels, scatter_in_plane(): pl.pallas_call(functools.partial(plane_scatter_kernel, count), out_shape=...  115 us
    pallas_call x1, Pallas kernels, attend_back(): pl.pallas_call(attend_back_kernel, out_shape=[jax.ShapeDtypeStruct((rows,...  114 us
    pallas_call x1, Pallas kernels, scatter_sum(): pl.pallas_call(scatter_kernel, out_shape=[jax.ShapeDtypeStruct((rows, col...  114 us
    pallas_call x1, Pallas kernels, attend(): pl.pallas_call(attend_kernel, out_shape=[jax.ShapeDtypeStruct((nz, 2, 2,...  110 us
    pallas_call x1, Pallas kernels, gather_in_plane(): pl.pallas_call(functools.partial(plane_gather_kernel, count), out_shape=[...  94.6 us
    unnamed x88, local copies, waits for them, and re-layouts  18.5 us

profile of v8, /device:TPU:0, one launch (start us, length us, event | category | flops | bytes accessed | tf_op | source)
XLA Modules:
  0.0 747.1 jit_solution(15219182122348466211)
XLA Ops:
  2.0 94.6 %shard_map.254 = (bf16[4,2,2,128,1024]{4,3,2,1,0:T(8,128)(2,1)}, bf16[4,2,2,128,1024]{4,3,2,1,0:T(8,128)(2,1)}, bf16[4,2,2,128,1024]{4,3,2,1,0:T(8,128)(2,1)}, b...) custom-call(bf16[128,1024]{1,0:T(8,128)(2,1)} %refs_0_.1, ...), custom_call_target="tpu_custom_call" | custom-call | flops 99999997952 | bytes 100000000 | tf_op jit(solution)/shard_map/pallas_call | solution.py:1463
  96.6 1.2 broadcast_select_fusion.1
  99.7 1.6 fusion.2.normed_source.refs_0_.refs_1_.refs_2_
  102.6 1.5 sine_multiply_fusion
  104.1 109.7 %shard_map.255 = (bf16[4,2,2,2,192,2048]{5,4,3,2,1,0:T(8,128)(2,1)}, f32[384,1024]{1,0:T(8,128)}, f32[384,1024]{1,0:T(8,128)}, bf16[384,1024]{1,0:T(8,128)(2,1)}...) custom-call(bf16[192,2048]{1,0:T(8,128)(2,1)} %src.1, ...), custom_call_target="tpu_custom_call" | custom-call | flops 99999997952 | bytes 100000000 | tf_op jit(solution)/shard_map/pallas_call | solution.py:1085
  213.8 1.7 multiply_reduce_fusion.2
  216.7 1.1 multiply_convert_fusion.src
  218.7 0.9 pad.4.router_ref
  219.6 138.3 %shard_map.256 = (bf16[4,2,2,2,192,2048]{5,4,3,2,1,0:T(8,128)(2,1)}, bf16[4,2,2,384,2048]{4,3,2,1,0:T(8,128)(2,1)}, bf16[4,2,2,384,2176]{4,3,2,1,0:T(8,128)(2,1)...) custom-call(bf16[192,2048]{1,0:T(8,128)(2,1)} %multiply_convert_fusi, ...), custom_call_target="tpu_custom_call" | custom-call | flops 99999997952 | bytes 100000000 | tf_op jit(solution)/shard_map/pallas_call | solution.py:1901
  358.0 113.6 %shard_map.257 = (bf16[192,2176]{1,0:T(8,128)(2,1)}, f32[2048,512]{1,0:T(8,128)}, f32[2048,512]{1,0:T(8,128)}, f32[512,2048]{1,0:T(8,128)}) custom-call(bf16[4,2,2,2,192,2176]{5,4,3,2,1,0:T(8,128)(2,1)} %bitcast.61, bf16[24,256,2048]{2,1,0:T(8,128)(2,1)} %bitcast.65, bf16[24,256,2048]{2,1,0:T(8,128)(2,1)} %bitcast.63, bf16[24,256,512]{2,1,0:T(8,128)(2,1)} %bitcast.66, ...), custom_call_target="tpu_custom_call" | custom-call | flops 99999997952 | bytes 100000000 | tf_op jit(solution)/shard_map/pallas_call | solution.py:915
  472.6 1.5 fusion.21
  474.4 1.3 multiply_reduce_fusion
  475.7 1.9 fusion.19
  477.6 114.4 %shard_map.258 = (bf16[192,2048]{1,0:T(8,128)(2,1)}, bf16[384,2048]{1,0:T(8,128)(2,1)}, bf16[384,1024]{1,0:T(8,128)(2,1)}, bf16[384,1024]{1,0:T(8,128)(2,1)}, bf...) custom-call(bf16[4,2,2,2,192,2048]{5,4,3,2,1,0:T(8,128)(2,1)} %bitcast.64, bf16[192,2048]{1,0:T(8,128)(2,1)} %get-tuple-element.152.own_grad, ...), custom_call_target="tpu_custom_call" | custom-call | flops 99999997952 | bytes 100000000 | tf_op jit(solution)/shard_map/pallas_call | solution.py:1268
  592.1 4.4 fusion.23
  596.6 1.8 fusion.22
  599.4 2.3 fusion.3
  601.6 1.7 copy-done.3
  603.3 1.0 dynamic-slice_convert_fusion.refs_9_
  606.7 1.4 concatenate.11.refs_8_
  608.1 115.5 %shard_map.259 = (f32[128,1024]{1,0:T(8,128)}, f32[128,1024]{1,0:T(8,128)}, f32[128,1024]{1,0:T(8,128)}, f32[128,1024]{1,0:T(8,128)}, f32[24,2048]{1,0:T(8,128)}, /*index=5*/bf16[192,2048]{1,0:T(8,128)(2,1)}) custom-call(bf16[384,2048]{1,0:T(8,128)(2,1)} %fusion.2.normed_source.refs_0_.refs_1_.refs_2_, ...), custom_call_target="tpu_custom_call" | custom-call | flops 99999997952 | bytes 100000000 | tf_op jit(solution)/shard_map/pallas_call | solution.py:1666
  723.6 2.3 fusion.5
  726.2 3.5 fusion.7
  729.6 1.0 copy.43
  730.6 1.6 slice_bitcast_fusion
  732.3 1.6 fusion.20
  733.9 1.1 add_convert_fusion
  737.4 2.1 copy.56
  739.6 1.6 copy-done.13
  741.1 2.1 copy.57
  743.3 1.6 copy-done.12
  744.9 2.0 copy.58
  (113 shorter events, 13.9 us)
Async XLA Ops:
  2.0 94.6 %copy-start.5 = (bf16[192,2048]{1,0:T(8,128)(2,1)S(1)}, bf16[192,2048]{1,0:T(8,128)(2,1)}, u32[]{:S(2)}) copy-start(bf16[192,2048]{1,0:T(8,128)(2,1)} %refs_5_.1) | copy-start | bytes 2359300
  97.9 1.8 copy-start.28
  99.7 2.2 copy-start.37
  213.8 2.9 copy-start.26
  215.5 2.9 copy-start.20
  216.1 1.6 copy-start.33
  357.9 114.7 %copy-start.21 = (bf16[2048,16]{0,1:T(8,128)(2,1)S(1)}, bf16[2048,16]{0,1:T(8,128)(2,1)}, u32[]{:S(2)}) copy-start(bf16[2048,16]{0,1:T(8,128)(2,1)} %param.26) | copy-start | bytes 196612
  357.9 116.2 %copy-start.30 = (s32[384,8]{0,1:T(8,128)S(1)}, s32[384,8]{0,1:T(8,128)}, u32[]{:S(2)}) copy-start(s32[384,8]{0,1:T(8,128)} %param.16) | copy-start | bytes 36868
  358.0 116.3 %copy-start.1 = (f32[192,2048]{1,0:T(8,128)S(1)}, f32[192,2048]{1,0:T(8,128)}, u32[]{:S(2)}) copy-start(f32[192,2048]{1,0:T(8,128)} %copy-done) | copy-start | bytes 4718596
  358.0 116.3 %copy-start.27 = (f32[2048]{0:T(1024)S(1)}, f32[2048]{0:T(1024)}, u32[]{:S(2)}) copy-start(f32[2048]{0:T(1024)} %param.25) | copy-start | bytes 24580
  358.0 116.3 %copy-start.34 = (f32[192]{0:T(256)S(1)}, f32[192]{0:T(256)}, u32[]{:S(2)}) copy-start(f32[192]{0:T(256)} %copy-done.33) | copy-start | bytes 2308
  471.6 2.7 copy-start.16
  592.1 4.4 copy-start.38
  592.1 4.4 copy-start.39
  596.5 1.9 copy-start.8
  596.5 1.9 copy-start.10
  596.5 2.7 copy-start.15
  596.5 2.8 copy-start.19
  596.5 2.8 copy-start.32
  601.6 1.7 copy-start.3
  608.1 115.5 %copy-start.6 = (bf16[192,2048]{1,0:T(8,128)(2,1)S(1)}, bf16[192,2048]{1,0:T(8,128)(2,1)}, u32[]{:S(2)}) copy-start(bf16[192,2048]{1,0:T(8,128)(2,1)} %refs_5_.1) | copy-start | bytes 2359300
  608.1 115.5 %copy-start.29 = (f32[2048]{0:T(1024)S(1)}, f32[2048]{0:T(1024)}, u32[]{:S(2)}) copy-start(f32[2048]{0:T(1024)} %param.18) | copy-start | bytes 24580
  723.6 2.6 copy-start.4
  726.2 3.5 copy-start.25
  726.2 7.7 %copy-start.2 = (f32[192,2048]{1,0:T(8,128)S(1)}, f32[192,2048]{1,0:T(8,128)}, u32[]{:S(2)}) copy-start(f32[192,2048]{1,0:T(8,128)} %copy-done) | copy-start | bytes 4718596
  729.6 4.2 copy-start.18
  729.6 5.3 copy-start.24
  730.6 5.1 copy-start.23
  733.9 3.6 copy-start.14
  734.9 1.7 copy-start.22
  737.4 3.7 copy-start.13
  741.1 3.7 copy-start.12
  (8 other events, 9.5 us)
